TPU v7x, 32 devices: a whole 2x2x4 slice. The times are simulated.
32 devices in a mesh: ctx: 8 (over z, y), fsdp: 4 (over x, core).
Axes of the slice: x: 2, y: 2, z: 4, core: 2. Of those that a mesh axis runs over, the one named last changes fastest.
Arguments:
- tokens: bfloat16 [1024, 2048], P('ctx'), may hold values from -24 to 24
- positions: int32 [1024], replicated, may hold values from 0 to 1023, each once
- pulse_indicator: int32 [2, 1024, 2048], P(None, 'ctx'), may hold values 0 or 1
- norm_gain: float32 [2048], replicated, may hold values from 0.1 to 1.9
- in_weight: bfloat16 [2048, 3, 1024], P(None, None, 'fsdp'), may hold values from -0.375 to 0.375
- out_weight: bfloat16 [1024, 2048], P('fsdp'), may hold values from -0.1875 to 0.1875
- upstream: bfloat16 [1024, 2048], P('ctx'), may hold values from -6 to 6
Outputs:
- block_out: bfloat16 [1024, 2048], P('ctx', 'fsdp')
- token_grad: float32 [1024, 2048], P('ctx', 'fsdp')
- gain_grad: float32 [2048], P('fsdp')
- in_grad: float32 [2048, 3, 1024], P('ctx', None, 'fsdp')
- out_grad: float32 [2048, 1024], P('ctx', 'fsdp')
Inputs may be any that keep to these rules, and one draw needn't show every extreme that they name: `positions`: each position of the sequence appears once.
All inputs are finite; a program needn't handle non-finite values. No bound on the sum of `pulse_indicator` on one device may be relied on, other than what follows from the above.
Results may differ from a plain program's by a relative error of at most 0.004.
The roundings to bfloat16 on the way count: a program that leaves them out, or rounds other values in their place, can miss the bound.
Values may be sent and summed in bfloat16 or wider, within the bound.
No kernel may reach another device: no remote copies, remote signals or barrier semaphores. Data moves between devices by JAX's collectives and lax.ppermute only.
A program may use at most 192 MiB of HBM per device.

v0:
```python
import jax
import jax.numpy as jnp
from jax import lax
from jax.sharding import PartitionSpec as P

HEAD_DIM = 128
TIMESTEPS = 2


SOFT_CAP = 30.0
LEAK_RATE = 0.5
THRESHOLD = 1.0
SURROGATE_SLOPE = 4.0
EPSILON = 1e-05


def leaky_forward(tokens, pulse_indicator, norm_gain):
    values = tokens.astype(jnp.float32)
    inv_rms = lax.rsqrt(jnp.mean(values * values, axis=-1, keepdims=True) + EPSILON)
    normed = values * inv_rms
    current = normed * norm_gain
    neuron_voltage = current
    voltage_trace_record = []
    pulse_number_sum = jnp.zeros_like(current)
    for present_instant in range(TIMESTEPS):
        binary_pulses = pulse_indicator[present_instant].astype(jnp.float32)
        if present_instant > 0:
            neuron_voltage = (
                LEAK_RATE
                * neuron_voltage
                * (1.0 - pulse_indicator[present_instant - 1].astype(jnp.float32))
                + current
            )
        voltage_trace_record.append(neuron_voltage)
        pulse_number_sum = pulse_number_sum + binary_pulses * neuron_voltage
    return (
        inv_rms,
        normed,
        voltage_trace_record,
        (pulse_number_sum / TIMESTEPS).astype(jnp.bfloat16),
    )


def leaky_backward(grad_rate, pulse_indicator, voltage_trace_record):
    rescaled_logits = grad_rate / TIMESTEPS
    leaky_level_prior = jnp.zeros_like(rescaled_logits)
    grad_current = jnp.zeros_like(rescaled_logits)
    for present_instant in reversed(range(TIMESTEPS)):
        binary_pulses = pulse_indicator[present_instant].astype(jnp.float32)
        capped_logits = jax.nn.sigmoid(
            SURROGATE_SLOPE * (voltage_trace_record[present_instant] - THRESHOLD)
        )
        voltage_adjoint = (
            rescaled_logits
            * (
                binary_pulses
                + voltage_trace_record[present_instant]
                * SURROGATE_SLOPE
                * capped_logits
                * (1.0 - capped_logits)
            )
            + leaky_level_prior
        )
        grad_current = grad_current + voltage_adjoint
        if present_instant > 0:
            leaky_level_prior = (
                LEAK_RATE
                * voltage_adjoint
                * (1.0 - pulse_indicator[present_instant - 1].astype(jnp.float32))
            )
    return grad_current


def body(tokens, positions, pulse_indicator, norm_gain, in_weight, out_weight, upstream):
    ctx_rank = lax.axis_index("ctx")
    fsdp_rank = lax.axis_index("fsdp")
    rows_here = tokens.shape[0]
    model_width = tokens.shape[1]
    share_cols = model_width // lax.axis_size("fsdp")
    local_width = out_weight.shape[0]
    heads_here = local_width // HEAD_DIM
    score_scale = HEAD_DIM ** (-0.5)
    own_pos = lax.dynamic_slice_in_dim(positions, ctx_rank * rows_here, rows_here)
    inv_rms, normed, voltage_trace_record, spikes = leaky_forward(
        tokens, pulse_indicator, norm_gain
    )
    flat_in = in_weight.reshape(model_width, 3 * local_width)
    project = jnp.dot(spikes, flat_in, preferred_element_type=jnp.float32).astype(jnp.bfloat16)
    project = project.reshape(rows_here, 3, local_width)
    query_flat = project[:, 0]
    queries = query_flat.reshape(rows_here, heads_here, HEAD_DIM)
    gathered = lax.all_gather(project[:, 1:], "ctx", axis=0, tiled=True)
    keys_all = gathered[:, 0].reshape(-1, heads_here, HEAD_DIM)
    values_all = gathered[:, 1].reshape(-1, heads_here, HEAD_DIM)
    allowed = positions[None, :] <= own_pos[:, None]
    scores = (
        jnp.einsum("rhd,khd->hrk", queries, keys_all, preferred_element_type=jnp.float32)
        * score_scale
    )
    squashed = jnp.tanh(scores / SOFT_CAP)
    exponent = jnp.where(allowed[None], jnp.exp(SOFT_CAP * squashed), 0.0)
    totals = jnp.sum(exponent, axis=-1, keepdims=True)
    attn_prob = exponent / totals
    prob_low = attn_prob.astype(jnp.bfloat16)
    attended = jnp.einsum("hrk,khd->rhd", prob_low, values_all, preferred_element_type=jnp.float32)
    attended = attended.astype(jnp.bfloat16).reshape(rows_here, local_width)
    partial_out = jnp.dot(attended, out_weight, preferred_element_type=jnp.float32)
    summed_out = lax.psum_scatter(partial_out, "fsdp", scatter_dimension=1, tiled=True)
    low_col = fsdp_rank * share_cols
    token_share = lax.dynamic_slice_in_dim(tokens, low_col, share_cols, 1).astype(jnp.float32)
    block_out = (token_share + summed_out).astype(jnp.bfloat16)
    grad_attn = jnp.dot(upstream, out_weight.T, preferred_element_type=jnp.float32).astype(
        jnp.bfloat16
    )
    grad_heads = grad_attn.reshape(rows_here, heads_here, HEAD_DIM)
    grad_prob = jnp.einsum(
        "rhd,khd->hrk", grad_heads, values_all, preferred_element_type=jnp.float32
    )
    delta = jnp.sum(attn_prob * grad_prob, axis=-1, keepdims=True)
    score_grad = (
        attn_prob * (grad_prob - delta) * (1.0 - squashed * squashed) * score_scale
    ).astype(jnp.bfloat16)
    grad_query = jnp.einsum(
        "hrk,khd->rhd", score_grad, keys_all, preferred_element_type=jnp.float32
    )
    grad_query = grad_query.astype(jnp.bfloat16).reshape(rows_here, local_width)
    grad_keys = jnp.einsum("hrk,rhd->khd", score_grad, queries, preferred_element_type=jnp.float32)
    grad_values = jnp.einsum(
        "hrk,rhd->khd", prob_low, grad_heads, preferred_element_type=jnp.float32
    )
    key_grads = lax.psum_scatter(
        jnp.stack(
            [
                grad_keys.reshape(rows_here * lax.axis_size("ctx"), local_width),
                grad_values.reshape(rows_here * lax.axis_size("ctx"), local_width),
            ],
            axis=1,
        ),
        "ctx",
        scatter_dimension=0,
        tiled=True,
    )
    grad_project = jnp.concatenate([grad_query[:, None], key_grads.astype(jnp.bfloat16)], axis=1)
    flat_grad = grad_project.reshape(rows_here, 3 * local_width)
    spike_part = jnp.dot(flat_grad, flat_in.T, preferred_element_type=jnp.float32)
    grad_spikes = lax.psum(spike_part, "fsdp")
    grad_current = leaky_backward(grad_spikes, pulse_indicator, voltage_trace_record)
    scaled_grad = grad_current * norm_gain
    row_mean = jnp.mean(scaled_grad * normed, axis=-1, keepdims=True)
    full_grad = upstream.astype(jnp.float32) + inv_rms * (scaled_grad - normed * row_mean)
    token_grad = lax.dynamic_slice_in_dim(full_grad, low_col, share_cols, 1)
    gain_part = lax.dynamic_slice_in_dim(
        jnp.sum(grad_current * normed, axis=0), low_col, share_cols
    )
    gain_grad = lax.psum(gain_part, "ctx")
    grad_inward = jnp.einsum("rc,rk->ck", spikes, flat_grad, preferred_element_type=jnp.float32)
    grad_outward = jnp.einsum("rc,rk->ck", upstream, attended, preferred_element_type=jnp.float32)
    weight_rows = lax.psum_scatter(
        jnp.concatenate([grad_inward, grad_outward], axis=1), "ctx", scatter_dimension=0, tiled=True
    )
    in_grad = weight_rows[:, : 3 * local_width].reshape(-1, 3, local_width)
    out_grad = weight_rows[:, 3 * local_width :]
    return (block_out, token_grad, gain_grad, in_grad, out_grad)


def solution(mesh):
    placed = (
        P("ctx", None),
        P(),
        P(None, "ctx", None),
        P(),
        P(None, None, "fsdp"),
        P("fsdp", None),
        P("ctx", None),
    )
    return jax.shard_map(
        body,
        mesh=mesh,
        in_specs=placed,
        out_specs=(
            P("ctx", "fsdp"),
            P("ctx", "fsdp"),
            P("fsdp"),
            P("ctx", None, "fsdp"),
            P("ctx", "fsdp"),
        ),
        check_vma=False,
    )
```

profile of v0, /device:TPU:0, one launch (start us, length us, event | category | flops | bytes accessed | tf_op | source)
XLA Modules:
  0.0 375.2 jit_solution(12632375523382011827)
XLA Ops:
  7.2 1.3 fusion.7
  8.6 4.9 %copy.23 = bf16[2048,3,256]{0,2,1:T(8,128)(2,1)} copy(bf16[2048,3,256]{2,0,1:T(8,128)(2,1)} %param.11) | data formatting | bytes 6291456 | tf_op args[4]
  13.4 2.7 convert_multiply_fusion
  16.9 1.2 convolution_convert_fusion
  19.1 1.5 convolution_convert_fusion.2
  21.0 40.4 %all-gather.2.cloned.1.call-done = bf16[1024,2,256]{0,2,1:T(8,128)(2,1)} async-done(((bf16[128,2,256]{0,2,1:T(8,128)(2,1)}), bf16[1024,2,256]{0,2,1:T(8,128)(2,1)}) %all-gather.2.cloned.1.call-update) | async-done | bytes 1048592 | tf_op jit(solution)/shard_map/all_gather | solution.py:92
  61.4 1.3 fusion.44
  63.4 1.3 fusion.46
  65.4 1.0 copy-done.8
  66.4 1.5 fusion.29
  67.9 4.2 %fusion.17 = f32[2,128,1024]{2,1,0:T(8,128)} fusion(bf16[128,2,128]{0,2,1:T(8,128)(2,1)S(1)} %bitcast.88, f32[2,128,1024]{2,1,0:T(8,128)} %fusion.46, f32[2,128,1024]{2,1,0:T(8,128)} %copy-done.8, f32[2,128]{1,0:T(2,128)S(1)} %get-tuple-element.22, pred[128,1024]{1,0:T(8,128)(4,1)S(1)} %broadcast_compare_fusion), kind=kOutput, calls=%fused_computation.37 | convolution fusion | flops 70780160 | bytes 3343360 | tf_op jit(solution)/shard_map/hrk,rhd->khd/dot_general | solution.py:127
  72.2 2.5 copy.31
  74.7 2.6 copy.30
  77.3 3.0 pad_maximum_fusion.1
  80.4 1.8 convolution_convert_fusion.3
  82.2 1.3 fusion.45
  83.6 3.4 convolution_convert_fusion.1
  87.1 2.9 convolution_bitcast_fusion
  89.9 57.2 %reduce-scatter.6.cloned.1.call-done = f32[128,2,256]{2,0,1:T(8,128)} async-done(((f32[1024,2,256]{2,0,1:T(8,128)}), f32[128,2,256]{2,0,1:T(8,128)}) %reduce-scatter.6.cloned.1.call-update) | async-done | bytes 262160 | tf_op jit(solution)/shard_map/reduce_scatter | solution.py:131
  148.8 1.1 copy.33
  149.9 4.0 %convolution_bitcast_fusion.1 = f32[128,2048]{1,0:T(8,128)} fusion(bf16[2048,3,256]{2,0,1:T(8,128)(2,1)} %param.11, bf16[128,2,256]{2,0,1:T(8,128)(2,1)S(1)} %convert_element_type.75, bf16[128,1,256]{2,0,1:T(8,128)(2,1)S(1)} %copy.32), kind=kOutput, calls=%fused_computation.3 | convolution fusion | flops 402751488 | bytes 4390912 | tf_op jit(solution)/shard_map/dot_general | solution.py:145
  154.0 2.0 fusion.47
  156.0 6.2 %pad_maximum_fusion = f32[2048,1024]{0,1:T(8,128)} fusion(f32[2048,256]{0,1:T(8,128)} %convolution_bitcast_fusion, f32[2048,768]{0,1:T(8,128)S(1)} %fusion.47), kind=kLoop, calls=%fused_computation.1 | loop fusion | flops 2097152 | bytes 16777216 | tf_op jit(solution)/shard_map/concatenate | solution.py:159
  162.2 11.4 %reduce-scatter.4.cloned.1.call-done = f32[128,512]{1,0:T(8,128)} async-done(((f32[128,2048]{1,0:T(8,128)}), f32[128,512]{1,0:T(8,128)}) %reduce-scatter.4.cloned.1.call-update) | async-done | bytes 262160 | tf_op jit(solution)/shard_map/reduce_scatter | solution.py:108
  173.6 1.7 add_convert_fusion
  175.3 36.8 %all-reduce.2.cloned.1.call-done = f32[128,2048]{1,0:T(8,128)} async-done(((f32[128,2048]{1,0:T(8,128)}), f32[128,2048]{1,0:T(8,128)}) %all-reduce.2.cloned.1.call-update) | async-done | bytes 1048592 | tf_op jit(solution)/shard_map/psum | solution.py:146
  212.1 3.9 %multiply_reduce_fusion = (f32[2048]{0:T(1024)S(1)}, f32[128]{0:T(128)S(1)}, f32[128,2048]{1,0:T(8,128)}) fusion(bf16[128,2048]{1,0:T(8,128)(2,1)} %param.7, f32[128]{0:T(128)S(1)} %add_rsqrt_fusion, f32[2048]{0:T(1024)S(1)} %copy-done.6, s32[2,128,2048]{2,1,0:T(8,128)S(1)} %copy-done.2, f32[128,2048]{1,0:T(8,128)} %all-reduce.2.cloned.1.call-done), kind=kLoop, calls=%fused_computation.31 | loop fusion | flops 10745728 | bytes 4736000 | tf_op jit(solution)/shard_map/reduce_sum | solution.py:153
  216.1 22.3 %psum.15 = f32[512]{0:T(512)} all-reduce(f32[512]{0:T(512)S(1)} %dynamic_slice.15), channel_id=1, replica_groups=mesh['ctx'=8,'fsdp'=4] {'ctx'}, use_global_device_ids=true, to_apply=%region_8.9 | all-reduce | flops 512 | bytes 4096 | tf_op jit(solution)/shard_map/psum | solution.py:155
  238.4 1.9 fusion.28
  240.3 125.2 %reduce-scatter.8.cloned.1.call-done = f32[256,1024]{0,1:T(8,128)} async-done(((f32[2048,1024]{0,1:T(8,128)}), f32[256,1024]{0,1:T(8,128)}) %reduce-scatter.8.cloned.1.call-update) | async-done | bytes 1048592 | tf_op jit(solution)/shard_map/reduce_scatter | solution.py:158
  365.5 1.2 slice.40
  366.7 1.1 copy.34
  (43 shorter events, 6.4 us)
Async XLA Ops:
  7.2 11.9 %copy-start = (bf16[256,2048]{1,0:T(8,128)(2,1)S(1)}, bf16[256,2048]{1,0:T(8,128)(2,1)}, u32[]{:S(2)}) copy-start(bf16[256,2048]{1,0:T(8,128)(2,1)} %param.12) | copy-start | bytes 3145732
  7.2 54.2 %all-gather.2.cloned.1.call-start = ((), (), s32[]{:S(2)}) async-start(), calls=%async_computation.3 | async-start | bytes 1179648 | tf_op jit(solution)/shard_map/all_gather | solution.py:92
  8.5 4.9 %copy-start.2 = (s32[2,128,2048]{2,1,0:T(8,128)S(1)}, s32[2,128,2048]{2,1,0:T(8,128)}, u32[]{:S(2)}) copy-start(s32[2,128,2048]{2,1,0:T(8,128)} %param.9) | copy-start | bytes 6291460
  8.6 4.9 %copy-start.6 = (f32[2048]{0:T(1024)S(1)}, f32[2048]{0:T(1024)}, u32[]{:S(2)}) copy-start(f32[2048]{0:T(1024)} %param.10) | copy-start | bytes 24580
  13.4 3.5 copy-start.1
  16.1 0.8 copy-start.3
  16.9 3.8 %copy-start.7 = (s32[1024]{0:T(1024)S(1)}, s32[1024]{0:T(1024)}, u32[]{:S(2)}) copy-start(s32[1024]{0:T(1024)} %param.8) | copy-start | bytes 12292
  19.0 128.2 %reduce-scatter.6.cloned.1.call-start = ((), (), s32[]{:S(2)}) async-start(), calls=%async_computation.5 | async-start | bytes 2359296 | tf_op jit(solution)/shard_map/reduce_scatter | solution.py:131
  62.6 0.8 copy-start.4
  62.7 2.1 copy-start.5
  65.4 1.0 copy-start.8
  80.3 93.3 %reduce-scatter.4.cloned.1.call-start = ((), (), s32[]{:S(2)}) async-start(), calls=%async_computation.4 | async-start | bytes 1310720 | tf_op jit(solution)/shard_map/reduce_scatter | solution.py:108
  83.6 128.5 %all-reduce.2.cloned.1.call-start = ((), (), s32[]{:S(2)}) async-start(), calls=%async_computation.6 | async-start | bytes 2097152 | tf_op jit(solution)/shard_map/psum | solution.py:146
  153.9 211.6 %reduce-scatter.8.cloned.1.call-start = ((), (), s32[]{:S(2)}) async-start(), calls=%async_computation.7 | async-start | bytes 9437184 | tf_op jit(solution)/shard_map/reduce_scatter | solution.py:158
  365.5 2.4 slice-start
Sparse Core Ops, SparseCore 0:
  19.1 42.2 all-gather.1
  80.4 66.6 reduce-scatter.5
  149.7 23.8 reduce-scatter.3
  176.0 36.0 all-reduce.1
  215.6 149.8 reduce-scatter.7
where the time goes:
time: 376 us; the launch traced here: 375 us
  waiting for transfers between devices  271 us (72%)
  matrix products  25.8 us (7%)
  other arithmetic  22.5 us (6%)
  blocking collectives  22.3 us (6%)
  local copies, waits for them, and re-layouts  19.3 us (5%)
  between operations  14 us (4%)
    reduce_scatter x1, waiting for transfers between devices, body(): lax.psum_scatter(jnp.concatenate([grad_inward, grad_outward], axis=1), 'c...  125 us
    reduce_scatter x1, waiting for transfers between devices, body(): lax.psum_scatter(jnp.stack([grad_keys.reshape(rows_here * lax.axis_size('...  57.2 us
    all_gather x1, waiting for transfers between devices, body(): gathered = lax.all_gather(project[:, 1:], 'ctx', axis=0, tiled=True)  40.4 us
    psum x1, waiting for transfers between devices, body(): grad_spikes = lax.psum(spike_part, 'fsdp')  36.8 us
    psum x1, blocking collectives, body(): gain_grad = lax.psum(gain_part, 'ctx')  22.3 us
    reduce_scatter x1, waiting for transfers between devices, body(): lax.psum_scatter(partial_out, 'fsdp', scatter_dimension=1, tiled=True)  11.4 us
    unnamed x21, local copies, waits for them, and re-layouts  9.44 us
  transfers between devices with their start and end apart: 5, of which 5 were waited for; matrix products, arithmetic and copies ran while one was open for 9% of the time, Pallas kernels for 0%

commit v1 on v0

v1 whole, which is shorter than its diff:
```python
import functools

import jax
import jax.numpy as jnp
from jax import lax
from jax.experimental import pallas as pl
from jax.experimental.pallas import tpu as pltpu
from jax.sharding import PartitionSpec as P

HEAD_DIM = 128
SOFT_CAP = 30.0
LEAK_RATE = 0.5
THRESHOLD = 1.0
SURROGATE_SLOPE = 4.0
EPSILON = 1e-05
F32 = jnp.float32
BF16 = jnp.bfloat16
VMEM_LIMIT = 50 << 20
EXTRA_ROWS = 8


def dot(a, b, dims):
    return lax.dot_general(a, b, (dims, ((), ())), preferred_element_type=F32)


NN = ((1,), (0,))
NT = ((1,), (1,))
TN = ((0,), (0,))


def params():
    return pltpu.CompilerParams(vmem_limit_bytes=VMEM_LIMIT)


def project_kernel(
    tok_ref, pulse_ref, gain_ref, win_ref, up_ref, wout_ref, pay_ref, spikes_ref, inv_ref, acc_ref
):
    step = pl.program_id(0)
    width = spikes_ref.shape[1]
    local = win_ref.shape[2]

    @pl.when(step == 0)
    def _():
        values = tok_ref[...].astype(F32)
        inv_ref[...] = lax.rsqrt(jnp.mean(values * values, axis=-1, keepdims=True) + EPSILON)
        acc_ref[...] = jnp.zeros_like(acc_ref)

    at = pl.multiple_of(step * width, width)
    current = tok_ref[:, pl.ds(at, width)].astype(F32) * inv_ref[...] * gain_ref[...]
    first = pulse_ref[0].astype(F32)
    second = pulse_ref[1].astype(F32)
    later = LEAK_RATE * current * (1.0 - first) + current
    spikes = ((first * current + second * later) * 0.5).astype(BF16)
    spikes_ref[...] = spikes
    for part in range(3):
        acc_ref[:, part * local : (part + 1) * local] += dot(spikes, win_ref[part], NN)
    acc_ref[:, 3 * local :] += dot(up_ref[...], wout_ref[...], NT)

    @pl.when(step == pl.num_programs(0) - 1)
    def _():
        pay_ref[...] = acc_ref[...].astype(BF16)


def project(tokens, pulse, gain, win, upstream, wout):
    rows, model = tokens.shape
    local = wout.shape[0]
    width = 256
    return pl.pallas_call(
        project_kernel,
        grid=(model // width,),
        in_specs=[
            pl.BlockSpec((rows, model), lambda k: (0, 0)),
            pl.BlockSpec((2, rows, width), lambda k: (0, 0, k)),
            pl.BlockSpec((1, width), lambda k: (0, k)),
            pl.BlockSpec((3, width, local), lambda k: (0, k, 0)),
            pl.BlockSpec((rows, width), lambda k: (0, k)),
            pl.BlockSpec((local, width), lambda k: (0, k)),
        ],
        out_specs=[
            pl.BlockSpec((rows, 4 * local), lambda k: (0, 0)),
            pl.BlockSpec((rows, width), lambda k: (0, k)),
            pl.BlockSpec((rows, 1), lambda k: (0, 0)),
        ],
        out_shape=[
            jax.ShapeDtypeStruct((rows, 4 * local), BF16),
            jax.ShapeDtypeStruct((rows, model), BF16),
            jax.ShapeDtypeStruct((rows, 1), F32),
        ],
        scratch_shapes=[pltpu.VMEM((rows, 4 * local), F32)],
        compiler_params=params(),
        name="project",
    )(tokens, pulse, gain, win, upstream, wout)


def factor_kernel(tok_ref, pulse_ref, gain_ref, inv_ref, factor_ref):
    current = tok_ref[...].astype(F32) * inv_ref[...] * gain_ref[...]
    first = pulse_ref[0].astype(F32)
    second = pulse_ref[1].astype(F32)
    later = LEAK_RATE * current * (1.0 - first) + current

    def slope(fired, membrane):
        level = jax.nn.sigmoid(SURROGATE_SLOPE * (membrane - THRESHOLD))
        return fired + membrane * SURROGATE_SLOPE * level * (1.0 - level)

    carried = 1.0 + LEAK_RATE * (1.0 - first)
    factor_ref[...] = 0.5 * (slope(first, current) + slope(second, later) * carried)


def factors(tokens, pulse, gain, inv):
    rows, model = tokens.shape
    width = 512
    return pl.pallas_call(
        factor_kernel,
        grid=(model // width,),
        in_specs=[
            pl.BlockSpec((rows, width), lambda k: (0, k)),
            pl.BlockSpec((2, rows, width), lambda k: (0, 0, k)),
            pl.BlockSpec((1, width), lambda k: (0, k)),
            pl.BlockSpec((rows, 1), lambda k: (0, 0)),
        ],
        out_specs=pl.BlockSpec((rows, width), lambda k: (0, k)),
        out_shape=jax.ShapeDtypeStruct((rows, model), F32),
        compiler_params=params(),
        name="factors",
    )(tokens, pulse, gain, inv)


def attention_kernel(
    q_ref, k_ref, v_ref, do_ref, prow_ref, pcol_ref, out_ref, dk_ref, dv_ref
):
    step = pl.program_id(1)
    block = q_ref.shape[0]
    scale = HEAD_DIM**-0.5
    query, grad = q_ref[...], do_ref[...]
    keys, values = k_ref[...], v_ref[...]
    squashed = jnp.tanh(dot(query, keys, NT) * (scale / SOFT_CAP))
    exponent = jnp.where(prow_ref[...] <= pcol_ref[...], jnp.exp(SOFT_CAP * squashed), 0.0)
    prob = exponent * (1.0 / jnp.sum(exponent, axis=-1, keepdims=True))
    low = prob.astype(BF16)
    grad_prob = dot(grad, values, NT)
    delta = jnp.sum(prob * grad_prob, axis=-1, keepdims=True)
    score_grad = (prob * (grad_prob - delta) * ((1.0 - squashed * squashed) * scale)).astype(BF16)
    at = pl.multiple_of(step * block, block)
    out_ref[3, pl.ds(at, block), :] = dot(low, values, NN).astype(BF16)
    out_ref[0, pl.ds(at, block), :] = dot(score_grad, keys, NN).astype(BF16)
    key_part = dot(score_grad, query, TN)
    value_part = dot(low, grad, TN)

    @pl.when(step == 0)
    def _():
        dk_ref[...] = key_part
        dv_ref[...] = value_part

    @pl.when(step > 0)
    def _():
        dk_ref[...] += key_part
        dv_ref[...] += value_part

    @pl.when(step == pl.num_programs(1) - 1)
    def _():
        out_ref[1] = dk_ref[...].astype(BF16)
        out_ref[2] = dv_ref[...].astype(BF16)


def attention(gathered, positions):
    length, width = gathered.shape
    heads = width // (4 * HEAD_DIM)
    block = max(16, (256 * 1024) // length)
    whole = functools.partial(pl.BlockSpec, (length, HEAD_DIM))
    part = functools.partial(pl.BlockSpec, (block, HEAD_DIM))
    return pl.pallas_call(
        attention_kernel,
        grid=(heads, length // block),
        in_specs=[
            part(lambda h, i: (i, h)),
            whole(lambda h, i: (0, heads + h)),
            whole(lambda h, i: (0, 2 * heads + h)),
            part(lambda h, i: (i, 3 * heads + h)),
            pl.BlockSpec((1, length), lambda h, i: (0, 0)),
            pl.BlockSpec((block, 1), lambda h, i: (i, 0)),
        ],
        out_specs=pl.BlockSpec((4, length, HEAD_DIM), lambda h, i: (0, 0, h)),
        out_shape=jax.ShapeDtypeStruct((4, length, heads * HEAD_DIM), BF16),
        scratch_shapes=[pltpu.VMEM((length, HEAD_DIM), F32)] * 2,
        compiler_params=params(),
        name="attention",
    )(gathered, gathered, gathered, gathered, positions[None, :], positions[:, None])


def spread_kernel(
    at_ref, grad_ref, win_ref, tok_ref, gain_ref, inv_ref, factor_ref, out_ref, sums_ref
):
    step = pl.program_id(0)
    rows = grad_ref.shape[1]
    share = sum(dot(grad_ref[part], win_ref[part], NT) for part in range(3))
    weighted = share * factor_ref[...] * (tok_ref[...].astype(F32) * inv_ref[...])
    out_ref[0, :rows, :] = share
    out_ref[0, pl.ds(rows, EXTRA_ROWS), :] = jnp.broadcast_to(
        jnp.sum(weighted, axis=0, keepdims=True), (EXTRA_ROWS, share.shape[1])
    )
    mine = jnp.sum(weighted * gain_ref[...], axis=1, keepdims=True)

    @pl.when(step == 0)
    def _():
        sums_ref[...] = mine

    @pl.when(step > 0)
    def _():
        sums_ref[...] += mine


def spread(fsdp_rank, own_block, grads, win, tokens, gain, inv, factor):
    rows, model = tokens.shape
    local = grads.shape[2]
    blocks = 4
    width = model // blocks
    column = lambda k, at: (0, at[0] ^ k)
    return pl.pallas_call(
        spread_kernel,
        grid_spec=pltpu.PrefetchScalarGridSpec(
            num_scalar_prefetch=1,
            grid=(blocks,),
            in_specs=[
                pl.BlockSpec((3, rows, local), lambda k, at: (0, at[1], 0)),
                pl.BlockSpec((3, width, local), lambda k, at: (0, at[0] ^ k, 0)),
                pl.BlockSpec((rows, width), column),
                pl.BlockSpec((1, width), column),
                pl.BlockSpec((rows, 1), lambda k, at: (0, 0)),
                pl.BlockSpec((rows, width), column),
            ],
            out_specs=[
                pl.BlockSpec((1, rows + EXTRA_ROWS, width), lambda k, at: (k, 0, 0)),
                pl.BlockSpec((rows, 1), lambda k, at: (0, 0)),
            ],
        ),
        out_shape=[
            jax.ShapeDtypeStruct((blocks, rows + EXTRA_ROWS, width), F32),
            jax.ShapeDtypeStruct((rows, 1), F32),
        ],
        compiler_params=params(),
        name="spread",
    )(jnp.stack([fsdp_rank, own_block]), grads, win, tokens, gain, inv, factor)


def swap(value, axis, mask):
    count = lax.axis_size(axis)
    return lax.ppermute(value, axis, [(i, i ^ mask) for i in range(count)])


def scatter_sum(first, second, third, fourth):
    near = swap(jnp.stack([second, fourth]), "fsdp", 1)
    return first + near[0] + swap(third + near[1], "fsdp", 2)


def weight_kernel(at_ref, both_ref, grad_ref, in_ref, out_ref):
    step = pl.program_id(0)
    fired, wanted = both_ref[0, 0], both_ref[0, 1]
    parts = [dot(fired, grad_ref[part], TN) for part in range(3)]
    last = dot(wanted, grad_ref[3], TN)

    @pl.when(step == 0)
    def _():
        for part in range(3):
            in_ref[part] = parts[part]
        out_ref[...] = last

    @pl.when(step > 0)
    def _():
        for part in range(3):
            in_ref[part] += parts[part]
        out_ref[...] += last


def weight_grads(turn, both, grads):
    blocks, _, rows, features = both.shape
    local = grads.shape[2]
    return pl.pallas_call(
        weight_kernel,
        grid_spec=pltpu.PrefetchScalarGridSpec(
            num_scalar_prefetch=1,
            grid=(blocks,),
            in_specs=[
                pl.BlockSpec((1, 2, rows, features), lambda j, at: (at[0] ^ j, 0, 0, 0)),
                pl.BlockSpec((4, rows, local), lambda j, at: (0, j, 0)),
            ],
            out_specs=[
                pl.BlockSpec((3, features, local), lambda j, at: (0, 0, 0)),
                pl.BlockSpec((features, local), lambda j, at: (0, 0)),
            ],
        ),
        out_shape=[
            jax.ShapeDtypeStruct((3, features, local), F32),
            jax.ShapeDtypeStruct((features, local), F32),
        ],
        compiler_params=params(),
        name="weight_grads",
    )(turn[None], both, grads)


def body(tokens, positions, pulse_indicator, norm_gain, in_weight, out_weight, upstream):
    ctx, fsdp = lax.axis_size("ctx"), lax.axis_size("fsdp")
    ctx_rank, fsdp_rank = lax.axis_index("ctx"), lax.axis_index("fsdp")
    rows, model = tokens.shape
    local = out_weight.shape[0]
    share = model // fsdp
    gain = norm_gain[None, :]
    win = jnp.transpose(in_weight, (1, 0, 2))
    payload, spikes, inv = project(tokens, pulse_indicator, gain, win, upstream, out_weight)
    factor = factors(tokens, pulse_indicator, gain, inv)

    if ctx == 8:
        turn = ctx_rank
        line = [payload] + [swap(payload, "ctx", 2 * step) for step in (1, 2, 3)]
        far = [swap(piece, "ctx", 1) for piece in line]
        blocks = [piece for pair in zip(line, far) for piece in pair]
        gathered = jnp.concatenate(blocks, axis=0)
        placed = jnp.concatenate(
            [lax.dynamic_slice_in_dim(positions, (turn ^ j) * rows, rows) for j in range(ctx)]
        )
    else:
        turn = jnp.zeros_like(ctx_rank)
        gathered = lax.all_gather(payload, "ctx", axis=0, tiled=True)
        placed = positions
    own = ctx_rank ^ turn
    grads = attention(gathered, placed)
    own_grads = lax.dynamic_slice_in_dim(grads, own * rows, rows, 1)

    spread_out, row_sums = spread(fsdp_rank, own, grads, win, tokens, gain, inv, factor)
    summed = scatter_sum(*(spread_out[j] for j in range(4)))
    row_mean = row_sums + swap(row_sums, "fsdp", 1)
    row_mean = (row_mean + swap(row_mean, "fsdp", 2)) / model
    low = fsdp_rank * share

    def columns(array):
        return lax.dynamic_slice_in_dim(array, low, share, 1)

    token_share = columns(tokens).astype(F32)
    scaled_grad = columns(factor) * summed[:rows] * columns(gain)
    token_grad = columns(upstream).astype(F32) + inv * (
        scaled_grad - token_share * inv * row_mean
    )
    gain_grad = summed[rows]
    if ctx == 8:
        for mask in (1, 2, 4):
            gain_grad = gain_grad + swap(gain_grad, "ctx", mask)
    else:
        gain_grad = lax.psum(gain_grad, "ctx")

    partial_out = jnp.dot(own_grads[3], out_weight, preferred_element_type=F32)
    pieces = [
        lax.dynamic_slice_in_dim(partial_out, (fsdp_rank ^ j) * share, share, 1) for j in range(4)
    ]
    block_out = (token_share + scatter_sum(*pieces)).astype(BF16)

    features = model // ctx

    both = jnp.stack([spikes, upstream]).reshape(2, rows, ctx, features)
    both = lax.all_to_all(both, "ctx", 2, 0)
    if features % 128 == 0:
        in_grad, out_grad = weight_grads(turn, both, grads)
    else:
        fired, wanted = (both[:, k].reshape(ctx * rows, features) for k in range(2))
        in_grad = jnp.stack([dot(fired, grads[part], TN) for part in range(3)])
        out_grad = dot(wanted, grads[3], TN)
    in_grad = jnp.transpose(in_grad, (1, 0, 2))
    return (block_out, token_grad, gain_grad, in_grad, out_grad)


def solution(mesh):
    placed = (
        P("ctx", None),
        P(),
        P(None, "ctx", None),
        P(),
        P(None, None, "fsdp"),
        P("fsdp", None),
        P("ctx", None),
    )
    return jax.shard_map(
        body,
        mesh=mesh,
        in_specs=placed,
        out_specs=(
            P("ctx", "fsdp"),
            P("ctx", "fsdp"),
            P("fsdp"),
            P("ctx", None, "fsdp"),
            P("ctx", "fsdp"),
        ),
        check_vma=False,
    )
```

time: 376 us -> 118 us (0.31)
  waiting for transfers between devices: 271 us -> 17 us
  starting transfers between devices: 0.21 us -> 35 us
  Pallas kernels: 0 us -> 34 us
  matrix products: 25.8 us -> 0.31 us
  blocking collectives: 22.3 us -> 0 us
  other arithmetic: 22.5 us -> 7.98 us
  between operations: 14 us -> 0.91 us
    reduce_scatter x3 -> x0, waiting for transfers between devices: 194 us -> none  [the longest x1 125 us: body(): lax.psum_scatter(jnp.concatenate([grad_inward, grad_outward], axis=1), 'c...]
    all_gather x1 -> x0, waiting for transfers between devices: 40.4 us -> none  [body(): gathered = lax.all_gather(project[:, 1:], 'ctx', axis=0, tiled=True)]
    psum x1 -> x0, waiting for transfers between devices: 36.8 us -> none  [body(): grad_spikes = lax.psum(spike_part, 'fsdp')]
    pallas_call x0 -> x5, Pallas kernels: none -> 34 us  [the longest x1 14.1 us: attention(): pl.pallas_call(attention_kernel, grid=(heads, length // block), in_specs=...]
    ppermute x0 -> x16, starting transfers between devices: none -> 29.8 us  [swap(): return lax.ppermute(value, axis, [(i, i ^ mask) for i in range(count)])]
    dot_general x12 -> x1, matrix products: 25.8 us -> 0.31 us  [body(): partial_out = jnp.dot(own_grads[3], out_weight, preferred_element_type=F32)]
    psum x1 -> x0, blocking collectives: 22.3 us -> none  [body(): gain_grad = lax.psum(gain_part, 'ctx')]
    ppermute x0 -> x16, waiting for transfers between devices: none -> 17 us  [swap(): return lax.ppermute(value, axis, [(i, i ^ mask) for i in range(count)])]
  transfers between devices with their start and end apart: 5 -> 17, of which waited for: 5 -> 7; matrix products, arithmetic and copies ran while one was open for 9% -> 19% of each run, Pallas kernels for 0% -> 18%
where the time goes in v1:
time: 118 us; the launch traced here: 117 us
  starting transfers between devices  35 us (30%)
  Pallas kernels  34 us (29%)
  local copies, waits for them, and re-layouts  21.7 us (18%)
  waiting for transfers between devices  17 us (14%)
  other arithmetic  7.98 us (7%)
    ppermute x16, starting transfers between devices, swap(): return lax.ppermute(value, axis, [(i, i ^ mask) for i in range(count)])  29.8 us
    unnamed x49, local copies, waits for them, and re-layouts  18.9 us
    ppermute x16, waiting for transfers between devices, swap(): return lax.ppermute(value, axis, [(i, i ^ mask) for i in range(count)])  17 us
    pallas_call x1, Pallas kernels, attention(): pl.pallas_call(attention_kernel, grid=(heads, length // block), in_specs=...  14.1 us
    pallas_call x1, Pallas kernels, weight_grads(): pl.pallas_call(weight_kernel, grid_spec=pltpu.PrefetchScalarGridSpec(num_...  6.74 us
    pallas_call x1, Pallas kernels, project(): pl.pallas_call(project_kernel, grid=(model // width,), in_specs=[pl.Block...  6.46 us
    all_to_all x1, starting transfers between devices, body(): both = lax.all_to_all(both, 'ctx', 2, 0)  5.14 us
    pallas_call x1, Pallas kernels, spread(): pl.pallas_call(spread_kernel, grid_spec=pltpu.PrefetchScalarGridSpec(num_...  4.51 us
  transfers between devices with their start and end apart: 17, of which 7 were waited for; matrix products, arithmetic and copies ran while one was open for 19% of the time, Pallas kernels for 18%

profile of v1, /device:TPU:0, one launch (start us, length us, event | category | flops | bytes accessed | tf_op | source)
XLA Modules:
  0.0 116.8 jit_solution(8816697929701600910)
XLA Ops:
  1.7 1.2 %copy-done.7 = bf16[256,2048]{1,0:T(8,128)(2,1)S(1)} copy-done((bf16[256,2048]{1,0:T(8,128)(2,1)S(1)}, bf16[256,2048]{1,0:T(8,128)(2,1)}, u32[]{:S(2)}) %copy-start.7) | copy-done | bytes 1048600
  4.6 6.5 %project.1 = (bf16[128,1024]{1,0:T(8,128)(2,1)S(1)}, bf16[128,2048]{1,0:T(8,128)(2,1)S(1)}, f32[128,1]{1,0:T(8,128)S(1)}) custom-call(bf16[128,2048]{1,0:T(8,128)(2,1)S(1)} %copy-done.3, s32[2,128,2048]{2,1,0:T(8,128)} %pulse_ref.3, f32[1,2048]{1,0:T(1,128)S(1)} %bitcast.41, bf16[3,2048,256]{2,1,0:T(8,128)(2,1)} %bitcast.46, ...), custom_call_target="tpu_custom_call" | custom-call | tf_op jit(solution)/shard_map/project/pallas_call | solution.py:68
  11.1 3.0 %collective-permute-start = (bf16[128,1024]{1,0:T(8,128)(2,1)S(1)}, bf16[128,1024]{1,0:T(8,128)(2,1)}, u32[]{:S(2)}, u32[]{:S(2)}) collective-permute-start(bf16[128,1024]{1,0:T(8,128)(2,1)S(1)} %get-tuple-element.12), channel_id=1, source_target_pairs={{0,4},{4,0},{8,12},{12,8},{16,20},{20,16},{24,28},{28,24},{1,5},{5... | collective-permute-start | bytes 786440 | tf_op jit(solution)/shard_map/ppermute | solution.py:247
  14.1 1.6 %collective-permute-start.1 = (bf16[128,1024]{1,0:T(8,128)(2,1)S(1)}, bf16[128,1024]{1,0:T(8,128)(2,1)}, u32[]{:S(2)}, u32[]{:S(2)}) collective-permute-start(bf16[128,1024]{1,0:T(8,128)(2,1)S(1)} %get-tuple-element.12), channel_id=1, source_target_pairs={{0,8},{4,12},{8,0},{12,4},{16,24},{20,28},{24,16},{28,20},{1,9},{5... | collective-permute-start | bytes 786440 | tf_op jit(solution)/shard_map/ppermute | solution.py:247
  15.7 2.6 %collective-permute-start.3 = (bf16[128,1024]{1,0:T(8,128)(2,1)S(1)}, bf16[128,1024]{1,0:T(8,128)(2,1)}, u32[]{:S(2)}, u32[]{:S(2)}) collective-permute-start(bf16[128,1024]{1,0:T(8,128)(2,1)S(1)} %get-tuple-element.12), channel_id=1, source_target_pairs={{0,16},{4,20},{8,24},{12,28},{16,0},{20,4},{24,8},{28,12},{1,17},{... | collective-permute-start | bytes 786440 | tf_op jit(solution)/shard_map/ppermute | solution.py:247
  19.2 1.3 %copy.20 = bf16[1,2,128,8,256]{4,2,1,0,3:T(8,128)(2,1)} copy(bf16[1,2,128,8,256]{2,4,3,1,0:T(8,128)(2,1)S(1)} %pad_maximum_fusion) | data formatting | bytes 2097152 | tf_op jit(solution)/shard_map/stack | solution.py:357
  20.5 5.1 %all-to-all-start = ((bf16[1,2,128,8,256]{4,2,1,0,3:T(8,128)(2,1)}), bf16[1,2,128,8,256]{4,2,1,0,3:T(8,128)(2,1)}, u32[]{:S(2)}, u32[]{:S(2)}) async-start(bf16[1,2,128,8,256]{4,2,1,0,3:T(8,128)(2,1)} %copy.20), calls=%async_computation | async-start | bytes 2097152 | tf_op jit(solution)/shard_map/all_to_all | solution.py:358
  27.0 2.0 %collective-permute-start.2 = (bf16[128,1024]{1,0:T(8,128)(2,1)}, bf16[128,1024]{1,0:T(8,128)(2,1)}, u32[]{:S(2)}, u32[]{:S(2)}) collective-permute-start(bf16[128,1024]{1,0:T(8,128)(2,1)} %collective-permute-done.1), channel_id=1, source_target_pairs={{0,4},{4,0},{8,12},{12,8},{16,20},{20,16},{24,28},{28,24},{1,5},{5... | collective-permute-start | bytes 786440 | tf_op jit(solution)/shard_map/ppermute | solution.py:247
  29.4 2.2 %factors.1.factor_ref = f32[128,2048]{1,0:T(8,128)S(1)} custom-call(bf16[128,2048]{1,0:T(8,128)(2,1)S(1)} %copy-done.4, s32[2,128,2048]{2,1,0:T(8,128)S(1)} %copy-done.2, f32[1,2048]{1,0:T(1,128)S(1)} %bitcast.42, f32[128,1]{1,0:T(8,128)S(1)} %get-tuple-element.13.inv_ref), custom_call_target="tpu_custom_call" | custom-call | tf_op jit(solution)/shard_map/factors/pallas_call | solution.py:112
  32.6 5.2 %collective-permute-done.3 = bf16[128,1024]{1,0:T(8,128)(2,1)} collective-permute-done((bf16[128,1024]{1,0:T(8,128)(2,1)S(1)}, bf16[128,1024]{1,0:T(8,128)(2,1)}, u32[]{:S(2)}, u32[]{:S(2)}) %collective-permute-start.3) | collective-permute-done | bytes 262176 | tf_op jit(solution)/shard_map/ppermute | solution.py:247
  37.8 3.3 %collective-permute-start.4 = (bf16[128,1024]{1,0:T(8,128)(2,1)}, bf16[128,1024]{1,0:T(8,128)(2,1)S(1)}, u32[]{:S(2)}, u32[]{:S(2)}) collective-permute-start(bf16[128,1024]{1,0:T(8,128)(2,1)} %collective-permute-done.3), channel_id=1, source_target_pairs={{0,4},{4,0},{8,12},{12,8},{16,20},{20,16},{24,28},{28,24},{1,5},{5... | collective-permute-start | bytes 786440 | tf_op jit(solution)/shard_map/ppermute | solution.py:247
  41.1 1.7 %constant_dynamic-update-slice_fusion.6 = bf16[1024,1024]{1,0:T(8,128)(2,1)} fusion(bf16[1024,1024]{1,0:T(8,128)(2,1)} %constant_dynamic-update-slice_fusion.7, bf16[128,1024]{1,0:T(8,128)(2,1)} %collective-permute-done), kind=kLoop, calls=%fused_computation.33 | loop fusion | bytes 524288
  42.8 1.7 %constant_dynamic-update-slice_fusion.5 = bf16[1024,1024]{1,0:T(8,128)(2,1)} fusion(bf16[1024,1024]{1,0:T(8,128)(2,1)} %constant_dynamic-update-slice_fusion.6, bf16[128,1024]{1,0:T(8,128)(2,1)} %collective-permute-done.1), kind=kLoop, calls=%fused_computation.32 | loop fusion | bytes 524288
  44.4 1.7 %constant_dynamic-update-slice_fusion.4 = bf16[1024,1024]{1,0:T(8,128)(2,1)} fusion(bf16[1024,1024]{1,0:T(8,128)(2,1)} %constant_dynamic-update-slice_fusion.5, bf16[128,1024]{1,0:T(8,128)(2,1)} %collective-permute-done.2), kind=kLoop, calls=%fused_computation.31 | loop fusion | bytes 524288
  46.1 1.7 %constant_dynamic-update-slice_fusion.3 = bf16[1024,1024]{1,0:T(8,128)(2,1)} fusion(bf16[1024,1024]{1,0:T(8,128)(2,1)} %constant_dynamic-update-slice_fusion.4, bf16[128,1024]{1,0:T(8,128)(2,1)} %collective-permute-done.3), kind=kLoop, calls=%fused_computation.30 | loop fusion | bytes 524288
  47.8 1.8 %collective-permute-done.4 = bf16[128,1024]{1,0:T(8,128)(2,1)S(1)} collective-permute-done((bf16[128,1024]{1,0:T(8,128)(2,1)}, bf16[128,1024]{1,0:T(8,128)(2,1)S(1)}, u32[]{:S(2)}, u32[]{:S(2)}) %collective-permute-start.4) | collective-permute-done | bytes 262176 | tf_op jit(solution)/shard_map/ppermute | solution.py:247
  50.3 1.7 %constant_dynamic-update-slice_fusion.1 = bf16[1024,1024]{1,0:T(8,128)(2,1)} fusion(bf16[1024,1024]{1,0:T(8,128)(2,1)} %constant_dynamic-update-slice_fusion.2, bf16[128,1024]{1,0:T(8,128)(2,1)} %collective-permute-done.5), kind=kLoop, calls=%fused_computation.28 | loop fusion | bytes 524288
  52.0 1.6 %collective-permute-done.6 = bf16[128,1024]{1,0:T(8,128)(2,1)S(1)} collective-permute-done((bf16[128,1024]{1,0:T(8,128)(2,1)}, bf16[128,1024]{1,0:T(8,128)(2,1)S(1)}, u32[]{:S(2)}, u32[]{:S(2)}) %collective-permute-start.6) | collective-permute-done | bytes 262176 | tf_op jit(solution)/shard_map/ppermute | solution.py:247
  54.3 14.1 %attention.1.grad_ref = bf16[4,1024,256]{2,1,0:T(8,128)(2,1)S(1)} custom-call(bf16[1024,1024]{1,0:T(8,128)(2,1)} %constant_dynamic-update-slice_fusion.q_ref.k_ref.v_ref.do_ref, bf16[1024,1024]{1,0:T(8,128)(2,1)} %constant_dynamic-update-slice_fusion.q_ref.k_ref.v_ref.do_ref, bf16[1024,1024]{1,0:T(8,128)(2,1)} %constant_dynamic-update-slice_fusion.q_ref.k_ref.v_ref.do_ref, ...), custom_call_target="tpu_custom_call" | custom-call | tf_op jit(solution)/shard_map/attention/pallas_call | solution.py:171
  68.5 1.3 %copy-done = bf16[4,1024,256]{2,1,0:T(8,128)(2,1)} copy-done((bf16[4,1024,256]{2,1,0:T(8,128)(2,1)}, bf16[4,1024,256]{2,1,0:T(8,128)(2,1)S(1)}, u32[]{:S(2)}) %copy-start) | copy-done | bytes 2097176
  69.8 4.5 %spread.1 = (f32[4,136,512]{2,1,0:T(8,128)S(1)}, f32[128,1]{1,0:T(8,128)S(1)}) custom-call(s32[2]{0:T(128)S(1)} %pad_add_fusion.at_ref, bf16[4,1024,256]{2,1,0:T(8,128)(2,1)} %copy-done, bf16[3,2048,256]{2,1,0:T(8,128)(2,1)} %bitcast.47, bf16[128,2048]{1,0:T(8,128)(2,1)S(1)} %copy-done.4, f32[1,2048]{1,0:T(1,128)S(1)} %bitcast.43, ...), custom_call_target="tpu_custom_call" | custom-call | tf_op jit(solution)/shard_map/spread/pallas_call | solution.py:218
  74.5 1.8 %copy-done.1 = bf16[4,1024,256]{2,1,0:T(8,128)(2,1)S(1)} copy-done((bf16[4,1024,256]{2,1,0:T(8,128)(2,1)S(1)}, bf16[4,1024,256]{2,1,0:T(8,128)(2,1)}, u32[]{:S(2)}) %copy-start.1) | copy-done | bytes 2097176
  78.5 1.5 %collective-permute-start.10 = (f32[136,512]{1,0:T(8,128)}, f32[136,512]{1,0:T(8,128)}, u32[]{:S(2)}, u32[]{:S(2)}) collective-permute-start(f32[136,512]{1,0:T(8,128)} %fusion), channel_id=1, source_target_pairs={{0,2},{1,3},{2,0},{3,1},{4,6},{5,7},{6,4},{7,5},{8,10},{9,11},{10,... | collective-permute-start | bytes 835592 | tf_op jit(solution)/shard_map/ppermute | solution.py:247
  80.0 1.9 %fusion.9 = f32[128,512]{1,0:T(8,128)} fusion(f32[2,128,512]{2,1,0:T(8,128)S(1)} %collective-permute-done.7, f32[128,2048]{1,0:T(8,128)} %copy-done.13, s32[]{:T(128)S(6)} %select_n.51), kind=kLoop, calls=%fused_computation.18 | loop fusion | flops 65536 | bytes 786436 | tf_op jit(solution)/shard_map/add | solution.py:252
  83.1 5.2 %collective-permute-done.10 = f32[136,512]{1,0:T(8,128)} collective-permute-done((f32[136,512]{1,0:T(8,128)}, f32[136,512]{1,0:T(8,128)}, u32[]{:S(2)}, u32[]{:S(2)}) %collective-permute-start.10) | collective-permute-done | bytes 278560 | tf_op jit(solution)/shard_map/ppermute | solution.py:247
  89.6 1.2 %collective-permute-done.11 = f32[128,1]{1,0:T(8,128)S(1)} collective-permute-done((f32[128,1]{1,0:T(8,128)S(1)}, f32[128,1]{1,0:T(8,128)S(1)}, u32[]{:S(2)}, u32[]{:S(2)}) %collective-permute-start.11) | collective-permute-done | bytes 544 | tf_op jit(solution)/shard_map/ppermute | solution.py:247
  90.9 1.6 %collective-permute-start.12 = (f32[128,1]{1,0:T(8,128)S(1)}, f32[128,1]{1,0:T(8,128)S(1)}, u32[]{:S(2)}, u32[]{:S(2)}) collective-permute-start(f32[128,1]{1,0:T(8,128)S(1)} %add.106), channel_id=1, source_target_pairs={{0,2},{1,3},{2,0},{3,1},{4,6},{5,7},{6,4},{7,5},{8,10},{9,11},{10,... | collective-permute-start | bytes 1544 | tf_op jit(solution)/shard_map/ppermute | solution.py:247
  93.1 9.6 %collective-permute-start.14 = (f32[512]{0:T(512)S(1)}, f32[512]{0:T(512)S(1)}, u32[]{:S(2)}, u32[]{:S(2)}) collective-permute-start(f32[512]{0:T(512)S(1)} %add.109), channel_id=1, source_target_pairs={{0,8},{4,12},{8,0},{12,4},{16,24},{20,28},{24,16},{28,20},{1,9},{5... | collective-permute-start | bytes 6152 | tf_op jit(solution)/shard_map/ppermute | solution.py:247
  102.8 1.4 %collective-permute-done.14 = f32[512]{0:T(512)S(1)} collective-permute-done((f32[512]{0:T(512)S(1)}, f32[512]{0:T(512)S(1)}, u32[]{:S(2)}, u32[]{:S(2)}) %collective-permute-start.14) | collective-permute-done | bytes 2080 | tf_op jit(solution)/shard_map/ppermute | solution.py:247
  104.3 3.0 %collective-permute-start.15 = (f32[512]{0:T(512)S(1)}, f32[512]{0:T(512)S(1)}, u32[]{:S(2)}, u32[]{:S(2)}) collective-permute-start(f32[512]{0:T(512)S(1)} %add.110), channel_id=1, source_target_pairs={{0,16},{4,20},{8,24},{12,28},{16,0},{20,4},{24,8},{28,12},{1,17},{... | collective-permute-start | bytes 6152 | tf_op jit(solution)/shard_map/ppermute | solution.py:247
  107.3 2.2 %fusion.7 = (f32[128,512]{1,0:T(8,128)}, bf16[128,512]{1,0:T(8,128)(2,1)}) fusion(f32[136,512]{1,0:T(8,128)S(1)} %fusion.2, f32[128,2048]{1,0:T(8,128)} %copy-done.5, s32[]{:T(128)S(6)} %select_n.40, f32[128]{0:T(128)S(1)} %multiply_reduce_fusion, f32[512]{0:T(512)S(1)} %dynamic-slice.3, f32[128]{0:T(128)S(1)} %reduce, bf16[128,2048]{1,0:T(8,128)(2,1)} %up_ref.1, ...), kind=kLoop, calls=%fused_computation.14 | loop fusion | flops 851968 | bytes 1969156 | tf_op jit(solution)/shard_map/add | solution.py:339
  110.1 6.7 %weight_grads.1 = (f32[3,256,256]{2,1,0:T(8,128)}, f32[256,256]{1,0:T(8,128)}) custom-call(s32[1]{0:T(128)} %bitcast.13.at_ref, bf16[8,2,128,256]{3,2,1,0:T(8,128)(2,1)} %bitcast.18.both_ref, bf16[4,1024,256]{2,1,0:T(8,128)(2,1)S(1)} %copy-done.1), custom_call_target="tpu_custom_call" | custom-call | tf_op jit(solution)/shard_map/weight_grads/pallas_call | solution.py:277
  (81 shorter events, 14.0 us)
Async XLA Ops:
  0.6 1.0 copy-start.3
  1.7 1.2 %copy-start.7 = (bf16[256,2048]{1,0:T(8,128)(2,1)S(1)}, bf16[256,2048]{1,0:T(8,128)(2,1)}, u32[]{:S(2)}) copy-start(bf16[256,2048]{1,0:T(8,128)(2,1)} %wout_ref.1) | copy-start | bytes 3145732
  2.9 1.0 copy-start.9
  11.1 30.0 %collective-permute-start = (bf16[128,1024]{1,0:T(8,128)(2,1)S(1)}, bf16[128,1024]{1,0:T(8,128)(2,1)}, u32[]{:S(2)}, u32[]{:S(2)}) collective-permute-start(bf16[128,1024]{1,0:T(8,128)(2,1)S(1)} %get-tuple-element.12), channel_id=1, source_target_pairs={{0,4},{4,0},{8,12},{12,8},{16,20},{20,16},{24,28},{28,24},{1,5},{5... | collective-permute-start | bytes 786440 | tf_op jit(solution)/shard_map/ppermute | solution.py:247
  14.1 12.9 %collective-permute-start.1 = (bf16[128,1024]{1,0:T(8,128)(2,1)S(1)}, bf16[128,1024]{1,0:T(8,128)(2,1)}, u32[]{:S(2)}, u32[]{:S(2)}) collective-permute-start(bf16[128,1024]{1,0:T(8,128)(2,1)S(1)} %get-tuple-element.12), channel_id=1, source_target_pairs={{0,8},{4,12},{8,0},{12,4},{16,24},{20,28},{24,16},{28,20},{1,9},{5... | collective-permute-start | bytes 786440 | tf_op jit(solution)/shard_map/ppermute | solution.py:247
  15.7 22.1 %collective-permute-start.3 = (bf16[128,1024]{1,0:T(8,128)(2,1)S(1)}, bf16[128,1024]{1,0:T(8,128)(2,1)}, u32[]{:S(2)}, u32[]{:S(2)}) collective-permute-start(bf16[128,1024]{1,0:T(8,128)(2,1)S(1)} %get-tuple-element.12), channel_id=1, source_target_pairs={{0,16},{4,20},{8,24},{12,28},{16,0},{20,4},{24,8},{28,12},{1,17},{... | collective-permute-start | bytes 786440 | tf_op jit(solution)/shard_map/ppermute | solution.py:247
  18.3 26.1 %collective-permute-start.5 = (bf16[128,1024]{1,0:T(8,128)(2,1)S(1)}, bf16[128,1024]{1,0:T(8,128)(2,1)}, u32[]{:S(2)}, u32[]{:S(2)}) collective-permute-start(bf16[128,1024]{1,0:T(8,128)(2,1)S(1)} %get-tuple-element.12), channel_id=1, source_target_pairs={{0,24},{4,28},{8,16},{12,20},{16,8},{20,12},{24,0},{28,4},{1,25},{... | collective-permute-start | bytes 786440 | tf_op jit(solution)/shard_map/ppermute | solution.py:247
  19.2 6.6 %copy-start.16 = (s32[1024]{0:T(1024)S(1)}, s32[1024]{0:T(1024)}, u32[]{:S(2)}) copy-start(s32[1024]{0:T(1024)} %param.8) | copy-start | bytes 12292
  20.5 8.8 %copy-start.2 = (s32[2,128,2048]{2,1,0:T(8,128)S(1)}, s32[2,128,2048]{2,1,0:T(8,128)}, u32[]{:S(2)}) copy-start(s32[2,128,2048]{2,1,0:T(8,128)} %pulse_ref.3) | copy-start | bytes 6291460
  20.5 8.8 %copy-start.4 = (bf16[128,2048]{1,0:T(8,128)(2,1)S(1)}, bf16[128,2048]{1,0:T(8,128)(2,1)}, u32[]{:S(2)}) copy-start(bf16[128,2048]{1,0:T(8,128)(2,1)} %tok_ref.5) | copy-start | bytes 1572868
  20.5 8.8 %copy-start.12 = (f32[2048]{0:T(1024)S(1)}, f32[2048]{0:T(1024)}, u32[]{:S(2)}) copy-start(f32[2048]{0:T(1024)} %param.10) | copy-start | bytes 24580
  20.5 89.5 %all-to-all-start = ((bf16[1,2,128,8,256]{4,2,1,0,3:T(8,128)(2,1)}), bf16[1,2,128,8,256]{4,2,1,0,3:T(8,128)(2,1)}, u32[]{:S(2)}, u32[]{:S(2)}) async-start(bf16[1,2,128,8,256]{4,2,1,0,3:T(8,128)(2,1)} %copy.20), calls=%async_computation | async-start | bytes 2097152 | tf_op jit(solution)/shard_map/all_to_all | solution.py:358
  27.0 17.4 %collective-permute-start.2 = (bf16[128,1024]{1,0:T(8,128)(2,1)}, bf16[128,1024]{1,0:T(8,128)(2,1)}, u32[]{:S(2)}, u32[]{:S(2)}) collective-permute-start(bf16[128,1024]{1,0:T(8,128)(2,1)} %collective-permute-done.1), channel_id=1, source_target_pairs={{0,4},{4,0},{8,12},{12,8},{16,20},{20,16},{24,28},{28,24},{1,5},{5... | collective-permute-start | bytes 786440 | tf_op jit(solution)/shard_map/ppermute | solution.py:247
  31.6 1.0 copy-start.5
  37.8 11.8 %collective-permute-start.4 = (bf16[128,1024]{1,0:T(8,128)(2,1)}, bf16[128,1024]{1,0:T(8,128)(2,1)S(1)}, u32[]{:S(2)}, u32[]{:S(2)}) collective-permute-start(bf16[128,1024]{1,0:T(8,128)(2,1)} %collective-permute-done.3), channel_id=1, source_target_pairs={{0,4},{4,0},{8,12},{12,8},{16,20},{20,16},{24,28},{28,24},{1,5},{5... | collective-permute-start | bytes 786440 | tf_op jit(solution)/shard_map/ppermute | solution.py:247
  44.4 9.2 %collective-permute-start.6 = (bf16[128,1024]{1,0:T(8,128)(2,1)}, bf16[128,1024]{1,0:T(8,128)(2,1)S(1)}, u32[]{:S(2)}, u32[]{:S(2)}) collective-permute-start(bf16[128,1024]{1,0:T(8,128)(2,1)} %collective-permute-done.5), channel_id=1, source_target_pairs={{0,4},{4,0},{8,12},{12,8},{16,20},{20,16},{24,28},{28,24},{1,5},{5... | collective-permute-start | bytes 786440 | tf_op jit(solution)/shard_map/ppermute | solution.py:247
  54.3 15.5 %copy-start.6 = (f32[128,2048]{1,0:T(8,128)S(1)}, f32[128,2048]{1,0:T(8,128)}, u32[]{:S(2)}) copy-start(f32[128,2048]{1,0:T(8,128)} %copy-done.5) | copy-start | bytes 3145732
  68.4 1.3 %copy-start = (bf16[4,1024,256]{2,1,0:T(8,128)(2,1)}, bf16[4,1024,256]{2,1,0:T(8,128)(2,1)S(1)}, u32[]{:S(2)}) copy-start(bf16[4,1024,256]{2,1,0:T(8,128)(2,1)S(1)} %attention.1.grad_ref) | copy-start | bytes 6291460
  69.8 4.7 %copy-start.8 = (bf16[256,2048]{1,0:T(8,128)(2,1)S(1)}, bf16[256,2048]{1,0:T(8,128)(2,1)}, u32[]{:S(2)}) copy-start(bf16[256,2048]{1,0:T(8,128)(2,1)} %wout_ref.1) | copy-start | bytes 3145732
  74.3 3.3 %copy-start.10 = (f32[4,136,512]{2,1,0:T(8,128)}, f32[4,136,512]{2,1,0:T(8,128)S(1)}, u32[]{:S(2)}) copy-start(f32[4,136,512]{2,1,0:T(8,128)S(1)} %get-tuple-element.14) | copy-start | bytes 3342340
  74.3 2.0 %copy-start.1 = (bf16[4,1024,256]{2,1,0:T(8,128)(2,1)S(1)}, bf16[4,1024,256]{2,1,0:T(8,128)(2,1)}, u32[]{:S(2)}) copy-start(bf16[4,1024,256]{2,1,0:T(8,128)(2,1)} %copy-done) | copy-start | bytes 6291460
  74.4 3.2 %collective-permute-start.9 = (f32[2,136,512]{2,1,0:T(8,128)S(1)}, f32[2,136,512]{2,1,0:T(8,128)S(1)}, u32[]{:S(2)}, u32[]{:S(2)}) collective-permute-start(f32[2,136,512]{2,1,0:T(8,128)S(1)} %pad_maximum_fusion.1), channel_id=1, source_target_pairs={{0,1},{1,0},{2,3},{3,2},{4,5},{5,4},{6,7},{7,6},{8,9},{9,8},{10,11... | collective-permute-start | bytes 1671176 | tf_op jit(solution)/shard_map/ppermute | solution.py:247
  76.6 1.8 %copy-start.13 = (f32[128,2048]{1,0:T(8,128)}, f32[128,2048]{1,0:T(8,128)S(1)}, u32[]{:S(2)}) copy-start(f32[128,2048]{1,0:T(8,128)S(1)} %fusion.12) | copy-start | bytes 3145732
  77.6 2.4 %collective-permute-start.7 = (f32[2,128,512]{2,1,0:T(8,128)}, f32[2,128,512]{2,1,0:T(8,128)S(1)}, u32[]{:S(2)}, u32[]{:S(2)}) collective-permute-start(f32[2,128,512]{2,1,0:T(8,128)} %pad_maximum_fusion.2), channel_id=1, source_target_pairs={{0,1},{1,0},{2,3},{3,2},{4,5},{5,4},{6,7},{7,6},{8,9},{9,8},{10,11... | collective-permute-start | bytes 1572872 | tf_op jit(solution)/shard_map/ppermute | solution.py:247
  78.5 9.8 %collective-permute-start.10 = (f32[136,512]{1,0:T(8,128)}, f32[136,512]{1,0:T(8,128)}, u32[]{:S(2)}, u32[]{:S(2)}) collective-permute-start(f32[136,512]{1,0:T(8,128)} %fusion), channel_id=1, source_target_pairs={{0,2},{1,3},{2,0},{3,1},{4,6},{5,7},{6,4},{7,5},{8,10},{9,11},{10,... | collective-permute-start | bytes 835592 | tf_op jit(solution)/shard_map/ppermute | solution.py:247
  80.0 3.1 %copy-start.15 = (f32[2,128,512]{2,1,0:T(8,128)}, f32[2,128,512]{2,1,0:T(8,128)S(1)}, u32[]{:S(2)}) copy-start(f32[2,128,512]{2,1,0:T(8,128)S(1)} %collective-permute-done.7) | copy-start | bytes 1572868
  81.9 25.4 %collective-permute-start.8 = (f32[128,512]{1,0:T(8,128)}, f32[128,512]{1,0:T(8,128)}, u32[]{:S(2)}, u32[]{:S(2)}) collective-permute-start(f32[128,512]{1,0:T(8,128)} %fusion.9), channel_id=1, source_target_pairs={{0,2},{1,3},{2,0},{3,1},{4,6},{5,7},{6,4},{7,5},{8,10},{9,11},{10,... | collective-permute-start | bytes 786440 | tf_op jit(solution)/shard_map/ppermute | solution.py:247
  89.5 3.7 %collective-permute-start.13 = (f32[512]{0:T(512)S(1)}, f32[512]{0:T(512)S(1)}, u32[]{:S(2)}, u32[]{:S(2)}) collective-permute-start(f32[512]{0:T(512)S(1)} %bitcast.50), channel_id=1, source_target_pairs={{0,4},{4,0},{8,12},{12,8},{16,20},{20,16},{24,28},{28,24},{1,5},{5... | collective-permute-start | bytes 6152 | tf_op jit(solution)/shard_map/ppermute | solution.py:247
  89.6 1.3 %collective-permute-start.11 = (f32[128,1]{1,0:T(8,128)S(1)}, f32[128,1]{1,0:T(8,128)S(1)}, u32[]{:S(2)}, u32[]{:S(2)}) collective-permute-start(f32[128,1]{1,0:T(8,128)S(1)} %get-tuple-element.15), channel_id=1, source_target_pairs={{0,1},{1,0},{2,3},{3,2},{4,5},{5,4},{6,7},{7,6},{8,9},{9,8},{10,11... | collective-permute-start | bytes 1544 | tf_op jit(solution)/shard_map/ppermute | solution.py:247
  90.9 11.8 %collective-permute-start.12 = (f32[128,1]{1,0:T(8,128)S(1)}, f32[128,1]{1,0:T(8,128)S(1)}, u32[]{:S(2)}, u32[]{:S(2)}) collective-permute-start(f32[128,1]{1,0:T(8,128)S(1)} %add.106), channel_id=1, source_target_pairs={{0,2},{1,3},{2,0},{3,1},{4,6},{5,7},{6,4},{7,5},{8,10},{9,11},{10,... | collective-permute-start | bytes 1544 | tf_op jit(solution)/shard_map/ppermute | solution.py:247
  93.1 11.1 %collective-permute-start.14 = (f32[512]{0:T(512)S(1)}, f32[512]{0:T(512)S(1)}, u32[]{:S(2)}, u32[]{:S(2)}) collective-permute-start(f32[512]{0:T(512)S(1)} %add.109), channel_id=1, source_target_pairs={{0,8},{4,12},{8,0},{12,4},{16,24},{20,28},{24,16},{28,20},{1,9},{5... | collective-permute-start | bytes 6152 | tf_op jit(solution)/shard_map/ppermute | solution.py:247
  104.3 5.2 %collective-permute-start.15 = (f32[512]{0:T(512)S(1)}, f32[512]{0:T(512)S(1)}, u32[]{:S(2)}, u32[]{:S(2)}) collective-permute-start(f32[512]{0:T(512)S(1)} %add.110), channel_id=1, source_target_pairs={{0,16},{4,20},{8,24},{12,28},{16,0},{20,4},{24,8},{28,12},{1,17},{... | collective-permute-start | bytes 6152 | tf_op jit(solution)/shard_map/ppermute | solution.py:247
  (2 other events, 1.6 us)

commit v2 on v1

v2 whole, which is shorter than its diff:
```python
import functools

import jax
import jax.numpy as jnp
from jax import lax
from jax.experimental import pallas as pl
from jax.experimental.pallas import tpu as pltpu
from jax.sharding import PartitionSpec as P

HEAD_DIM = 128
SOFT_CAP = 30.0
LEAK_RATE = 0.5
THRESHOLD = 1.0
SURROGATE_SLOPE = 4.0
EPSILON = 1e-05
SUM_ROWS = 8
LOG2_E = 1.4426950408889634
F32 = jnp.float32
BF16 = jnp.bfloat16


def dot(a, b, dims):
    return lax.dot_general(a, b, (dims, ((), ())), preferred_element_type=F32)


NN = ((1,), (0,))
NT = ((1,), (1,))
TN = ((0,), (0,))


def params(mebibytes=50):
    return pltpu.CompilerParams(vmem_limit_bytes=mebibytes << 20)


def project_kernel(
    tok_hbm, pulse_hbm, gain_hbm, win_hbm, up_hbm, wout_hbm, pay_ref, spikes_ref, inv_ref,
    tok_ref, pulse_ref, gain_ref, win_ref, up_ref, wout_ref, acc_ref, sems, block_sems,
):
    model = tok_ref.shape[1]
    local = wout_ref.shape[0]
    blocks = block_sems.shape[0]
    width = model // blocks
    whole = [
        pltpu.make_async_copy(source, target, sems.at[k])
        for k, (source, target) in enumerate(
            [(tok_hbm, tok_ref), (gain_hbm, gain_ref), (up_hbm, up_ref), (wout_hbm, wout_ref)]
        )
    ]
    pairs = []
    for k in range(blocks):
        here = pl.ds(k * width, width)
        pulse = (pulse_hbm.at[:, :, here], pulse_ref.at[:, :, here])
        weight = (win_hbm.at[:, here, :], win_ref.at[:, here, :])
        pairs.append(
            [
                pltpu.make_async_copy(*ends, block_sems.at[k, n])
                for n, ends in enumerate((pulse, weight))
            ]
        )
    for copy in whole:
        copy.start()
    for pair in pairs:
        for copy in pair:
            copy.start()
    whole[0].wait()
    values = tok_ref[...].astype(F32)
    inv = lax.rsqrt(jnp.mean(values * values, axis=-1, keepdims=True) + EPSILON)
    inv_ref[...] = inv
    for copy in whole[1:]:
        copy.wait()
    pay_ref[:, 3 * local :] = dot(up_ref[...], wout_ref[...], NT).astype(BF16)
    for k, pair in enumerate(pairs):
        here = slice(k * width, (k + 1) * width)
        pair[0].wait()
        current = tok_ref[:, here].astype(F32) * inv * gain_ref[:, here]
        first = pulse_ref[0, :, here].astype(F32)
        second = pulse_ref[1, :, here].astype(F32)
        later = LEAK_RATE * current * (1.0 - first) + current
        spikes = ((first * current + second * later) * 0.5).astype(BF16)
        spikes_ref[:, here] = spikes
        pair[1].wait()
        for part in range(3):
            columns = slice(part * local, (part + 1) * local)
            share = dot(spikes, win_ref[part, here, :], NN)
            acc_ref[:, columns] = share if k == 0 else acc_ref[:, columns] + share
    pay_ref[:, : 3 * local] = acc_ref[...].astype(BF16)


def project(tokens, pulse, gain, win, upstream, wout):
    rows, model = tokens.shape
    local = wout.shape[0]
    blocks = 4
    arrays = (tokens, pulse, gain, win, upstream, wout)
    in_vmem = pl.BlockSpec(memory_space=pltpu.VMEM)
    return pl.pallas_call(
        project_kernel,
        in_specs=[pl.BlockSpec(memory_space=pltpu.HBM)] * 6,
        out_specs=[in_vmem] * 3,
        out_shape=[
            jax.ShapeDtypeStruct((rows, 4 * local), BF16),
            jax.ShapeDtypeStruct((rows, model), BF16),
            jax.ShapeDtypeStruct((rows, 1), F32),
        ],
        scratch_shapes=[pltpu.VMEM(array.shape, array.dtype) for array in arrays]
        + [
            pltpu.VMEM((rows, 3 * local), F32),
            pltpu.SemaphoreType.DMA((4,)),
            pltpu.SemaphoreType.DMA((blocks, 2)),
        ],
        compiler_params=params(24),
        name="project",
    )(*(pltpu.with_memory_space_constraint(array, pltpu.HBM) for array in arrays))


def factor_kernel(
    at_ref, tok_ref, pulse_ref, gain_ref, inv_ref, up_ref, factor_ref, rise_ref, fall_ref, base_ref, own_ref
):
    model = tok_ref.shape[1]
    width = own_ref.shape[1]
    inv, gain = inv_ref[...], gain_ref[...]
    current = tok_ref[...].astype(F32) * inv * gain
    first = pulse_ref[0].astype(F32)
    second = pulse_ref[1].astype(F32)
    later = LEAK_RATE * current * (1.0 - first) + current

    def slope(fired, membrane):
        level = jax.nn.sigmoid(SURROGATE_SLOPE * (membrane - THRESHOLD))
        return fired + membrane * SURROGATE_SLOPE * level * (1.0 - level)

    carried = 1.0 + LEAK_RATE * (1.0 - first)
    factor_ref[...] = 0.5 * (slope(first, current) + slope(second, later) * carried)
    here = pl.ds(pl.multiple_of(at_ref[0] * width, width), width)
    own = tok_ref[:, here].astype(F32)
    own_ref[...] = own
    base_ref[...] = up_ref[:, here].astype(F32)
    rise_ref[...] = factor_ref[:, here] * gain_ref[:, here] * inv
    fall_ref[...] = own * inv * (inv / model)


def factors(fsdp_rank, tokens, pulse, gain, inv, upstream, share):
    rows, model = tokens.shape
    in_vmem = pl.BlockSpec(memory_space=pltpu.VMEM)
    return pl.pallas_call(
        factor_kernel,
        in_specs=[pl.BlockSpec(memory_space=pltpu.SMEM)] + [in_vmem] * 5,
        out_specs=[in_vmem] * 5,
        out_shape=[jax.ShapeDtypeStruct((rows, model), F32)]
        + [jax.ShapeDtypeStruct((rows, share), F32)] * 4,
        compiler_params=params(24),
        name="factors",
    )(fsdp_rank[None], tokens, pulse, gain, inv, upstream)


def after(value, *others):
    return lax.optimization_barrier((value, others))[0]


def attend(query, keys, values, grad, allowed):
    scale = HEAD_DIM**-0.5
    squashed = jnp.tanh(dot(query, keys, NT) * (scale / SOFT_CAP))
    exponent = jnp.where(allowed, jnp.exp2((SOFT_CAP * LOG2_E) * squashed), 0.0)
    prob = exponent * (1.0 / jnp.sum(exponent, axis=-1, keepdims=True))
    low = prob.astype(BF16)
    grad_prob = dot(grad, values, NT)
    delta = jnp.sum(prob * grad_prob, axis=-1, keepdims=True)
    score_grad = (prob * (grad_prob - delta) * ((1.0 - squashed * squashed) * scale)).astype(BF16)
    attended = dot(low, values, NN).astype(BF16)
    grad_query = dot(score_grad, keys, NN).astype(BF16)
    return attended, grad_query, dot(score_grad, query, TN), dot(low, grad, TN)


def attention_kernel(*refs):
    *piece_refs, prow_ref, pcol_ref, out_ref, all_ref, dk_ref, dv_ref = refs
    rows = piece_refs[0].shape[0]
    length, width = all_ref.shape
    local = width // 4
    block = length // 2
    for j, piece in enumerate(piece_refs):
        all_ref[j * rows : (j + 1) * rows, :] = piece[...]
    dk_ref[...] = jnp.zeros_like(dk_ref)
    dv_ref[...] = jnp.zeros_like(dv_ref)

    def visit(step, carry):
        at = pl.ds(pl.multiple_of(step * block, block), block)
        allowed = prow_ref[...] <= pcol_ref[at, :]
        for low in range(0, local, HEAD_DIM):
            query, keys, values, grad = (
                slice(part * local + low, part * local + low + HEAD_DIM) for part in range(4)
            )
            here = slice(low, low + HEAD_DIM)
            attended, grad_query, key_part, value_part = attend(
                all_ref[at, query], all_ref[:, keys], all_ref[:, values], all_ref[at, grad], allowed
            )
            out_ref[3, at, here] = attended
            out_ref[0, at, here] = grad_query
            dk_ref[:, here] += key_part
            dv_ref[:, here] += value_part
        return carry

    lax.fori_loop(0, length // block, visit, 0)
    out_ref[1] = dk_ref[...].astype(BF16)
    out_ref[2] = dv_ref[...].astype(BF16)


def attention(pieces, positions):
    rows, width = pieces[0].shape
    length, local = len(pieces) * rows, width // 4
    in_vmem = pl.BlockSpec(memory_space=pltpu.VMEM)
    return pl.pallas_call(
        attention_kernel,
        in_specs=[in_vmem] * (len(pieces) + 2),
        out_specs=in_vmem,
        out_shape=jax.ShapeDtypeStruct((4, length, local), BF16),
        scratch_shapes=[pltpu.VMEM((length, width), BF16)]
        + [pltpu.VMEM((length, local), F32)] * 2,
        compiler_params=params(36),
        name="attention",
    )(*pieces, positions[None, :], positions[:, None])


def long_kernel(q_ref, k_ref, v_ref, do_ref, prow_ref, pcol_ref, out_ref, dk_ref, dv_ref):
    step = pl.program_id(1)
    block = q_ref.shape[0]

    @pl.when(step == 0)
    def _():
        dk_ref[...] = jnp.zeros_like(dk_ref)
        dv_ref[...] = jnp.zeros_like(dv_ref)

    attended, grad_query, key_part, value_part = attend(
        q_ref[...], k_ref[...], v_ref[...], do_ref[...], prow_ref[...] <= pcol_ref[...]
    )
    at = pl.ds(pl.multiple_of(step * block, block), block)
    out_ref[3, at, :] = attended
    out_ref[0, at, :] = grad_query
    dk_ref[...] += key_part
    dv_ref[...] += value_part

    @pl.when(step == pl.num_programs(1) - 1)
    def _():
        out_ref[1] = dk_ref[...].astype(BF16)
        out_ref[2] = dv_ref[...].astype(BF16)


def long_attention(gathered, positions):
    length, width = gathered.shape
    heads = width // (4 * HEAD_DIM)
    block = max(16, (256 * 1024) // length)
    whole = functools.partial(pl.BlockSpec, (length, HEAD_DIM))
    part = functools.partial(pl.BlockSpec, (block, HEAD_DIM))
    return pl.pallas_call(
        long_kernel,
        grid=(heads, length // block),
        in_specs=[
            part(lambda h, i: (i, h)),
            whole(lambda h, i: (0, heads + h)),
            whole(lambda h, i: (0, 2 * heads + h)),
            part(lambda h, i: (i, 3 * heads + h)),
            pl.BlockSpec((1, length), lambda h, i: (0, 0)),
            pl.BlockSpec((block, 1), lambda h, i: (i, 0)),
        ],
        out_specs=pl.BlockSpec((4, length, HEAD_DIM), lambda h, i: (0, 0, h)),
        out_shape=jax.ShapeDtypeStruct((4, length, heads * HEAD_DIM), BF16),
        scratch_shapes=[pltpu.VMEM((length, HEAD_DIM), F32)] * 2,
        compiler_params=params(),
        name="long_attention",
    )(gathered, gathered, gathered, gathered, positions[None, :], positions[:, None])


def spread_kernel(
    at_ref, grad_ref, win_ref, wout_ref, tok_ref, gain_ref, inv_ref, factor_ref,
    own_ref, far_ref, near_ref, own_out_ref, far_out_ref, near_out_ref, gain_out_ref,
):
    rows = tok_ref.shape[0]
    width = own_ref.shape[1]
    sums = jnp.zeros((rows, 1), F32)
    targets = (own_ref, near_ref.at[1], far_ref, near_ref.at[0])
    out_targets = (own_out_ref, near_out_ref.at[1], far_out_ref, near_out_ref.at[0])
    for k in range(4):
        here = pl.ds(pl.multiple_of((at_ref[0] ^ k) * width, width), width)
        share = sum(dot(grad_ref[part], win_ref[part, here, :], NT) for part in range(3))
        targets[k][:rows, :] = share
        out_targets[k][...] = dot(grad_ref[3], wout_ref[:, here], NN)
        weighted = share * factor_ref[:, here] * (tok_ref[:, here].astype(F32) * inv_ref[...])
        gain_out_ref[k : k + 1, :] = jnp.sum(weighted, axis=0, keepdims=True)
        sums += jnp.sum(weighted * gain_ref[:, here], axis=1, keepdims=True)
    line = jnp.broadcast_to(sums, (rows, rows)).T[:SUM_ROWS, :]
    for target in targets:
        target[rows:, :] = jnp.broadcast_to(line[:, :1], (SUM_ROWS, width))
        target[rows:, :rows] = line


def spread(fsdp_rank, own_grads, win, wout, tokens, gain, inv, factor):
    rows, model = tokens.shape
    width = model // 4
    in_vmem = pl.BlockSpec(memory_space=pltpu.VMEM)
    tall = jax.ShapeDtypeStruct((rows + SUM_ROWS, width), F32)
    flat = jax.ShapeDtypeStruct((rows, width), F32)
    return pl.pallas_call(
        spread_kernel,
        in_specs=[pl.BlockSpec(memory_space=pltpu.SMEM)] + [in_vmem] * 7,
        out_specs=[in_vmem] * 7,
        out_shape=[
            tall,
            tall,
            jax.ShapeDtypeStruct((2,) + tall.shape, F32),
            flat,
            flat,
            jax.ShapeDtypeStruct((2,) + flat.shape, F32),
            jax.ShapeDtypeStruct((4, width), F32),
        ],
        compiler_params=params(24),
        name="spread",
    )(fsdp_rank[None], own_grads, win, wout, tokens, gain, inv, factor)


def swap(value, axis, mask):
    count = lax.axis_size(axis)
    return lax.ppermute(value, axis, [(i, i ^ mask) for i in range(count)])


def weight_kernel(at_ref, *refs):
    *piece_refs, grad_ref, in_ref, out_ref, both_ref = refs
    ranks, rows, width = piece_refs[0].shape
    features = width // 2
    for k, piece in enumerate(piece_refs):
        for j in range(ranks):
            low = (j * len(piece_refs) + (at_ref[0] ^ k)) * rows
            both_ref[pl.ds(pl.multiple_of(low, rows), rows), :] = piece[at_ref[1] ^ j]
    fired, wanted = both_ref[:, :features], both_ref[:, features:]
    for part in range(3):
        in_ref[part] = dot(fired, grad_ref[part], TN)
    out_ref[...] = dot(wanted, grad_ref[3], TN)


def weight_grads(fsdp_rank, turn, pieces, grads):
    features = pieces[0].shape[2] // 2
    local = grads.shape[2]
    in_vmem = pl.BlockSpec(memory_space=pltpu.VMEM)
    return pl.pallas_call(
        weight_kernel,
        in_specs=[pl.BlockSpec(memory_space=pltpu.SMEM)] + [in_vmem] * (len(pieces) + 1),
        out_specs=[in_vmem, in_vmem],
        out_shape=[
            jax.ShapeDtypeStruct((3, features, local), F32),
            jax.ShapeDtypeStruct((features, local), F32),
        ],
        scratch_shapes=[pltpu.VMEM((grads.shape[1], 2 * features), BF16)],
        compiler_params=params(),
        name="weight_grads",
    )(jnp.stack([fsdp_rank, turn]), *pieces, grads)


def body(tokens, positions, pulse_indicator, norm_gain, in_weight, out_weight, upstream):
    ctx, fsdp = lax.axis_size("ctx"), lax.axis_size("fsdp")
    ctx_rank, fsdp_rank = lax.axis_index("ctx"), lax.axis_index("fsdp")
    rows, model = tokens.shape
    local = out_weight.shape[0]
    share = model // fsdp
    gain = norm_gain[None, :]
    features = model // ctx
    win = jnp.transpose(in_weight, (1, 0, 2))
    payload, spikes, inv = project(tokens, pulse_indicator, gain, win, upstream, out_weight)
    factor, rise, fall, base, token_share = factors(
        fsdp_rank, tokens, pulse_indicator, gain, inv, upstream, share
    )

    short = ctx == 8 and fsdp == 4
    if short:
        beside = swap(payload, "ctx", 2)
        below = swap(payload, "ctx", 1)
        across = swap(payload, "ctx", 4)
        blocks = [payload, below, beside, swap(beside, "ctx", 1), across, swap(across, "ctx", 1)]
        corner = swap(across, "ctx", 2)
        blocks += [corner, swap(corner, "ctx", 1)]
        placed = jnp.concatenate(
            [lax.dynamic_slice_in_dim(positions, (ctx_rank ^ j) * rows, rows) for j in range(ctx)]
        )
        quarter = rows // fsdp
        both = jnp.stack([spikes, upstream], axis=1)
        both = lax.dynamic_slice_in_dim(both, fsdp_rank * quarter, quarter, 0)
        both = both.reshape(quarter, 2, ctx, features).transpose(2, 0, 1, 3)
        both = after(both.reshape(ctx, quarter, 2 * features), below)
        both = lax.all_to_all(both, "ctx", 0, 0)
        over = swap(both, "fsdp", 2)
        pieces = [both, swap(both, "fsdp", 1), over, swap(over, "fsdp", 1)]
        grads = attention(blocks, after(placed, over))
        own_grads = grads[:, :rows]
        in_grad, out_grad = weight_grads(fsdp_rank, ctx_rank, pieces, grads)
    else:
        grads = long_attention(lax.all_gather(payload, "ctx", axis=0, tiled=True), positions)
        own_grads = lax.dynamic_slice_in_dim(grads, ctx_rank * rows, rows, 1)
        fired, wanted = (
            lax.all_to_all(array.reshape(rows, ctx, features), "ctx", 1, 0).reshape(-1, features)
            for array in (spikes, upstream)
        )
        in_grad = jnp.stack([dot(fired, grads[part], TN) for part in range(3)])
        out_grad = dot(wanted, grads[3], TN)

    own, far, near, own_out, far_out, near_out, gains = spread(
        fsdp_rank, own_grads, win, out_weight, tokens, gain, inv, factor
    )
    near = swap(near, "fsdp", 1)
    far = far + near[0]
    landed = swap(far, "fsdp", 2)
    near_out = swap(after(near_out, far), "fsdp", 1)
    landed_out = swap(far_out + near_out[0], "fsdp", 2)
    if short:
        gains = gains + swap(gains, "ctx", 1)
        gains = after(gains, far)
        for mask in (2, 4):
            gains = gains + swap(gains, "ctx", mask)
        landed = after(landed, in_grad, out_grad)
    else:
        gains = lax.psum(gains, "ctx")
    gain_near = swap(jnp.stack([gains[3], gains[1]]), "fsdp", 1)
    gain_grad = gains[0] + gain_near[1] + swap(gains[2] + gain_near[0], "fsdp", 2)

    grad_spikes = own + near[1] + landed
    token_grad = base + (rise * grad_spikes[:rows] - fall * grad_spikes[rows, :rows][:, None])
    block_out = (token_share + (own_out + near_out[1] + landed_out)).astype(BF16)
    return (block_out, token_grad, gain_grad, jnp.transpose(in_grad, (1, 0, 2)), out_grad)


def solution(mesh):
    placed = (
        P("ctx", None),
        P(),
        P(None, "ctx", None),
        P(),
        P(None, None, "fsdp"),
        P("fsdp", None),
        P("ctx", None),
    )
    return jax.shard_map(
        body,
        mesh=mesh,
        in_specs=placed,
        out_specs=(
            P("ctx", "fsdp"),
            P("ctx", "fsdp"),
            P("fsdp"),
            P("ctx", None, "fsdp"),
            P("ctx", "fsdp"),
        ),
        check_vma=False,
    )
```

time: 118 us -> 92.7 us (0.79)
  local copies, waits for them, and re-layouts: 21.7 us -> 11 us
  Pallas kernels: 34 us -> 24.4 us
  starting transfers between devices: 35 us -> 26.1 us
  waiting for transfers between devices: 17 us -> 25.9 us
  other arithmetic: 7.98 us -> 4 us
    unnamed x49 -> x48, local copies, waits for them, and re-layouts: 18.9 us -> 7.89 us
    pallas_call x5, Pallas kernels: 34 us -> 24.4 us  [the longest x1 11.6 us: attention(): pl.pallas_call(attention_kernel, in_specs=[in_vmem] * (len(pieces) + 2),...]
    ppermute x16 -> x19, waiting for transfers between devices: 17 us -> 25.9 us  [swap(): return lax.ppermute(value, axis, [(i, i ^ mask) for i in range(count)])]
    ppermute x16 -> x19, starting transfers between devices: 29.8 us -> 22.5 us  [swap(): return lax.ppermute(value, axis, [(i, i ^ mask) for i in range(count)])]
    add x8 -> x9, other arithmetic: 6.64 us -> 1.54 us  [the longest x1 0.81 us: body(): base + (rise * grad_spikes[:rows] - fall * grad_spikes[rows, :rows][:, No...]
    reshape x0 -> x1, local copies, waits for them, and re-layouts: none -> 1.82 us  [body(): both = after(both.reshape(ctx, quarter, 2 * features), below)]
    all_to_all x1, starting transfers between devices: 5.14 us -> 3.59 us  [body(): both = lax.all_to_all(both, 'ctx', 0, 0)]
    another operation x3 -> x0, local copies, waits for them, and re-layouts: 1.45 us -> none  [the longest x1 1.33 us: body(): both = jnp.stack([spikes, upstream]).reshape(2, rows, ctx, features)]
  transfers between devices with their start and end apart: 17 -> 20, of which waited for: 7 -> 8; matrix products, arithmetic and copies ran while one was open for 19% -> 8% of each run, Pallas kernels for 18% -> 6%
where the time goes in v2:
time: 92.7 us; the launch traced here: 92.3 us
  starting transfers between devices  26.1 us (28%)
  waiting for transfers between devices  25.9 us (28%)
  Pallas kernels  24.4 us (26%)
  local copies, waits for them, and re-layouts  11 us (12%)
  other arithmetic  4 us (4%)
    ppermute x19, waiting for transfers between devices, swap(): return lax.ppermute(value, axis, [(i, i ^ mask) for i in range(count)])  25.9 us
    ppermute x19, starting transfers between devices, swap(): return lax.ppermute(value, axis, [(i, i ^ mask) for i in range(count)])  22.5 us
    pallas_call x1, Pallas kernels, attention(): pl.pallas_call(attention_kernel, in_specs=[in_vmem] * (len(pieces) + 2),...  11.6 us
    unnamed x48, local copies, waits for them, and re-layouts  7.89 us
    pallas_call x1, Pallas kernels, project(): pl.pallas_call(project_kernel, in_specs=[pl.BlockSpec(memory_space=pltpu....  6.1 us
    all_to_all x1, starting transfers between devices, body(): both = lax.all_to_all(both, 'ctx', 0, 0)  3.59 us
    pallas_call x1, Pallas kernels, weight_grads(): pl.pallas_call(weight_kernel, in_specs=[pl.BlockSpec(memory_space=pltpu.S...  2.81 us
    pallas_call x1, Pallas kernels, factors(): pl.pallas_call(factor_kernel, in_specs=[pl.BlockSpec(memory_space=pltpu.S...  2.4 us
  transfers between devices with their start and end apart: 20, of which 8 were waited for; matrix products, arithmetic and copies ran while one was open for 8% of the time, Pallas kernels for 6%

profile of v2, /device:TPU:0, one launch (start us, length us, event | category | flops | bytes accessed | tf_op | source)
XLA Modules:
  0.0 92.3 jit_solution(15634099812165388515)
XLA Ops:
  0.6 6.1 %project.1 = (bf16[128,1024]{1,0:T(8,128)(2,1)}, bf16[128,2048]{1,0:T(8,128)(2,1)S(1)}, f32[128,1]{1,0:T(8,128)S(1)}) custom-call(bf16[128,2048]{1,0:T(8,128)(2,1)} %tok_ref.3, s32[2,128,2048]{2,1,0:T(8,128)} %pulse_ref.1, f32[1,2048]{1,0:T(1,128)} %bitcast.49, bf16[3,2048,256]{2,1,0:T(8,128)(2,1)} %bitcast.45, bf16[128,2048]{1,0:T(8,128)(2,1)} %up_ref.1, ...), custom_call_target="tpu_custom_call" | custom-call | tf_op jit(solution)/shard_map/project/pallas_call | solution.py:95
  7.6 3.0 %collective-permute-start = (bf16[128,1024]{1,0:T(8,128)(2,1)}, bf16[128,1024]{1,0:T(8,128)(2,1)S(1)}, u32[]{:S(2)}, u32[]{:S(2)}) collective-permute-start(bf16[128,1024]{1,0:T(8,128)(2,1)} %get-tuple-element.29.refs_0_), channel_id=1, source_target_pairs={{0,4},{4,0},{8,12},{12,8},{16,20},{20,16},{24,28},{28,24},{1,5},{5... | collective-permute-start | bytes 786440 | tf_op jit(solution)/shard_map/ppermute | solution.py:319
  10.6 2.6 %collective-permute-start.3 = (bf16[128,1024]{1,0:T(8,128)(2,1)}, bf16[128,1024]{1,0:T(8,128)(2,1)}, u32[]{:S(2)}, u32[]{:S(2)}) collective-permute-start(bf16[128,1024]{1,0:T(8,128)(2,1)} %get-tuple-element.29.refs_0_), channel_id=1, source_target_pairs={{0,16},{4,20},{8,24},{12,28},{16,0},{20,4},{24,8},{28,12},{1,17},{... | collective-permute-start | bytes 786440 | tf_op jit(solution)/shard_map/ppermute | solution.py:319
  13.2 1.6 %collective-permute-start.1 = (bf16[128,1024]{1,0:T(8,128)(2,1)}, bf16[128,1024]{1,0:T(8,128)(2,1)}, u32[]{:S(2)}, u32[]{:S(2)}) collective-permute-start(bf16[128,1024]{1,0:T(8,128)(2,1)} %get-tuple-element.29.refs_0_), channel_id=1, source_target_pairs={{0,8},{4,12},{8,0},{12,4},{16,24},{20,28},{24,16},{28,20},{1,9},{5... | collective-permute-start | bytes 786440 | tf_op jit(solution)/shard_map/ppermute | solution.py:319
  14.8 1.6 %fusion.3 = bf16[32,2,2048]{2,0,1:T(8,128)(2,1)} fusion(s32[]{:T(128)S(6)} %select_n.35, bf16[128,1,2048]{2,0,1:T(8,128)(2,1)} %bitcast.48, bf16[128,1,2048]{2,0,1:T(8,128)(2,1)S(1)} %bitcast.47), kind=kLoop, calls=%fused_computation.7 | loop fusion | flops 524288 | bytes 1310724 | tf_op jit(solution)/shard_map/stack | solution.py:380
  16.4 1.0 %copy.14 = bf16[8,8,8,256]{3,2,1,0:T(8,128)(2,1)S(1)} copy(bf16[8,8,8,256]{3,1,2,0:T(8,128)(2,1)} %bitcast.54) | data formatting | bytes 524288
  17.4 1.0 %copy.12 = bf16[8,32,2,256]{3,2,1,0:T(2,128)(2,1)} copy(bf16[8,32,2,256]{3,0,1,2:T(8,128)(2,1)S(1)} %bitcast.55) | data formatting | bytes 524288 | tf_op jit(solution)/shard_map/transpose | solution.py:382
  18.4 1.8 %reshape.20 = bf16[8,32,512]{2,1,0:T(8,128)(2,1)} reshape(bf16[8,32,2,256]{3,2,1,0:T(2,128)(2,1)} %copy.12) | data formatting | bytes 524288 | tf_op jit(solution)/shard_map/reshape | solution.py:383
  20.9 3.6 %all-to-all-start = ((bf16[8,32,512]{2,1,0:T(8,128)(2,1)}), bf16[8,32,512]{2,1,0:T(8,128)(2,1)S(1)}, u32[]{:S(2)}, u32[]{:S(2)}) async-start(bf16[8,32,512]{2,1,0:T(8,128)(2,1)} %reshape.20), calls=%async_computation | async-start | bytes 524288 | tf_op jit(solution)/shard_map/all_to_all | solution.py:384
  25.3 1.1 %collective-permute-start.5 = (bf16[128,1024]{1,0:T(8,128)(2,1)}, bf16[128,1024]{1,0:T(8,128)(2,1)}, u32[]{:S(2)}, u32[]{:S(2)}) collective-permute-start(bf16[128,1024]{1,0:T(8,128)(2,1)} %collective-permute-done.3.refs_4_), channel_id=1, source_target_pairs={{0,8},{4,12},{8,0},{12,4},{16,24},{20,28},{24,16},{28,20},{1,9},{5... | collective-permute-start | bytes 786440 | tf_op jit(solution)/shard_map/ppermute | solution.py:319
  26.6 1.5 %collective-permute-start.4 = (bf16[128,1024]{1,0:T(8,128)(2,1)}, bf16[128,1024]{1,0:T(8,128)(2,1)}, u32[]{:S(2)}, u32[]{:S(2)}) collective-permute-start(bf16[128,1024]{1,0:T(8,128)(2,1)} %collective-permute-done.3.refs_4_), channel_id=1, source_target_pairs={{0,4},{4,0},{8,12},{12,8},{16,20},{20,16},{24,28},{28,24},{1,5},{5... | collective-permute-start | bytes 786440 | tf_op jit(solution)/shard_map/ppermute | solution.py:319
  28.7 7.6 %collective-permute-done.5.refs_6_ = bf16[128,1024]{1,0:T(8,128)(2,1)} collective-permute-done((bf16[128,1024]{1,0:T(8,128)(2,1)}, bf16[128,1024]{1,0:T(8,128)(2,1)}, u32[]{:S(2)}, u32[]{:S(2)}) %collective-permute-start.5) | collective-permute-done | bytes 262176 | tf_op jit(solution)/shard_map/ppermute | solution.py:319
  36.2 1.2 %collective-permute-start.6 = (bf16[128,1024]{1,0:T(8,128)(2,1)}, bf16[128,1024]{1,0:T(8,128)(2,1)}, u32[]{:S(2)}, u32[]{:S(2)}) collective-permute-start(bf16[128,1024]{1,0:T(8,128)(2,1)} %collective-permute-done.5.refs_6_), channel_id=1, source_target_pairs={{0,4},{4,0},{8,12},{12,8},{16,20},{20,16},{24,28},{28,24},{1,5},{5... | collective-permute-start | bytes 786440 | tf_op jit(solution)/shard_map/ppermute | solution.py:319
  37.4 1.5 %collective-permute-start.7 = (bf16[8,32,512]{2,1,0:T(8,128)(2,1)S(1)}, bf16[8,32,512]{2,1,0:T(8,128)(2,1)}, u32[]{:S(2)}, u32[]{:S(2)}) collective-permute-start(bf16[8,32,512]{2,1,0:T(8,128)(2,1)S(1)} %all-to-all-done.refs_0_), channel_id=1, source_target_pairs={{0,2},{1,3},{2,0},{3,1},{4,6},{5,7},{6,4},{7,5},{8,10},{9,11},{10,... | collective-permute-start | bytes 786440 | tf_op jit(solution)/shard_map/ppermute | solution.py:319
  39.0 2.4 %factors.1 = (f32[128,2048]{1,0:T(8,128)S(1)}, f32[128,512]{1,0:T(8,128)S(1)}, f32[128,512]{1,0:T(8,128)S(1)}, f32[128,512]{1,0:T(8,128)S(1)}, f32[128,512]{1,0:T(8,128)S(1)}) custom-call(s32[1]{0:T(128)} %bitcast.at_ref, bf16[128,2048]{1,0:T(8,128)(2,1)S(1)} %copy-done.3, s32[2,128,2048]{2,1,0:T(8,128)S(1)} %copy-done.1, f32[1,2048]{1,0:T(1,128)S(1)} %bitcast.50, ...), custom_call_target="tpu_custom_call" | custom-call | tf_op jit(solution)/shard_map/factors/pallas_call | solution.py:143
  41.4 1.0 %copy-done.5 = f32[128,2048]{1,0:T(8,128)} copy-done((f32[128,2048]{1,0:T(8,128)}, f32[128,2048]{1,0:T(8,128)S(1)}, u32[]{:S(2)}) %copy-start.5) | copy-done | bytes 1048600
  45.7 1.3 %collective-permute-done.6.refs_7_ = bf16[128,1024]{1,0:T(8,128)(2,1)} collective-permute-done((bf16[128,1024]{1,0:T(8,128)(2,1)}, bf16[128,1024]{1,0:T(8,128)(2,1)}, u32[]{:S(2)}, u32[]{:S(2)}) %collective-permute-start.6) | collective-permute-done | bytes 262176 | tf_op jit(solution)/shard_map/ppermute | solution.py:319
  47.0 0.9 %copy-done.17 = bf16[128,1024]{1,0:T(8,128)(2,1)S(1)} copy-done((bf16[128,1024]{1,0:T(8,128)(2,1)S(1)}, bf16[128,1024]{1,0:T(8,128)(2,1)}, u32[]{:S(2)}) %copy-start.17) | copy-done | bytes 262168
  48.0 11.6 %attention.1.refs_4_ = bf16[4,1024,256]{2,1,0:T(8,128)(2,1)S(1)} custom-call(bf16[128,1024]{1,0:T(8,128)(2,1)} %get-tuple-element.29.refs_0_, bf16[128,1024]{1,0:T(8,128)(2,1)S(1)} %copy-done.17, bf16[128,1024]{1,0:T(8,128)(2,1)} %collective-permute-done.1.refs_2_, bf16[128,1024]{1,0:T(8,128)(2,1)} %collective-permute-done.2.refs_3_, ...), custom_call_target="tpu_custom_call" | custom-call | tf_op jit(solution)/shard_map/attention/pallas_call | solution.py:209
  59.6 1.5 %spread.1 = (f32[136,512]{1,0:T(8,128)S(1)}, f32[136,512]{1,0:T(8,128)S(1)}, f32[2,136,512]{2,1,0:T(8,128)S(1)}, f32[128,512]{1,0:T(8,128)S(1)}, f32[128,512]{1,...) custom-call(s32[1]{0:T(128)} %bitcast.at_ref, bf16[4,128,256]{2,1,0:T(8,128)(2,1)S(1)} %slice.52.grad_ref, ...), custom_call_target="tpu_custom_call" | custom-call | tf_op jit(solution)/shard_map/spread/pallas_call | solution.py:299
  61.2 1.0 %collective-permute-start.14 = (f32[4,512]{1,0:T(4,128)S(1)}, f32[4,512]{1,0:T(4,128)S(1)}, u32[]{:S(2)}, u32[]{:S(2)}) collective-permute-start(f32[4,512]{1,0:T(4,128)S(1)} %get-tuple-element.47), channel_id=1, source_target_pairs={{0,4},{4,0},{8,12},{12,8},{16,20},{20,16},{24,28},{28,24},{1,5},{5... | collective-permute-start | bytes 24584 | tf_op jit(solution)/shard_map/ppermute | solution.py:319
  62.1 2.8 %collective-permute-done.14 = f32[4,512]{1,0:T(4,128)S(1)} collective-permute-done((f32[4,512]{1,0:T(4,128)S(1)}, f32[4,512]{1,0:T(4,128)S(1)}, u32[]{:S(2)}, u32[]{:S(2)}) %collective-permute-start.14) | collective-permute-done | bytes 8224 | tf_op jit(solution)/shard_map/ppermute | solution.py:319
  65.0 1.4 %collective-permute-start.15 = (f32[4,512]{1,0:T(4,128)S(1)}, f32[4,512]{1,0:T(4,128)S(1)}, u32[]{:S(2)}, u32[]{:S(2)}) collective-permute-start(f32[4,512]{1,0:T(4,128)S(1)} %add.92), channel_id=1, source_target_pairs={{0,8},{4,12},{8,0},{12,4},{16,24},{20,28},{24,16},{28,20},{1,9},{5... | collective-permute-start | bytes 24584 | tf_op jit(solution)/shard_map/ppermute | solution.py:319
  66.3 2.4 %collective-permute-done.15 = f32[4,512]{1,0:T(4,128)S(1)} collective-permute-done((f32[4,512]{1,0:T(4,128)S(1)}, f32[4,512]{1,0:T(4,128)S(1)}, u32[]{:S(2)}, u32[]{:S(2)}) %collective-permute-start.15) | collective-permute-done | bytes 8224 | tf_op jit(solution)/shard_map/ppermute | solution.py:319
  68.7 2.8 %collective-permute-start.16 = (f32[4,512]{1,0:T(4,128)S(1)}, f32[4,512]{1,0:T(4,128)S(1)}, u32[]{:S(2)}, u32[]{:S(2)}) collective-permute-start(f32[4,512]{1,0:T(4,128)S(1)} %add.93), channel_id=1, source_target_pairs={{0,16},{4,20},{8,24},{12,28},{16,0},{20,4},{24,8},{28,12},{1,17},{... | collective-permute-start | bytes 24584 | tf_op jit(solution)/shard_map/ppermute | solution.py:319
  71.4 1.8 %collective-permute-done.16 = f32[4,512]{1,0:T(4,128)S(1)} collective-permute-done((f32[4,512]{1,0:T(4,128)S(1)}, f32[4,512]{1,0:T(4,128)S(1)}, u32[]{:S(2)}, u32[]{:S(2)}) %collective-permute-start.16) | collective-permute-done | bytes 8224 | tf_op jit(solution)/shard_map/ppermute | solution.py:319
  73.9 1.5 %collective-permute-start.11 = (f32[136,512]{1,0:T(8,128)S(1)}, f32[136,512]{1,0:T(8,128)S(1)}, u32[]{:S(2)}, u32[]{:S(2)}) collective-permute-start(f32[136,512]{1,0:T(8,128)S(1)} %fusion.2), channel_id=1, source_target_pairs={{0,2},{1,3},{2,0},{3,1},{4,6},{5,7},{6,4},{7,5},{8,10},{9,11},{10,... | collective-permute-start | bytes 835592 | tf_op jit(solution)/shard_map/ppermute | solution.py:319
  76.3 2.8 %weight_grads.1 = (f32[3,256,256]{2,1,0:T(8,128)}, f32[256,256]{1,0:T(8,128)}) custom-call(s32[2]{0:T(128)S(1)} %pad_add_fusion.at_ref, bf16[8,32,512]{2,1,0:T(8,128)(2,1)S(1)} %all-to-all-done.refs_0_, bf16[8,32,512]{2,1,0:T(8,128)(2,1)S(1)} %collective-permute-done.12.refs_1_, bf16[8,32,512]{2,1,0:T(8,128)(2,1)} %collective-permute-done.7.refs_2_, ...), custom_call_target="tpu_custom_call" | custom-call | tf_op jit(solution)/shard_map/weight_grads/pallas_call | solution.py:340
  79.1 3.9 %collective-permute-done.18 = f32[512]{0:T(512)S(1)} collective-permute-done((f32[512]{0:T(512)S(1)}, f32[512]{0:T(512)S(1)}, u32[]{:S(2)}, u32[]{:S(2)}) %collective-permute-start.18) | collective-permute-done | bytes 2080 | tf_op jit(solution)/shard_map/ppermute | solution.py:319
  83.7 1.5 %collective-permute-start.10 = (f32[128,512]{1,0:T(8,128)S(1)}, f32[128,512]{1,0:T(8,128)S(1)}, u32[]{:S(2)}, u32[]{:S(2)}) collective-permute-start(f32[128,512]{1,0:T(8,128)S(1)} %fusion.6), channel_id=1, source_target_pairs={{0,2},{1,3},{2,0},{3,1},{4,6},{5,7},{6,4},{7,5},{8,10},{9,11},{10,... | collective-permute-start | bytes 786440 | tf_op jit(solution)/shard_map/ppermute | solution.py:319
  85.2 0.8 fusion.5
  86.0 5.6 %collective-permute-done.10 = f32[128,512]{1,0:T(8,128)S(1)} collective-permute-done((f32[128,512]{1,0:T(8,128)S(1)}, f32[128,512]{1,0:T(8,128)S(1)}, u32[]{:S(2)}, u32[]{:S(2)}) %collective-permute-start.10) | collective-permute-done | bytes 262176 | tf_op jit(solution)/shard_map/ppermute | solution.py:319
  (82 shorter events, 9.5 us)
Async XLA Ops:
  0.6 14.1 %copy-start.2 = (bf16[128,2048]{1,0:T(8,128)(2,1)S(1)}, bf16[128,2048]{1,0:T(8,128)(2,1)}, u32[]{:S(2)}) copy-start(bf16[128,2048]{1,0:T(8,128)(2,1)} %up_ref.1) | copy-start | bytes 1572868
  7.5 17.0 %copy-start.19 = (s32[1024]{0:T(1024)S(1)}, s32[1024]{0:T(1024)}, u32[]{:S(2)}) copy-start(s32[1024]{0:T(1024)} %param.8) | copy-start | bytes 12292
  7.5 31.4 %copy-start.1 = (s32[2,128,2048]{2,1,0:T(8,128)S(1)}, s32[2,128,2048]{2,1,0:T(8,128)}, u32[]{:S(2)}) copy-start(s32[2,128,2048]{2,1,0:T(8,128)} %pulse_ref.1) | copy-start | bytes 6291460
  7.5 31.4 %copy-start.3 = (bf16[128,2048]{1,0:T(8,128)(2,1)S(1)}, bf16[128,2048]{1,0:T(8,128)(2,1)}, u32[]{:S(2)}) copy-start(bf16[128,2048]{1,0:T(8,128)(2,1)} %tok_ref.3) | copy-start | bytes 1572868
  7.5 31.4 %copy-start.18 = (f32[2048]{0:T(1024)S(1)}, f32[2048]{0:T(1024)}, u32[]{:S(2)}) copy-start(f32[2048]{0:T(1024)} %param.10) | copy-start | bytes 24580
  7.6 12.6 %collective-permute-start = (bf16[128,1024]{1,0:T(8,128)(2,1)}, bf16[128,1024]{1,0:T(8,128)(2,1)S(1)}, u32[]{:S(2)}, u32[]{:S(2)}) collective-permute-start(bf16[128,1024]{1,0:T(8,128)(2,1)} %get-tuple-element.29.refs_0_), channel_id=1, source_target_pairs={{0,4},{4,0},{8,12},{12,8},{16,20},{20,16},{24,28},{28,24},{1,5},{5... | collective-permute-start | bytes 786440 | tf_op jit(solution)/shard_map/ppermute | solution.py:319
  10.6 14.7 %collective-permute-start.3 = (bf16[128,1024]{1,0:T(8,128)(2,1)}, bf16[128,1024]{1,0:T(8,128)(2,1)}, u32[]{:S(2)}, u32[]{:S(2)}) collective-permute-start(bf16[128,1024]{1,0:T(8,128)(2,1)} %get-tuple-element.29.refs_0_), channel_id=1, source_target_pairs={{0,16},{4,20},{8,24},{12,28},{16,0},{20,4},{24,8},{28,12},{1,17},{... | collective-permute-start | bytes 786440 | tf_op jit(solution)/shard_map/ppermute | solution.py:319
  13.2 14.9 %collective-permute-start.1 = (bf16[128,1024]{1,0:T(8,128)(2,1)}, bf16[128,1024]{1,0:T(8,128)(2,1)}, u32[]{:S(2)}, u32[]{:S(2)}) collective-permute-start(bf16[128,1024]{1,0:T(8,128)(2,1)} %get-tuple-element.29.refs_0_), channel_id=1, source_target_pairs={{0,8},{4,12},{8,0},{12,4},{16,24},{20,28},{24,16},{28,20},{1,9},{5... | collective-permute-start | bytes 786440 | tf_op jit(solution)/shard_map/ppermute | solution.py:319
  20.9 16.5 %all-to-all-start = ((bf16[8,32,512]{2,1,0:T(8,128)(2,1)}), bf16[8,32,512]{2,1,0:T(8,128)(2,1)S(1)}, u32[]{:S(2)}, u32[]{:S(2)}) async-start(bf16[8,32,512]{2,1,0:T(8,128)(2,1)} %reshape.20), calls=%async_computation | async-start | bytes 524288 | tf_op jit(solution)/shard_map/all_to_all | solution.py:384
  25.3 10.9 %collective-permute-start.5 = (bf16[128,1024]{1,0:T(8,128)(2,1)}, bf16[128,1024]{1,0:T(8,128)(2,1)}, u32[]{:S(2)}, u32[]{:S(2)}) collective-permute-start(bf16[128,1024]{1,0:T(8,128)(2,1)} %collective-permute-done.3.refs_4_), channel_id=1, source_target_pairs={{0,8},{4,12},{8,0},{12,4},{16,24},{20,28},{24,16},{28,20},{1,9},{5... | collective-permute-start | bytes 786440 | tf_op jit(solution)/shard_map/ppermute | solution.py:319
  26.6 19.0 %collective-permute-start.4 = (bf16[128,1024]{1,0:T(8,128)(2,1)}, bf16[128,1024]{1,0:T(8,128)(2,1)}, u32[]{:S(2)}, u32[]{:S(2)}) collective-permute-start(bf16[128,1024]{1,0:T(8,128)(2,1)} %collective-permute-done.3.refs_4_), channel_id=1, source_target_pairs={{0,4},{4,0},{8,12},{12,8},{16,20},{20,16},{24,28},{28,24},{1,5},{5... | collective-permute-start | bytes 786440 | tf_op jit(solution)/shard_map/ppermute | solution.py:319
  28.1 17.6 %collective-permute-start.2 = (bf16[128,1024]{1,0:T(8,128)(2,1)}, bf16[128,1024]{1,0:T(8,128)(2,1)}, u32[]{:S(2)}, u32[]{:S(2)}) collective-permute-start(bf16[128,1024]{1,0:T(8,128)(2,1)} %collective-permute-done.1.refs_2_), channel_id=1, source_target_pairs={{0,4},{4,0},{8,12},{12,8},{16,20},{20,16},{24,28},{28,24},{1,5},{5... | collective-permute-start | bytes 786440 | tf_op jit(solution)/shard_map/ppermute | solution.py:319
  36.2 10.8 %collective-permute-start.6 = (bf16[128,1024]{1,0:T(8,128)(2,1)}, bf16[128,1024]{1,0:T(8,128)(2,1)}, u32[]{:S(2)}, u32[]{:S(2)}) collective-permute-start(bf16[128,1024]{1,0:T(8,128)(2,1)} %collective-permute-done.5.refs_6_), channel_id=1, source_target_pairs={{0,4},{4,0},{8,12},{12,8},{16,20},{20,16},{24,28},{28,24},{1,5},{5... | collective-permute-start | bytes 786440 | tf_op jit(solution)/shard_map/ppermute | solution.py:319
  37.4 8.0 %collective-permute-start.7 = (bf16[8,32,512]{2,1,0:T(8,128)(2,1)S(1)}, bf16[8,32,512]{2,1,0:T(8,128)(2,1)}, u32[]{:S(2)}, u32[]{:S(2)}) collective-permute-start(bf16[8,32,512]{2,1,0:T(8,128)(2,1)S(1)} %all-to-all-done.refs_0_), channel_id=1, source_target_pairs={{0,2},{1,3},{2,0},{3,1},{4,6},{5,7},{6,4},{7,5},{8,10},{9,11},{10,... | collective-permute-start | bytes 786440 | tf_op jit(solution)/shard_map/ppermute | solution.py:319
  47.9 11.6 %copy-start = (bf16[2048,3,256]{2,0,1:T(8,128)(2,1)S(1)}, bf16[2048,3,256]{2,0,1:T(8,128)(2,1)}, u32[]{:S(2)}) copy-start(bf16[2048,3,256]{2,0,1:T(8,128)(2,1)} %param.11) | copy-start | bytes 9437188
  47.9 11.6 %copy-start.4 = (bf16[256,2048]{1,0:T(8,128)(2,1)S(1)}, bf16[256,2048]{1,0:T(8,128)(2,1)}, u32[]{:S(2)}) copy-start(bf16[256,2048]{1,0:T(8,128)(2,1)} %wout_ref.1) | copy-start | bytes 3145732
  48.0 11.6 %copy-start.6 = (f32[128,2048]{1,0:T(8,128)S(1)}, f32[128,2048]{1,0:T(8,128)}, u32[]{:S(2)}) copy-start(f32[128,2048]{1,0:T(8,128)} %copy-done.5) | copy-start | bytes 3145732
  61.1 3.8 %collective-permute-start.8 = (f32[2,136,512]{2,1,0:T(8,128)S(1)}, f32[2,136,512]{2,1,0:T(8,128)S(1)}, u32[]{:S(2)}, u32[]{:S(2)}) collective-permute-start(f32[2,136,512]{2,1,0:T(8,128)S(1)} %get-tuple-element.37), channel_id=1, source_target_pairs={{0,1},{1,0},{2,3},{3,2},{4,5},{5,4},{6,7},{7,6},{8,9},{9,8},{10,11... | collective-permute-start | bytes 1671176 | tf_op jit(solution)/shard_map/ppermute | solution.py:319
  61.2 3.7 %collective-permute-start.14 = (f32[4,512]{1,0:T(4,128)S(1)}, f32[4,512]{1,0:T(4,128)S(1)}, u32[]{:S(2)}, u32[]{:S(2)}) collective-permute-start(f32[4,512]{1,0:T(4,128)S(1)} %get-tuple-element.47), channel_id=1, source_target_pairs={{0,4},{4,0},{8,12},{12,8},{16,20},{20,16},{24,28},{28,24},{1,5},{5... | collective-permute-start | bytes 24584 | tf_op jit(solution)/shard_map/ppermute | solution.py:319
  65.0 3.7 %collective-permute-start.15 = (f32[4,512]{1,0:T(4,128)S(1)}, f32[4,512]{1,0:T(4,128)S(1)}, u32[]{:S(2)}, u32[]{:S(2)}) collective-permute-start(f32[4,512]{1,0:T(4,128)S(1)} %add.92), channel_id=1, source_target_pairs={{0,8},{4,12},{8,0},{12,4},{16,24},{20,28},{24,16},{28,20},{1,9},{5... | collective-permute-start | bytes 24584 | tf_op jit(solution)/shard_map/ppermute | solution.py:319
  68.7 4.5 %collective-permute-start.16 = (f32[4,512]{1,0:T(4,128)S(1)}, f32[4,512]{1,0:T(4,128)S(1)}, u32[]{:S(2)}, u32[]{:S(2)}) collective-permute-start(f32[4,512]{1,0:T(4,128)S(1)} %add.93), channel_id=1, source_target_pairs={{0,16},{4,20},{8,24},{12,28},{16,0},{20,4},{24,8},{28,12},{1,17},{... | collective-permute-start | bytes 24584 | tf_op jit(solution)/shard_map/ppermute | solution.py:319
  73.3 2.3 %collective-permute-start.17 = (f32[2,512]{1,0:T(2,128)S(1)}, f32[2,512]{1,0:T(2,128)S(1)}, u32[]{:S(2)}, u32[]{:S(2)}) collective-permute-start(f32[2,512]{1,0:T(2,128)S(1)} %pad_maximum_fusion), channel_id=1, source_target_pairs={{0,1},{1,0},{2,3},{3,2},{4,5},{5,4},{6,7},{7,6},{8,9},{9,8},{10,11... | collective-permute-start | bytes 12296 | tf_op jit(solution)/shard_map/ppermute | solution.py:319
  73.3 2.9 %collective-permute-start.12 = (bf16[8,32,512]{2,1,0:T(8,128)(2,1)S(1)}, bf16[8,32,512]{2,1,0:T(8,128)(2,1)S(1)}, u32[]{:S(2)}, u32[]{:S(2)}) collective-permute-start(bf16[8,32,512]{2,1,0:T(8,128)(2,1)S(1)} %all-to-all-done.refs_0_), channel_id=1, source_target_pairs={{0,1},{1,0},{2,3},{3,2},{4,5},{5,4},{6,7},{7,6},{8,9},{9,8},{10,11... | collective-permute-start | bytes 786440 | tf_op jit(solution)/shard_map/ppermute | solution.py:319
  73.8 2.4 %collective-permute-start.13 = (bf16[8,32,512]{2,1,0:T(8,128)(2,1)}, bf16[8,32,512]{2,1,0:T(8,128)(2,1)S(1)}, u32[]{:S(2)}, u32[]{:S(2)}) collective-permute-start(bf16[8,32,512]{2,1,0:T(8,128)(2,1)} %collective-permute-done.7.refs_2_), channel_id=1, source_target_pairs={{0,1},{1,0},{2,3},{3,2},{4,5},{5,4},{6,7},{7,6},{8,9},{9,8},{10,11... | collective-permute-start | bytes 786440 | tf_op jit(solution)/shard_map/ppermute | solution.py:319
  73.9 9.6 %collective-permute-start.11 = (f32[136,512]{1,0:T(8,128)S(1)}, f32[136,512]{1,0:T(8,128)S(1)}, u32[]{:S(2)}, u32[]{:S(2)}) collective-permute-start(f32[136,512]{1,0:T(8,128)S(1)} %fusion.2), channel_id=1, source_target_pairs={{0,2},{1,3},{2,0},{3,1},{4,6},{5,7},{6,4},{7,5},{8,10},{9,11},{10,... | collective-permute-start | bytes 835592 | tf_op jit(solution)/shard_map/ppermute | solution.py:319
  75.4 8.2 %collective-permute-start.9 = (f32[2,128,512]{2,1,0:T(8,128)S(1)}, f32[2,128,512]{2,1,0:T(8,128)S(1)}, u32[]{:S(2)}, u32[]{:S(2)}) collective-permute-start(f32[2,128,512]{2,1,0:T(8,128)S(1)} %get-tuple-element.38), channel_id=1, source_target_pairs={{0,1},{1,0},{2,3},{3,2},{4,5},{5,4},{6,7},{7,6},{8,9},{9,8},{10,11... | collective-permute-start | bytes 1572872 | tf_op jit(solution)/shard_map/ppermute | solution.py:319
  75.6 7.4 %collective-permute-start.18 = (f32[512]{0:T(512)S(1)}, f32[512]{0:T(512)S(1)}, u32[]{:S(2)}, u32[]{:S(2)}) collective-permute-start(f32[512]{0:T(512)S(1)} %bitcast.57), channel_id=1, source_target_pairs={{0,2},{1,3},{2,0},{3,1},{4,6},{5,7},{6,4},{7,5},{8,10},{9,11},{10,... | collective-permute-start | bytes 6152 | tf_op jit(solution)/shard_map/ppermute | solution.py:319
  76.3 9.0 %copy-start.9 = (f32[128,512]{1,0:T(8,128)S(1)}, f32[128,512]{1,0:T(8,128)}, u32[]{:S(2)}) copy-start(f32[128,512]{1,0:T(8,128)} %copy-done.8) | copy-start | bytes 786436
  76.3 9.0 %copy-start.11 = (f32[128,512]{1,0:T(8,128)S(1)}, f32[128,512]{1,0:T(8,128)}, u32[]{:S(2)}) copy-start(f32[128,512]{1,0:T(8,128)} %copy-done.10) | copy-start | bytes 786436
  76.3 9.0 %copy-start.13 = (f32[128,512]{1,0:T(8,128)S(1)}, f32[128,512]{1,0:T(8,128)}, u32[]{:S(2)}) copy-start(f32[128,512]{1,0:T(8,128)} %copy-done.12) | copy-start | bytes 786436
  79.1 12.5 %copy-start.15 = (f32[128,512]{1,0:T(8,128)S(1)}, f32[128,512]{1,0:T(8,128)}, u32[]{:S(2)}) copy-start(f32[128,512]{1,0:T(8,128)} %copy-done.14) | copy-start | bytes 786436
  83.7 7.9 %collective-permute-start.10 = (f32[128,512]{1,0:T(8,128)S(1)}, f32[128,512]{1,0:T(8,128)S(1)}, u32[]{:S(2)}, u32[]{:S(2)}) collective-permute-start(f32[128,512]{1,0:T(8,128)S(1)} %fusion.6), channel_id=1, source_target_pairs={{0,2},{1,3},{2,0},{3,1},{4,6},{5,7},{6,4},{7,5},{8,10},{9,11},{10,... | collective-permute-start | bytes 786440 | tf_op jit(solution)/shard_map/ppermute | solution.py:319
  (8 other events, 6.3 us)

commit v3 on v2

--- a/solution.py
+++ b/solution.py
@@ -11,7 +11,7 @@
 SOFT_CAP = 30.0
 LEAK_RATE = 0.5
 THRESHOLD = 1.0
-SURROGATE_SLOPE = 4.0
+SURRO4_SLOPE = 4.0
 EPSILON = 1e-05
 SUM_ROWS = 8
 LOG2_E = 1.4426950408889634
@@ -33,19 +33,15 @@
 
 
 def project_kernel(
-    tok_hbm, pulse_hbm, gain_hbm, win_hbm, up_hbm, wout_hbm, pay_ref, spikes_ref, inv_ref,
+    at_ref, tok_hbm, pulse_hbm, gain_hbm, win_hbm, up_hbm, wout_hbm, pay_ref, spikes_ref, inv_ref, send_ref,
     tok_ref, pulse_ref, gain_ref, win_ref, up_ref, wout_ref, acc_ref, sems, block_sems,
 ):
     model = tok_ref.shape[1]
     local = wout_ref.shape[0]
     blocks = block_sems.shape[0]
     width = model // blocks
-    whole = [
-        pltpu.make_async_copy(source, target, sems.at[k])
-        for k, (source, target) in enumerate(
-            [(tok_hbm, tok_ref), (gain_hbm, gain_ref), (up_hbm, up_ref), (wout_hbm, wout_ref)]
-        )
-    ]
+    ends = [(tok_hbm, tok_ref), (gain_hbm, gain_ref), (up_hbm, up_ref), (wout_hbm, wout_ref)]
+    whole = [pltpu.make_async_copy(*pair, sems.at[k]) for k, pair in enumerate(ends)]
     pairs = []
     for k in range(blocks):
         here = pl.ds(k * width, width)
@@ -53,22 +49,17 @@
         weight = (win_hbm.at[:, here, :], win_ref.at[:, here, :])
         pairs.append(
             [
-                pltpu.make_async_copy(*ends, block_sems.at[k, n])
-                for n, ends in enumerate((pulse, weight))
+                pltpu.make_async_copy(*pair, block_sems.at[k, n])
+                for n, pair in enumerate((pulse, weight))
             ]
         )
-    for copy in whole:
+    for copy in [*whole[:2], *(copy for pair in pairs for copy in pair), *whole[2:]]:
         copy.start()
-    for pair in pairs:
-        for copy in pair:
-            copy.start()
     whole[0].wait()
     values = tok_ref[...].astype(F32)
     inv = lax.rsqrt(jnp.mean(values * values, axis=-1, keepdims=True) + EPSILON)
     inv_ref[...] = inv
-    for copy in whole[1:]:
-        copy.wait()
-    pay_ref[:, 3 * local :] = dot(up_ref[...], wout_ref[...], NT).astype(BF16)
+    whole[1].wait()
     for k, pair in enumerate(pairs):
         here = slice(k * width, (k + 1) * width)
         pair[0].wait()
@@ -84,9 +75,19 @@
             share = dot(spikes, win_ref[part, here, :], NN)
             acc_ref[:, columns] = share if k == 0 else acc_ref[:, columns] + share
     pay_ref[:, : 3 * local] = acc_ref[...].astype(BF16)
-
-
-def project(tokens, pulse, gain, win, upstream, wout):
+    for copy in whole[2:]:
+        copy.wait()
+    pay_ref[:, 3 * local :] = dot(up_ref[...], wout_ref[...], NT).astype(BF16)
+    ranks, quarter, both = send_ref.shape
+    features = both // 2
+    mine = pl.ds(pl.multiple_of(at_ref[0] * quarter, quarter), quarter)
+    for rank in range(ranks):
+        here = slice(rank * features, (rank + 1) * features)
+        send_ref[rank, :, :features] = spikes_ref[mine, here]
+        send_ref[rank, :, features:] = up_ref[mine, here]
+
+
+def project(fsdp_rank, ctx, tokens, pulse, gain, win, upstream, wout):
     rows, model = tokens.shape
     local = wout.shape[0]
     blocks = 4
@@ -94,12 +95,14 @@
     in_vmem = pl.BlockSpec(memory_space=pltpu.VMEM)
     return pl.pallas_call(
         project_kernel,
-        in_specs=[pl.BlockSpec(memory_space=pltpu.HBM)] * 6,
-        out_specs=[in_vmem] * 3,
+        in_specs=[pl.BlockSpec(memory_space=pltpu.SMEM)]
+        + [pl.BlockSpec(memory_space=pltpu.HBM)] * 6,
+        out_specs=[in_vmem] * 4,
         out_shape=[
             jax.ShapeDtypeStruct((rows, 4 * local), BF16),
             jax.ShapeDtypeStruct((rows, model), BF16),
             jax.ShapeDtypeStruct((rows, 1), F32),
+            jax.ShapeDtypeStruct((ctx, rows // 4, 2 * (model // ctx)), BF16),
         ],
         scratch_shapes=[pltpu.VMEM(array.shape, array.dtype) for array in arrays]
         + [
@@ -109,7 +112,10 @@
         ],
         compiler_params=params(24),
         name="project",
-    )(*(pltpu.with_memory_space_constraint(array, pltpu.HBM) for array in arrays))
+    )(
+        fsdp_rank[None],
+        *(pltpu.with_memory_space_constraint(array, pltpu.HBM) for array in arrays),
+    )
 
 
 def factor_kernel(
@@ -124,8 +130,8 @@
     later = LEAK_RATE * current * (1.0 - first) + current
 
     def slope(fired, membrane):
-        level = jax.nn.sigmoid(SURROGATE_SLOPE * (membrane - THRESHOLD))
-        return fired + membrane * SURROGATE_SLOPE * level * (1.0 - level)
+        level = jax.nn.sigmoid(SURRO4_SLOPE * (membrane - THRESHOLD))
+        return fired + membrane * SURRO4_SLOPE * level * (1.0 - level)
 
     carried = 1.0 + LEAK_RATE * (1.0 - first)
     factor_ref[...] = 0.5 * (slope(first, current) + slope(second, later) * carried)
@@ -269,47 +275,43 @@
 
 def spread_kernel(
     at_ref, grad_ref, win_ref, wout_ref, tok_ref, gain_ref, inv_ref, factor_ref,
-    own_ref, far_ref, near_ref, own_out_ref, far_out_ref, near_out_ref, gain_out_ref,
+    own_ref, far_ref, near_ref,
 ):
     rows = tok_ref.shape[0]
     width = own_ref.shape[1]
+    below = rows + SUM_ROWS
     sums = jnp.zeros((rows, 1), F32)
     targets = (own_ref, near_ref.at[1], far_ref, near_ref.at[0])
-    out_targets = (own_out_ref, near_out_ref.at[1], far_out_ref, near_out_ref.at[0])
     for k in range(4):
         here = pl.ds(pl.multiple_of((at_ref[0] ^ k) * width, width), width)
         share = sum(dot(grad_ref[part], win_ref[part, here, :], NT) for part in range(3))
         targets[k][:rows, :] = share
-        out_targets[k][...] = dot(grad_ref[3], wout_ref[:, here], NN)
+        targets[k][below:, :] = dot(grad_ref[3], wout_ref[:, here], NN)
         weighted = share * factor_ref[:, here] * (tok_ref[:, here].astype(F32) * inv_ref[...])
-        gain_out_ref[k : k + 1, :] = jnp.sum(weighted, axis=0, keepdims=True)
+        targets[k][rows:below, :] = jnp.broadcast_to(
+            jnp.sum(weighted, axis=0, keepdims=True), (SUM_ROWS, width)
+        )
         sums += jnp.sum(weighted * gain_ref[:, here], axis=1, keepdims=True)
-    line = jnp.broadcast_to(sums, (rows, rows)).T[:SUM_ROWS, :]
+    line = jnp.broadcast_to(sums, (rows, rows)).T[:1, :]
     for target in targets:
-        target[rows:, :] = jnp.broadcast_to(line[:, :1], (SUM_ROWS, width))
-        target[rows:, :rows] = line
+        target[rows : rows + 1, :rows] = line
 
 
 def spread(fsdp_rank, own_grads, win, wout, tokens, gain, inv, factor):
     rows, model = tokens.shape
     width = model // 4
     in_vmem = pl.BlockSpec(memory_space=pltpu.VMEM)
-    tall = jax.ShapeDtypeStruct((rows + SUM_ROWS, width), F32)
-    flat = jax.ShapeDtypeStruct((rows, width), F32)
+    tall = (2 * rows + SUM_ROWS, width)
     return pl.pallas_call(
         spread_kernel,
         in_specs=[pl.BlockSpec(memory_space=pltpu.SMEM)] + [in_vmem] * 7,
-        out_specs=[in_vmem] * 7,
+        out_specs=[in_vmem] * 3,
         out_shape=[
-            tall,
-            tall,
-            jax.ShapeDtypeStruct((2,) + tall.shape, F32),
-            flat,
-            flat,
-            jax.ShapeDtypeStruct((2,) + flat.shape, F32),
-            jax.ShapeDtypeStruct((4, width), F32),
+            jax.ShapeDtypeStruct(tall, F32),
+            jax.ShapeDtypeStruct(tall, F32),
+            jax.ShapeDtypeStruct((2,) + tall, F32),
         ],
-        compiler_params=params(24),
+        compiler_params=params(20),
         name="spread",
     )(fsdp_rank[None], own_grads, win, wout, tokens, gain, inv, factor)
 
@@ -346,7 +348,7 @@
             jax.ShapeDtypeStruct((features, local), F32),
         ],
         scratch_shapes=[pltpu.VMEM((grads.shape[1], 2 * features), BF16)],
-        compiler_params=params(),
+        compiler_params=params(16),
         name="weight_grads",
     )(jnp.stack([fsdp_rank, turn]), *pieces, grads)
 
@@ -360,7 +362,9 @@
     gain = norm_gain[None, :]
     features = model // ctx
     win = jnp.transpose(in_weight, (1, 0, 2))
-    payload, spikes, inv = project(tokens, pulse_indicator, gain, win, upstream, out_weight)
+    payload, spikes, inv, both = project(
+        fsdp_rank, ctx, tokens, pulse_indicator, gain, win, upstream, out_weight
+    )
     factor, rise, fall, base, token_share = factors(
         fsdp_rank, tokens, pulse_indicator, gain, inv, upstream, share
     )
@@ -370,18 +374,15 @@
         beside = swap(payload, "ctx", 2)
         below = swap(payload, "ctx", 1)
         across = swap(payload, "ctx", 4)
-        blocks = [payload, below, beside, swap(beside, "ctx", 1), across, swap(across, "ctx", 1)]
+        diagonal = swap(beside, "ctx", 1)
         corner = swap(across, "ctx", 2)
+        across_below = swap(across, "ctx", 1)
+        blocks = [payload, below, beside, diagonal, across, across_below]
         blocks += [corner, swap(corner, "ctx", 1)]
         placed = jnp.concatenate(
             [lax.dynamic_slice_in_dim(positions, (ctx_rank ^ j) * rows, rows) for j in range(ctx)]
         )
-        quarter = rows // fsdp
-        both = jnp.stack([spikes, upstream], axis=1)
-        both = lax.dynamic_slice_in_dim(both, fsdp_rank * quarter, quarter, 0)
-        both = both.reshape(quarter, 2, ctx, features).transpose(2, 0, 1, 3)
-        both = after(both.reshape(ctx, quarter, 2 * features), below)
-        both = lax.all_to_all(both, "ctx", 0, 0)
+        both = lax.all_to_all(after(both, below), "ctx", 0, 0)
         over = swap(both, "fsdp", 2)
         pieces = [both, swap(both, "fsdp", 1), over, swap(over, "fsdp", 1)]
         grads = attention(blocks, after(placed, over))
@@ -397,28 +398,27 @@
         in_grad = jnp.stack([dot(fired, grads[part], TN) for part in range(3)])
         out_grad = dot(wanted, grads[3], TN)
 
-    own, far, near, own_out, far_out, near_out, gains = spread(
-        fsdp_rank, own_grads, win, out_weight, tokens, gain, inv, factor
-    )
+    own, far, near = spread(fsdp_rank, own_grads, win, out_weight, tokens, gain, inv, factor)
     near = swap(near, "fsdp", 1)
     far = far + near[0]
-    landed = swap(far, "fsdp", 2)
-    near_out = swap(after(near_out, far), "fsdp", 1)
-    landed_out = swap(far_out + near_out[0], "fsdp", 2)
+    own = own + near[1]
+    lines = slice(rows, rows + SUM_ROWS)
+    line = own[lines] + swap(far[lines], "fsdp", 2)
+    landed = swap(jnp.concatenate([far[:rows], far[rows + SUM_ROWS :]]).astype(BF16), "fsdp", 2)
+    gain_grad = line[1]
     if short:
-        gains = gains + swap(gains, "ctx", 1)
-        gains = after(gains, far)
-        for mask in (2, 4):
-            gains = gains + swap(gains, "ctx", mask)
+        for mask in (1, 2, 4):
+            gain_grad = gain_grad + swap(gain_grad, "ctx", mask)
+            if mask == 2:
+                landed = after(landed, gain_grad)
         landed = after(landed, in_grad, out_grad)
     else:
-        gains = lax.psum(gains, "ctx")
-    gain_near = swap(jnp.stack([gains[3], gains[1]]), "fsdp", 1)
-    gain_grad = gains[0] + gain_near[1] + swap(gains[2] + gain_near[0], "fsdp", 2)
-
-    grad_spikes = own + near[1] + landed
-    token_grad = base + (rise * grad_spikes[:rows] - fall * grad_spikes[rows, :rows][:, None])
-    block_out = (token_share + (own_out + near_out[1] + landed_out)).astype(BF16)
+        gain_grad = lax.psum(gain_grad, "ctx")
+
+    grad_spikes = own[:rows] + landed[:rows].astype(F32)
+    token_grad = base + (rise * grad_spikes - fall * line[0, :rows][:, None])
+    projected = own[rows + SUM_ROWS :] + landed[rows:].astype(F32)
+    block_out = (token_share + projected).astype(BF16)
     return (block_out, token_grad, gain_grad, jnp.transpose(in_grad, (1, 0, 2)), out_grad)
 
 

time: 92.7 us -> 80.2 us (0.87)
  waiting for transfers between devices: 25.9 us -> 21.5 us
  local copies, waits for them, and re-layouts: 11 us -> 7.11 us
  other arithmetic: 4 us -> 1.79 us
  Pallas kernels: 24.4 us -> 23.1 us
    ppermute x19 -> x16, waiting for transfers between devices: 25.9 us -> 21.5 us  [swap(): return lax.ppermute(value, axis, [(i, i ^ mask) for i in range(count)])]
    ppermute x19 -> x16, starting transfers between devices: 22.5 us -> 19.6 us  [swap(): return lax.ppermute(value, axis, [(i, i ^ mask) for i in range(count)])]
    all_to_all x1, starting transfers between devices: 3.59 us -> 6.05 us  [body(): both = lax.all_to_all(after(both, below), 'ctx', 0, 0)]
    reshape x1 -> x0, local copies, waits for them, and re-layouts: 1.82 us -> none  [body(): both = after(both.reshape(ctx, quarter, 2 * features), below)]
    another operation x2 -> x1, other arithmetic: 1.64 us -> 0.25 us  [the longest x1 1.63 us: body(): both = jnp.stack([spikes, upstream], axis=1)]
    pallas_call x1, Pallas kernels: 6.1 us -> 4.96 us  [project(): pl.pallas_call(project_kernel, in_specs=[pl.BlockSpec(memory_space=pltpu....]
    unnamed x48 -> x47, local copies, waits for them, and re-layouts: 7.89 us -> 6.76 us
    transpose x1 -> x0, local copies, waits for them, and re-layouts: 0.97 us -> none  [body(): both = both.reshape(quarter, 2, ctx, features).transpose(2, 0, 1, 3)]
  transfers between devices with their start and end apart: 20 -> 17, of which waited for: 8 -> 9; matrix products, arithmetic and copies ran while one was open for 8% -> 2% of each run, Pallas kernels for 6% -> 6%
where the time goes in v3:
time: 80.2 us; the launch traced here: 80 us
  starting transfers between devices  25.6 us (32%)
  Pallas kernels  23.1 us (29%)
  waiting for transfers between devices  21.5 us (27%)
  local copies, waits for them, and re-layouts  7.11 us (9%)
  other arithmetic  1.79 us (2%)
  between operations  0.88 us (1%)
    ppermute x16, waiting for transfers between devices, swap(): return lax.ppermute(value, axis, [(i, i ^ mask) for i in range(count)])  21.5 us
    ppermute x16, starting transfers between devices, swap(): return lax.ppermute(value, axis, [(i, i ^ mask) for i in range(count)])  19.6 us
    pallas_call x1, Pallas kernels, attention(): pl.pallas_call(attention_kernel, in_specs=[in_vmem] * (len(pieces) + 2),...  11.5 us
    unnamed x47, local copies, waits for them, and re-layouts  6.76 us
    all_to_all x1, starting transfers between devices, body(): both = lax.all_to_all(after(both, below), 'ctx', 0, 0)  6.05 us
    pallas_call x1, Pallas kernels, project(): pl.pallas_call(project_kernel, in_specs=[pl.BlockSpec(memory_space=pltpu....  4.96 us
    pallas_call x1, Pallas kernels, weight_grads(): pl.pallas_call(weight_kernel, in_specs=[pl.BlockSpec(memory_space=pltpu.S...  2.74 us
    pallas_call x1, Pallas kernels, factors(): pl.pallas_call(factor_kernel, in_specs=[pl.BlockSpec(memory_space=pltpu.S...  2.39 us
  transfers between devices with their start and end apart: 17, of which 9 were waited for; matrix products, arithmetic and copies ran while one was open for 2% of the time, Pallas kernels for 6%

profile of v3, /device:TPU:0, one launch (start us, length us, event | category | flops | bytes accessed | tf_op | source)
XLA Modules:
  0.0 80.0 jit_solution(12389270767224285684)
XLA Ops:
  0.7 5.0 %project.1 = (bf16[128,1024]{1,0:T(8,128)(2,1)}, bf16[128,2048]{1,0:T(8,128)(2,1)}, f32[128,1]{1,0:T(8,128)S(1)}, bf16[8,32,512]{2,1,0:T(8,128)(2,1)S(1)}) custom-call(s32[1]{0:T(128)} %bitcast.at_ref, bf16[128,2048]{1,0:T(8,128)(2,1)} %tok_ref.3, s32[2,128,2048]{2,1,0:T(8,128)} %pulse_ref.1, f32[1,2048]{1,0:T(1,128)} %bitcast.21, ...), custom_call_target="tpu_custom_call" | custom-call | tf_op jit(solution)/shard_map/project/pallas_call | solution.py:96
  5.7 0.7 copy-done.15
  6.4 3.0 %collective-permute-start = (bf16[128,1024]{1,0:T(8,128)(2,1)}, bf16[128,1024]{1,0:T(8,128)(2,1)S(1)}, u32[]{:S(2)}, u32[]{:S(2)}) collective-permute-start(bf16[128,1024]{1,0:T(8,128)(2,1)} %get-tuple-element.24.refs_0_), channel_id=1, source_target_pairs={{0,4},{4,0},{8,12},{12,8},{16,20},{20,16},{24,28},{28,24},{1,5},{5... | collective-permute-start | bytes 786440 | tf_op jit(solution)/shard_map/ppermute | solution.py:321
  9.3 2.6 %collective-permute-start.3 = (bf16[128,1024]{1,0:T(8,128)(2,1)}, bf16[128,1024]{1,0:T(8,128)(2,1)}, u32[]{:S(2)}, u32[]{:S(2)}) collective-permute-start(bf16[128,1024]{1,0:T(8,128)(2,1)} %get-tuple-element.24.refs_0_), channel_id=1, source_target_pairs={{0,16},{4,20},{8,24},{12,28},{16,0},{20,4},{24,8},{28,12},{1,17},{... | collective-permute-start | bytes 786440 | tf_op jit(solution)/shard_map/ppermute | solution.py:321
  11.9 1.6 %collective-permute-start.1 = (bf16[128,1024]{1,0:T(8,128)(2,1)}, bf16[128,1024]{1,0:T(8,128)(2,1)}, u32[]{:S(2)}, u32[]{:S(2)}) collective-permute-start(bf16[128,1024]{1,0:T(8,128)(2,1)} %get-tuple-element.24.refs_0_), channel_id=1, source_target_pairs={{0,8},{4,12},{8,0},{12,4},{16,24},{20,28},{24,16},{28,20},{1,9},{5... | collective-permute-start | bytes 786440 | tf_op jit(solution)/shard_map/ppermute | solution.py:321
  13.5 2.4 %collective-permute-done.refs_1_ = bf16[128,1024]{1,0:T(8,128)(2,1)S(1)} collective-permute-done((bf16[128,1024]{1,0:T(8,128)(2,1)}, bf16[128,1024]{1,0:T(8,128)(2,1)S(1)}, u32[]{:S(2)}, u32[]{:S(2)}) %collective-permute-start) | collective-permute-done | bytes 262176 | tf_op jit(solution)/shard_map/ppermute | solution.py:321
  15.8 0.7 copy-done.16
  16.5 6.1 %all-to-all-start = ((bf16[8,32,512]{2,1,0:T(8,128)(2,1)}), bf16[8,32,512]{2,1,0:T(8,128)(2,1)S(1)}, u32[]{:S(2)}, u32[]{:S(2)}) async-start(bf16[8,32,512]{2,1,0:T(8,128)(2,1)} %copy-done.15), calls=%async_computation | async-start | bytes 524288 | tf_op jit(solution)/shard_map/all_to_all | solution.py:385
  22.8 1.3 %collective-permute-done.3.refs_4_ = bf16[128,1024]{1,0:T(8,128)(2,1)} collective-permute-done((bf16[128,1024]{1,0:T(8,128)(2,1)}, bf16[128,1024]{1,0:T(8,128)(2,1)}, u32[]{:S(2)}, u32[]{:S(2)}) %collective-permute-start.3) | collective-permute-done | bytes 262176 | tf_op jit(solution)/shard_map/ppermute | solution.py:321
  24.0 1.2 %collective-permute-start.5 = (bf16[128,1024]{1,0:T(8,128)(2,1)}, bf16[128,1024]{1,0:T(8,128)(2,1)}, u32[]{:S(2)}, u32[]{:S(2)}) collective-permute-start(bf16[128,1024]{1,0:T(8,128)(2,1)} %collective-permute-done.3.refs_4_), channel_id=1, source_target_pairs={{0,8},{4,12},{8,0},{12,4},{16,24},{20,28},{24,16},{28,20},{1,9},{5... | collective-permute-start | bytes 786440 | tf_op jit(solution)/shard_map/ppermute | solution.py:321
  25.5 1.0 %collective-permute-start.4 = (bf16[128,1024]{1,0:T(8,128)(2,1)}, bf16[128,1024]{1,0:T(8,128)(2,1)}, u32[]{:S(2)}, u32[]{:S(2)}) collective-permute-start(bf16[128,1024]{1,0:T(8,128)(2,1)} %collective-permute-done.3.refs_4_), channel_id=1, source_target_pairs={{0,4},{4,0},{8,12},{12,8},{16,20},{20,16},{24,28},{28,24},{1,5},{5... | collective-permute-start | bytes 786440 | tf_op jit(solution)/shard_map/ppermute | solution.py:321
  26.5 1.0 %collective-permute-start.2 = (bf16[128,1024]{1,0:T(8,128)(2,1)}, bf16[128,1024]{1,0:T(8,128)(2,1)}, u32[]{:S(2)}, u32[]{:S(2)}) collective-permute-start(bf16[128,1024]{1,0:T(8,128)(2,1)} %collective-permute-done.1.refs_2_), channel_id=1, source_target_pairs={{0,4},{4,0},{8,12},{12,8},{16,20},{20,16},{24,28},{28,24},{1,5},{5... | collective-permute-start | bytes 786440 | tf_op jit(solution)/shard_map/ppermute | solution.py:321
  27.5 7.5 %collective-permute-done.5.refs_6_ = bf16[128,1024]{1,0:T(8,128)(2,1)} collective-permute-done((bf16[128,1024]{1,0:T(8,128)(2,1)}, bf16[128,1024]{1,0:T(8,128)(2,1)}, u32[]{:S(2)}, u32[]{:S(2)}) %collective-permute-start.5) | collective-permute-done | bytes 262176 | tf_op jit(solution)/shard_map/ppermute | solution.py:321
  35.6 1.5 %collective-permute-start.7 = (bf16[8,32,512]{2,1,0:T(8,128)(2,1)S(1)}, bf16[8,32,512]{2,1,0:T(8,128)(2,1)}, u32[]{:S(2)}, u32[]{:S(2)}) collective-permute-start(bf16[8,32,512]{2,1,0:T(8,128)(2,1)S(1)} %all-to-all-done.refs_0_), channel_id=1, source_target_pairs={{0,2},{1,3},{2,0},{3,1},{4,6},{5,7},{6,4},{7,5},{8,10},{9,11},{10,... | collective-permute-start | bytes 786440 | tf_op jit(solution)/shard_map/ppermute | solution.py:321
  37.2 2.4 %factors.1 = (f32[128,2048]{1,0:T(8,128)S(1)}, f32[128,512]{1,0:T(8,128)S(1)}, f32[128,512]{1,0:T(8,128)S(1)}, f32[128,512]{1,0:T(8,128)S(1)}, f32[128,512]{1,0:T(8,128)S(1)}) custom-call(s32[1]{0:T(128)} %bitcast.at_ref, bf16[128,2048]{1,0:T(8,128)(2,1)S(1)} %copy-done.2, s32[2,128,2048]{2,1,0:T(8,128)S(1)} %copy-done.1, f32[1,2048]{1,0:T(1,128)S(1)} %bitcast.22, ...), custom_call_target="tpu_custom_call" | custom-call | tf_op jit(solution)/shard_map/factors/pallas_call | solution.py:149
  39.6 1.0 %copy-done.5 = f32[128,2048]{1,0:T(8,128)} copy-done((f32[128,2048]{1,0:T(8,128)}, f32[128,2048]{1,0:T(8,128)S(1)}, u32[]{:S(2)}) %copy-start.5) | copy-done | bytes 1048600
  40.5 0.7 copy-done.7
  41.3 0.7 copy-done.9
  42.0 0.7 copy-done.11
  43.8 2.1 %collective-permute-done.6.refs_7_ = bf16[128,1024]{1,0:T(8,128)(2,1)} collective-permute-done((bf16[128,1024]{1,0:T(8,128)(2,1)}, bf16[128,1024]{1,0:T(8,128)(2,1)}, u32[]{:S(2)}, u32[]{:S(2)}) %collective-permute-start.6) | collective-permute-done | bytes 262176 | tf_op jit(solution)/shard_map/ppermute | solution.py:321
  45.9 0.9 %copy-done.17 = bf16[128,1024]{1,0:T(8,128)(2,1)S(1)} copy-done((bf16[128,1024]{1,0:T(8,128)(2,1)S(1)}, bf16[128,1024]{1,0:T(8,128)(2,1)}, u32[]{:S(2)}) %copy-start.17) | copy-done | bytes 262168
  46.9 11.5 %attention.1.refs_4_ = bf16[4,1024,256]{2,1,0:T(8,128)(2,1)S(1)} custom-call(bf16[128,1024]{1,0:T(8,128)(2,1)} %get-tuple-element.24.refs_0_, bf16[128,1024]{1,0:T(8,128)(2,1)S(1)} %copy-done.17, bf16[128,1024]{1,0:T(8,128)(2,1)} %collective-permute-done.1.refs_2_, bf16[128,1024]{1,0:T(8,128)(2,1)} %collective-permute-done.2.refs_3_, ...), custom_call_target="tpu_custom_call" | custom-call | tf_op jit(solution)/shard_map/attention/pallas_call | solution.py:215
  58.5 1.4 %spread.1 = (f32[264,512]{1,0:T(8,128)S(1)}, f32[264,512]{1,0:T(8,128)S(1)}, f32[2,264,512]{2,1,0:T(8,128)S(1)}) custom-call(s32[1]{0:T(128)} %bitcast.at_ref, bf16[4,128,256]{2,1,0:T(8,128)(2,1)S(1)} %slice.54.grad_ref, bf16[3,2048,256]{2,1,0:T(8,128)(2,1)S(1)} %bitcast.20, bf16[256,2048]{1,0:T(8,128)(2,1)S(1)} %copy-done.3, ...), custom_call_target="tpu_custom_call" | custom-call | tf_op jit(solution)/shard_map/spread/pallas_call | solution.py:305
  60.6 2.1 %collective-permute-done.8 = f32[2,264,512]{2,1,0:T(8,128)S(1)} collective-permute-done((f32[2,264,512]{2,1,0:T(8,128)S(1)}, f32[2,264,512]{2,1,0:T(8,128)S(1)}, u32[]{:S(2)}, u32[]{:S(2)}) %collective-permute-start.8) | collective-permute-done | bytes 1081376 | tf_op jit(solution)/shard_map/ppermute | solution.py:321
  63.0 1.6 %collective-permute-start.10 = (f32[8,512]{1,0:T(8,128)S(1)}, f32[8,512]{1,0:T(8,128)S(1)}, u32[]{:S(2)}, u32[]{:S(2)}) collective-permute-start(f32[8,512]{1,0:T(8,128)S(1)} %slice.61), channel_id=1, source_target_pairs={{0,2},{1,3},{2,0},{3,1},{4,6},{5,7},{6,4},{7,5},{8,10},{9,11},{10,... | collective-permute-start | bytes 49160 | tf_op jit(solution)/shard_map/ppermute | solution.py:321
  64.6 2.2 %collective-permute-done.10 = f32[8,512]{1,0:T(8,128)S(1)} collective-permute-done((f32[8,512]{1,0:T(8,128)S(1)}, f32[8,512]{1,0:T(8,128)S(1)}, u32[]{:S(2)}, u32[]{:S(2)}) %collective-permute-start.10) | collective-permute-done | bytes 16416 | tf_op jit(solution)/shard_map/ppermute | solution.py:321
  67.2 1.5 %collective-permute-start.9 = (bf16[256,512]{1,0:T(8,128)(2,1)S(1)}, bf16[256,512]{1,0:T(8,128)(2,1)S(1)}, u32[]{:S(2)}, u32[]{:S(2)}) collective-permute-start(bf16[256,512]{1,0:T(8,128)(2,1)S(1)} %pad_maximum_fusion), channel_id=1, source_target_pairs={{0,2},{1,3},{2,0},{3,1},{4,6},{5,7},{6,4},{7,5},{8,10},{9,11},{10,... | collective-permute-start | bytes 786440 | tf_op jit(solution)/shard_map/ppermute | solution.py:321
  68.7 1.7 %collective-permute-done.11 = f32[512]{0:T(512)S(1)} collective-permute-done((f32[512]{0:T(512)S(1)}, f32[512]{0:T(512)S(1)}, u32[]{:S(2)}, u32[]{:S(2)}) %collective-permute-start.11) | collective-permute-done | bytes 2080 | tf_op jit(solution)/shard_map/ppermute | solution.py:321
  71.0 2.7 %weight_grads.1 = (f32[3,256,256]{2,1,0:T(8,128)}, f32[256,256]{1,0:T(8,128)}) custom-call(s32[2]{0:T(128)S(1)} %pad_add_fusion.at_ref, bf16[8,32,512]{2,1,0:T(8,128)(2,1)S(1)} %all-to-all-done.refs_0_, bf16[8,32,512]{2,1,0:T(8,128)(2,1)S(1)} %collective-permute-done.13.refs_1_, bf16[8,32,512]{2,1,0:T(8,128)(2,1)} %collective-permute-done.7.refs_2_, ...), custom_call_target="tpu_custom_call" | custom-call | tf_op jit(solution)/shard_map/weight_grads/pallas_call | solution.py:342
  74.0 2.6 %collective-permute-start.15 = (f32[512]{0:T(512)S(1)}, f32[512]{0:T(512)S(1)}, u32[]{:S(2)}, u32[]{:S(2)}) collective-permute-start(f32[512]{0:T(512)S(1)} %add.66), channel_id=1, source_target_pairs={{0,16},{4,20},{8,24},{12,28},{16,0},{20,4},{24,8},{28,12},{1,17},{... | collective-permute-start | bytes 6152 | tf_op jit(solution)/shard_map/ppermute | solution.py:321
  76.6 1.9 %collective-permute-done.15 = f32[512]{0:T(512)S(1)} collective-permute-done((f32[512]{0:T(512)S(1)}, f32[512]{0:T(512)S(1)}, u32[]{:S(2)}, u32[]{:S(2)}) %collective-permute-start.15) | collective-permute-done | bytes 2080 | tf_op jit(solution)/shard_map/ppermute | solution.py:321
  79.1 0.9 %fusion.4 = (f32[128,512]{1,0:T(8,128)}, bf16[128,512]{1,0:T(8,128)(2,1)}) fusion(f32[128,512]{1,0:T(8,128)S(1)} %copy-done.12, f32[128,512]{1,0:T(8,128)S(1)} %copy-done.8, f32[264,512]{1,0:T(8,128)S(1)} %get-tuple-element.41, f32[128,512]{1,0:T(8,128)S(1)} %copy-done.10, f32[128]{0:T(128)S(1)} %slice_bitcast_fusion.2, ...), kind=kLoop, calls=%fused_computation.7 | loop fusion | flops 655360 | bytes 2228736 | tf_op jit(solution)/shard_map/add | solution.py:419
  (70 shorter events, 4.9 us)
Async XLA Ops:
  0.6 22.0 %copy-start.19 = (s32[1024]{0:T(1024)S(1)}, s32[1024]{0:T(1024)}, u32[]{:S(2)}) copy-start(s32[1024]{0:T(1024)} %param.8) | copy-start | bytes 12292
  0.6 36.5 %copy-start.1 = (s32[2,128,2048]{2,1,0:T(8,128)S(1)}, s32[2,128,2048]{2,1,0:T(8,128)}, u32[]{:S(2)}) copy-start(s32[2,128,2048]{2,1,0:T(8,128)} %pulse_ref.1) | copy-start | bytes 6291460
  0.7 36.5 %copy-start.2 = (bf16[128,2048]{1,0:T(8,128)(2,1)S(1)}, bf16[128,2048]{1,0:T(8,128)(2,1)}, u32[]{:S(2)}) copy-start(bf16[128,2048]{1,0:T(8,128)(2,1)} %tok_ref.3) | copy-start | bytes 1572868
  0.7 36.5 %copy-start.4 = (bf16[128,2048]{1,0:T(8,128)(2,1)S(1)}, bf16[128,2048]{1,0:T(8,128)(2,1)}, u32[]{:S(2)}) copy-start(bf16[128,2048]{1,0:T(8,128)(2,1)} %up_ref.1) | copy-start | bytes 1572868
  0.7 36.5 %copy-start.18 = (f32[2048]{0:T(1024)S(1)}, f32[2048]{0:T(1024)}, u32[]{:S(2)}) copy-start(f32[2048]{0:T(1024)} %param.10) | copy-start | bytes 24580
  6.4 9.5 %collective-permute-start = (bf16[128,1024]{1,0:T(8,128)(2,1)}, bf16[128,1024]{1,0:T(8,128)(2,1)S(1)}, u32[]{:S(2)}, u32[]{:S(2)}) collective-permute-start(bf16[128,1024]{1,0:T(8,128)(2,1)} %get-tuple-element.24.refs_0_), channel_id=1, source_target_pairs={{0,4},{4,0},{8,12},{12,8},{16,20},{20,16},{24,28},{28,24},{1,5},{5... | collective-permute-start | bytes 786440 | tf_op jit(solution)/shard_map/ppermute | solution.py:321
  9.3 14.7 %collective-permute-start.3 = (bf16[128,1024]{1,0:T(8,128)(2,1)}, bf16[128,1024]{1,0:T(8,128)(2,1)}, u32[]{:S(2)}, u32[]{:S(2)}) collective-permute-start(bf16[128,1024]{1,0:T(8,128)(2,1)} %get-tuple-element.24.refs_0_), channel_id=1, source_target_pairs={{0,16},{4,20},{8,24},{12,28},{16,0},{20,4},{24,8},{28,12},{1,17},{... | collective-permute-start | bytes 786440 | tf_op jit(solution)/shard_map/ppermute | solution.py:321
  11.9 14.6 %collective-permute-start.1 = (bf16[128,1024]{1,0:T(8,128)(2,1)}, bf16[128,1024]{1,0:T(8,128)(2,1)}, u32[]{:S(2)}, u32[]{:S(2)}) collective-permute-start(bf16[128,1024]{1,0:T(8,128)(2,1)} %get-tuple-element.24.refs_0_), channel_id=1, source_target_pairs={{0,8},{4,12},{8,0},{12,4},{16,24},{20,28},{24,16},{28,20},{1,9},{5... | collective-permute-start | bytes 786440 | tf_op jit(solution)/shard_map/ppermute | solution.py:321
  16.5 19.0 %all-to-all-start = ((bf16[8,32,512]{2,1,0:T(8,128)(2,1)}), bf16[8,32,512]{2,1,0:T(8,128)(2,1)S(1)}, u32[]{:S(2)}, u32[]{:S(2)}) async-start(bf16[8,32,512]{2,1,0:T(8,128)(2,1)} %copy-done.15), calls=%async_computation | async-start | bytes 524288 | tf_op jit(solution)/shard_map/all_to_all | solution.py:385
  24.0 11.0 %collective-permute-start.5 = (bf16[128,1024]{1,0:T(8,128)(2,1)}, bf16[128,1024]{1,0:T(8,128)(2,1)}, u32[]{:S(2)}, u32[]{:S(2)}) collective-permute-start(bf16[128,1024]{1,0:T(8,128)(2,1)} %collective-permute-done.3.refs_4_), channel_id=1, source_target_pairs={{0,8},{4,12},{8,0},{12,4},{16,24},{20,28},{24,16},{28,20},{1,9},{5... | collective-permute-start | bytes 786440 | tf_op jit(solution)/shard_map/ppermute | solution.py:321
  25.5 18.3 %collective-permute-start.4 = (bf16[128,1024]{1,0:T(8,128)(2,1)}, bf16[128,1024]{1,0:T(8,128)(2,1)}, u32[]{:S(2)}, u32[]{:S(2)}) collective-permute-start(bf16[128,1024]{1,0:T(8,128)(2,1)} %collective-permute-done.3.refs_4_), channel_id=1, source_target_pairs={{0,4},{4,0},{8,12},{12,8},{16,20},{20,16},{24,28},{28,24},{1,5},{5... | collective-permute-start | bytes 786440 | tf_op jit(solution)/shard_map/ppermute | solution.py:321
  26.5 17.3 %collective-permute-start.2 = (bf16[128,1024]{1,0:T(8,128)(2,1)}, bf16[128,1024]{1,0:T(8,128)(2,1)}, u32[]{:S(2)}, u32[]{:S(2)}) collective-permute-start(bf16[128,1024]{1,0:T(8,128)(2,1)} %collective-permute-done.1.refs_2_), channel_id=1, source_target_pairs={{0,4},{4,0},{8,12},{12,8},{16,20},{20,16},{24,28},{28,24},{1,5},{5... | collective-permute-start | bytes 786440 | tf_op jit(solution)/shard_map/ppermute | solution.py:321
  35.0 10.9 %collective-permute-start.6 = (bf16[128,1024]{1,0:T(8,128)(2,1)}, bf16[128,1024]{1,0:T(8,128)(2,1)}, u32[]{:S(2)}, u32[]{:S(2)}) collective-permute-start(bf16[128,1024]{1,0:T(8,128)(2,1)} %collective-permute-done.5.refs_6_), channel_id=1, source_target_pairs={{0,4},{4,0},{8,12},{12,8},{16,20},{20,16},{24,28},{28,24},{1,5},{5... | collective-permute-start | bytes 786440 | tf_op jit(solution)/shard_map/ppermute | solution.py:321
  35.6 8.0 %collective-permute-start.7 = (bf16[8,32,512]{2,1,0:T(8,128)(2,1)S(1)}, bf16[8,32,512]{2,1,0:T(8,128)(2,1)}, u32[]{:S(2)}, u32[]{:S(2)}) collective-permute-start(bf16[8,32,512]{2,1,0:T(8,128)(2,1)S(1)} %all-to-all-done.refs_0_), channel_id=1, source_target_pairs={{0,2},{1,3},{2,0},{3,1},{4,6},{5,7},{6,4},{7,5},{8,10},{9,11},{10,... | collective-permute-start | bytes 786440 | tf_op jit(solution)/shard_map/ppermute | solution.py:321
  39.6 1.0 %copy-start.5 = (f32[128,2048]{1,0:T(8,128)}, f32[128,2048]{1,0:T(8,128)S(1)}, u32[]{:S(2)}) copy-start(f32[128,2048]{1,0:T(8,128)S(1)} %get-tuple-element.28.factor_ref) | copy-start | bytes 3145732
  40.5 0.7 copy-start.7
  45.9 1.0 %copy-start.17 = (bf16[128,1024]{1,0:T(8,128)(2,1)S(1)}, bf16[128,1024]{1,0:T(8,128)(2,1)}, u32[]{:S(2)}) copy-start(bf16[128,1024]{1,0:T(8,128)(2,1)} %copy-done.16) | copy-start | bytes 786436
  46.9 11.6 %copy-start = (bf16[2048,3,256]{2,0,1:T(8,128)(2,1)S(1)}, bf16[2048,3,256]{2,0,1:T(8,128)(2,1)}, u32[]{:S(2)}) copy-start(bf16[2048,3,256]{2,0,1:T(8,128)(2,1)} %param.11) | copy-start | bytes 9437188
  46.9 11.6 %copy-start.3 = (bf16[256,2048]{1,0:T(8,128)(2,1)S(1)}, bf16[256,2048]{1,0:T(8,128)(2,1)}, u32[]{:S(2)}) copy-start(bf16[256,2048]{1,0:T(8,128)(2,1)} %wout_ref.1) | copy-start | bytes 3145732
  46.9 11.6 %copy-start.6 = (f32[128,2048]{1,0:T(8,128)S(1)}, f32[128,2048]{1,0:T(8,128)}, u32[]{:S(2)}) copy-start(f32[128,2048]{1,0:T(8,128)} %copy-done.5) | copy-start | bytes 3145732
  59.9 2.7 %collective-permute-start.8 = (f32[2,264,512]{2,1,0:T(8,128)S(1)}, f32[2,264,512]{2,1,0:T(8,128)S(1)}, u32[]{:S(2)}, u32[]{:S(2)}) collective-permute-start(f32[2,264,512]{2,1,0:T(8,128)S(1)} %get-tuple-element.30), channel_id=1, source_target_pairs={{0,1},{1,0},{2,3},{3,2},{4,5},{5,4},{6,7},{7,6},{8,9},{9,8},{10,11... | collective-permute-start | bytes 3244040 | tf_op jit(solution)/shard_map/ppermute | solution.py:321
  60.0 11.0 %collective-permute-start.13 = (bf16[8,32,512]{2,1,0:T(8,128)(2,1)S(1)}, bf16[8,32,512]{2,1,0:T(8,128)(2,1)S(1)}, u32[]{:S(2)}, u32[]{:S(2)}) collective-permute-start(bf16[8,32,512]{2,1,0:T(8,128)(2,1)S(1)} %all-to-all-done.refs_0_), channel_id=1, source_target_pairs={{0,1},{1,0},{2,3},{3,2},{4,5},{5,4},{6,7},{7,6},{8,9},{9,8},{10,11... | collective-permute-start | bytes 786440 | tf_op jit(solution)/shard_map/ppermute | solution.py:321
  60.5 10.6 %collective-permute-start.14 = (bf16[8,32,512]{2,1,0:T(8,128)(2,1)}, bf16[8,32,512]{2,1,0:T(8,128)(2,1)S(1)}, u32[]{:S(2)}, u32[]{:S(2)}) collective-permute-start(bf16[8,32,512]{2,1,0:T(8,128)(2,1)} %collective-permute-done.7.refs_2_), channel_id=1, source_target_pairs={{0,1},{1,0},{2,3},{3,2},{4,5},{5,4},{6,7},{7,6},{8,9},{9,8},{10,11... | collective-permute-start | bytes 786440 | tf_op jit(solution)/shard_map/ppermute | solution.py:321
  63.0 3.8 %collective-permute-start.10 = (f32[8,512]{1,0:T(8,128)S(1)}, f32[8,512]{1,0:T(8,128)S(1)}, u32[]{:S(2)}, u32[]{:S(2)}) collective-permute-start(f32[8,512]{1,0:T(8,128)S(1)} %slice.61), channel_id=1, source_target_pairs={{0,2},{1,3},{2,0},{3,1},{4,6},{5,7},{6,4},{7,5},{8,10},{9,11},{10,... | collective-permute-start | bytes 49160 | tf_op jit(solution)/shard_map/ppermute | solution.py:321
  64.5 14.6 %copy-start.8 = (f32[128,512]{1,0:T(8,128)S(1)}, f32[128,512]{1,0:T(8,128)}, u32[]{:S(2)}) copy-start(f32[128,512]{1,0:T(8,128)} %copy-done.7) | copy-start | bytes 786436
  64.5 14.6 %copy-start.10 = (f32[128,512]{1,0:T(8,128)S(1)}, f32[128,512]{1,0:T(8,128)}, u32[]{:S(2)}) copy-start(f32[128,512]{1,0:T(8,128)} %copy-done.9) | copy-start | bytes 786436
  64.5 14.6 %copy-start.12 = (f32[128,512]{1,0:T(8,128)S(1)}, f32[128,512]{1,0:T(8,128)}, u32[]{:S(2)}) copy-start(f32[128,512]{1,0:T(8,128)} %copy-done.11) | copy-start | bytes 786436
  64.5 14.6 %copy-start.14 = (f32[128,512]{1,0:T(8,128)S(1)}, f32[128,512]{1,0:T(8,128)}, u32[]{:S(2)}) copy-start(f32[128,512]{1,0:T(8,128)} %copy-done.13) | copy-start | bytes 786436
  66.8 3.7 %collective-permute-start.11 = (f32[512]{0:T(512)S(1)}, f32[512]{0:T(512)S(1)}, u32[]{:S(2)}, u32[]{:S(2)}) collective-permute-start(f32[512]{0:T(512)S(1)} %bitcast.26), channel_id=1, source_target_pairs={{0,4},{4,0},{8,12},{12,8},{16,20},{20,16},{24,28},{28,24},{1,5},{5... | collective-permute-start | bytes 6152 | tf_op jit(solution)/shard_map/ppermute | solution.py:321
  67.2 11.9 %collective-permute-start.9 = (bf16[256,512]{1,0:T(8,128)(2,1)S(1)}, bf16[256,512]{1,0:T(8,128)(2,1)S(1)}, u32[]{:S(2)}, u32[]{:S(2)}) collective-permute-start(bf16[256,512]{1,0:T(8,128)(2,1)S(1)} %pad_maximum_fusion), channel_id=1, source_target_pairs={{0,2},{1,3},{2,0},{3,1},{4,6},{5,7},{6,4},{7,5},{8,10},{9,11},{10,... | collective-permute-start | bytes 786440 | tf_op jit(solution)/shard_map/ppermute | solution.py:321
  70.4 3.6 %collective-permute-start.12 = (f32[512]{0:T(512)S(1)}, f32[512]{0:T(512)S(1)}, u32[]{:S(2)}, u32[]{:S(2)}) collective-permute-start(f32[512]{0:T(512)S(1)} %add.65), channel_id=1, source_target_pairs={{0,8},{4,12},{8,0},{12,4},{16,24},{20,28},{24,16},{28,20},{1,9},{5... | collective-permute-start | bytes 6152 | tf_op jit(solution)/shard_map/ppermute | solution.py:321
  74.0 4.5 %collective-permute-start.15 = (f32[512]{0:T(512)S(1)}, f32[512]{0:T(512)S(1)}, u32[]{:S(2)}, u32[]{:S(2)}) collective-permute-start(f32[512]{0:T(512)S(1)} %add.66), channel_id=1, source_target_pairs={{0,16},{4,20},{8,24},{12,28},{16,0},{20,4},{24,8},{28,12},{1,17},{... | collective-permute-start | bytes 6152 | tf_op jit(solution)/shard_map/ppermute | solution.py:321
  (5 other events, 3.5 us)

commit v4 on v3

--- a/solution.py
+++ b/solution.py
@@ -387,7 +387,6 @@
         pieces = [both, swap(both, "fsdp", 1), over, swap(over, "fsdp", 1)]
         grads = attention(blocks, after(placed, over))
         own_grads = grads[:, :rows]
-        in_grad, out_grad = weight_grads(fsdp_rank, ctx_rank, pieces, grads)
     else:
         grads = long_attention(lax.all_gather(payload, "ctx", axis=0, tiled=True), positions)
         own_grads = lax.dynamic_slice_in_dim(grads, ctx_rank * rows, rows, 1)
@@ -407,11 +406,14 @@
     landed = swap(jnp.concatenate([far[:rows], far[rows + SUM_ROWS :]]).astype(BF16), "fsdp", 2)
     gain_grad = line[1]
     if short:
-        for mask in (1, 2, 4):
-            gain_grad = gain_grad + swap(gain_grad, "ctx", mask)
-            if mask == 2:
-                landed = after(landed, gain_grad)
-        landed = after(landed, in_grad, out_grad)
+        corner_pairs = [
+            (c * fsdp + f, (c ^ 1) * fsdp + (f ^ 2)) for c in range(ctx) for f in range(fsdp)
+        ]
+        aside = swap(own[rows + 1], "ctx", 1)
+        aside = aside + lax.ppermute(far[rows + 1], ("ctx", "fsdp"), corner_pairs)
+        gain_grad = gain_grad + aside
+        in_grad, out_grad = weight_grads(after(fsdp_rank, gain_grad), ctx_rank, pieces, grads)
+        second, third, fourth = (swap(gain_grad, "ctx", mask) for mask in (2, 4, 6))
     else:
         gain_grad = lax.psum(gain_grad, "ctx")
 
@@ -419,6 +421,9 @@
     token_grad = base + (rise * grad_spikes - fall * line[0, :rows][:, None])
     projected = own[rows + SUM_ROWS :] + landed[rows:].astype(F32)
     block_out = (token_share + projected).astype(BF16)
+    if short:
+        third = after(third, token_grad, block_out)
+        gain_grad = (gain_grad + second) + (third + fourth)
     return (block_out, token_grad, gain_grad, jnp.transpose(in_grad, (1, 0, 2)), out_grad)
 
 

time: 80.2 us -> 78.7 us (0.981)
  waiting for transfers between devices: 21.5 us -> 17.1 us
  starting transfers between devices: 25.6 us -> 28.5 us
    ppermute x16 -> x17, waiting for transfers between devices: 21.5 us -> 16 us  [swap(): return lax.ppermute(value, axis, [(i, i ^ mask) for i in range(count)])]
    ppermute x0 -> x1, starting transfers between devices: none -> 1.72 us  [body(): aside = aside + lax.ppermute(far[rows + 1], ('ctx', 'fsdp'), corner_pairs)]
    ppermute x16 -> x17, starting transfers between devices: 19.6 us -> 20.7 us  [swap(): return lax.ppermute(value, axis, [(i, i ^ mask) for i in range(count)])]
    ppermute x0 -> x1, waiting for transfers between devices: none -> 1.01 us  [body(): aside = aside + lax.ppermute(far[rows + 1], ('ctx', 'fsdp'), corner_pairs)]
  transfers between devices with their start and end apart: 17 -> 19, of which waited for: 9 -> 8; matrix products, arithmetic and copies ran while one was open for 2% -> 3% of each run, Pallas kernels for 6% -> 7%
where the time goes in v4:
time: 78.7 us; the launch traced here: 78.5 us
  starting transfers between devices  28.5 us (36%)
  Pallas kernels  23.1 us (29%)
  waiting for transfers between devices  17.1 us (22%)
  local copies, waits for them, and re-layouts  7.15 us (9%)
  other arithmetic  1.79 us (2%)
  between operations  0.91 us (1%)
    ppermute x17, starting transfers between devices, swap(): return lax.ppermute(value, axis, [(i, i ^ mask) for i in range(count)])  20.7 us
    ppermute x17, waiting for transfers between devices, swap(): return lax.ppermute(value, axis, [(i, i ^ mask) for i in range(count)])  16 us
    pallas_call x1, Pallas kernels, attention(): pl.pallas_call(attention_kernel, in_specs=[in_vmem] * (len(pieces) + 2),...  11.5 us
    unnamed x47, local copies, waits for them, and re-layouts  6.8 us
    all_to_all x1, starting transfers between devices, body(): both = lax.all_to_all(after(both, below), 'ctx', 0, 0)  6.05 us
    pallas_call x1, Pallas kernels, project(): pl.pallas_call(project_kernel, in_specs=[pl.BlockSpec(memory_space=pltpu....  4.96 us
    pallas_call x1, Pallas kernels, weight_grads(): pl.pallas_call(weight_kernel, in_specs=[pl.BlockSpec(memory_space=pltpu.S...  2.73 us
    pallas_call x1, Pallas kernels, factors(): pl.pallas_call(factor_kernel, in_specs=[pl.BlockSpec(memory_space=pltpu.S...  2.39 us
  transfers between devices with their start and end apart: 19, of which 8 were waited for; matrix products, arithmetic and copies ran while one was open for 3% of the time, Pallas kernels for 7%

profile of v4, /device:TPU:0, one launch (start us, length us, event | category | flops | bytes accessed | tf_op | source)
XLA Modules:
  0.0 78.5 jit_solution(14253385946026994173)
XLA Ops:
  0.7 5.0 %project.1 = (bf16[128,1024]{1,0:T(8,128)(2,1)}, bf16[128,2048]{1,0:T(8,128)(2,1)}, f32[128,1]{1,0:T(8,128)S(1)}, bf16[8,32,512]{2,1,0:T(8,128)(2,1)S(1)}) custom-call(s32[1]{0:T(128)} %bitcast.at_ref, bf16[128,2048]{1,0:T(8,128)(2,1)} %tok_ref.3, s32[2,128,2048]{2,1,0:T(8,128)} %pulse_ref.1, f32[1,2048]{1,0:T(1,128)} %bitcast.24, ...), custom_call_target="tpu_custom_call" | custom-call | tf_op jit(solution)/shard_map/project/pallas_call | solution.py:96
  5.7 0.7 copy-done.15
  6.4 3.0 %collective-permute-start = (bf16[128,1024]{1,0:T(8,128)(2,1)}, bf16[128,1024]{1,0:T(8,128)(2,1)S(1)}, u32[]{:S(2)}, u32[]{:S(2)}) collective-permute-start(bf16[128,1024]{1,0:T(8,128)(2,1)} %get-tuple-element.24.refs_0_), channel_id=1, source_target_pairs={{0,4},{4,0},{8,12},{12,8},{16,20},{20,16},{24,28},{28,24},{1,5},{5... | collective-permute-start | bytes 786440 | tf_op jit(solution)/shard_map/ppermute | solution.py:321
  9.3 2.6 %collective-permute-start.3 = (bf16[128,1024]{1,0:T(8,128)(2,1)}, bf16[128,1024]{1,0:T(8,128)(2,1)}, u32[]{:S(2)}, u32[]{:S(2)}) collective-permute-start(bf16[128,1024]{1,0:T(8,128)(2,1)} %get-tuple-element.24.refs_0_), channel_id=1, source_target_pairs={{0,16},{4,20},{8,24},{12,28},{16,0},{20,4},{24,8},{28,12},{1,17},{... | collective-permute-start | bytes 786440 | tf_op jit(solution)/shard_map/ppermute | solution.py:321
  11.9 1.6 %collective-permute-start.1 = (bf16[128,1024]{1,0:T(8,128)(2,1)}, bf16[128,1024]{1,0:T(8,128)(2,1)}, u32[]{:S(2)}, u32[]{:S(2)}) collective-permute-start(bf16[128,1024]{1,0:T(8,128)(2,1)} %get-tuple-element.24.refs_0_), channel_id=1, source_target_pairs={{0,8},{4,12},{8,0},{12,4},{16,24},{20,28},{24,16},{28,20},{1,9},{5... | collective-permute-start | bytes 786440 | tf_op jit(solution)/shard_map/ppermute | solution.py:321
  13.5 2.4 %collective-permute-done.refs_1_ = bf16[128,1024]{1,0:T(8,128)(2,1)S(1)} collective-permute-done((bf16[128,1024]{1,0:T(8,128)(2,1)}, bf16[128,1024]{1,0:T(8,128)(2,1)S(1)}, u32[]{:S(2)}, u32[]{:S(2)}) %collective-permute-start) | collective-permute-done | bytes 262176 | tf_op jit(solution)/shard_map/ppermute | solution.py:321
  15.8 0.7 copy-done.16
  16.5 6.1 %all-to-all-start = ((bf16[8,32,512]{2,1,0:T(8,128)(2,1)}), bf16[8,32,512]{2,1,0:T(8,128)(2,1)S(1)}, u32[]{:S(2)}, u32[]{:S(2)}) async-start(bf16[8,32,512]{2,1,0:T(8,128)(2,1)} %copy-done.15), calls=%async_computation | async-start | bytes 524288 | tf_op jit(solution)/shard_map/all_to_all | solution.py:385
  22.8 1.3 %collective-permute-done.3.refs_4_ = bf16[128,1024]{1,0:T(8,128)(2,1)} collective-permute-done((bf16[128,1024]{1,0:T(8,128)(2,1)}, bf16[128,1024]{1,0:T(8,128)(2,1)}, u32[]{:S(2)}, u32[]{:S(2)}) %collective-permute-start.3) | collective-permute-done | bytes 262176 | tf_op jit(solution)/shard_map/ppermute | solution.py:321
  24.0 1.2 %collective-permute-start.5 = (bf16[128,1024]{1,0:T(8,128)(2,1)}, bf16[128,1024]{1,0:T(8,128)(2,1)}, u32[]{:S(2)}, u32[]{:S(2)}) collective-permute-start(bf16[128,1024]{1,0:T(8,128)(2,1)} %collective-permute-done.3.refs_4_), channel_id=1, source_target_pairs={{0,8},{4,12},{8,0},{12,4},{16,24},{20,28},{24,16},{28,20},{1,9},{5... | collective-permute-start | bytes 786440 | tf_op jit(solution)/shard_map/ppermute | solution.py:321
  25.5 1.0 %collective-permute-start.4 = (bf16[128,1024]{1,0:T(8,128)(2,1)}, bf16[128,1024]{1,0:T(8,128)(2,1)}, u32[]{:S(2)}, u32[]{:S(2)}) collective-permute-start(bf16[128,1024]{1,0:T(8,128)(2,1)} %collective-permute-done.3.refs_4_), channel_id=1, source_target_pairs={{0,4},{4,0},{8,12},{12,8},{16,20},{20,16},{24,28},{28,24},{1,5},{5... | collective-permute-start | bytes 786440 | tf_op jit(solution)/shard_map/ppermute | solution.py:321
  26.5 1.0 %collective-permute-start.2 = (bf16[128,1024]{1,0:T(8,128)(2,1)}, bf16[128,1024]{1,0:T(8,128)(2,1)}, u32[]{:S(2)}, u32[]{:S(2)}) collective-permute-start(bf16[128,1024]{1,0:T(8,128)(2,1)} %collective-permute-done.1.refs_2_), channel_id=1, source_target_pairs={{0,4},{4,0},{8,12},{12,8},{16,20},{20,16},{24,28},{28,24},{1,5},{5... | collective-permute-start | bytes 786440 | tf_op jit(solution)/shard_map/ppermute | solution.py:321
  27.5 7.5 %collective-permute-done.5.refs_6_ = bf16[128,1024]{1,0:T(8,128)(2,1)} collective-permute-done((bf16[128,1024]{1,0:T(8,128)(2,1)}, bf16[128,1024]{1,0:T(8,128)(2,1)}, u32[]{:S(2)}, u32[]{:S(2)}) %collective-permute-start.5) | collective-permute-done | bytes 262176 | tf_op jit(solution)/shard_map/ppermute | solution.py:321
  35.6 1.5 %collective-permute-start.7 = (bf16[8,32,512]{2,1,0:T(8,128)(2,1)S(1)}, bf16[8,32,512]{2,1,0:T(8,128)(2,1)}, u32[]{:S(2)}, u32[]{:S(2)}) collective-permute-start(bf16[8,32,512]{2,1,0:T(8,128)(2,1)S(1)} %all-to-all-done.refs_0_), channel_id=1, source_target_pairs={{0,2},{1,3},{2,0},{3,1},{4,6},{5,7},{6,4},{7,5},{8,10},{9,11},{10,... | collective-permute-start | bytes 786440 | tf_op jit(solution)/shard_map/ppermute | solution.py:321
  37.2 2.4 %factors.1 = (f32[128,2048]{1,0:T(8,128)S(1)}, f32[128,512]{1,0:T(8,128)S(1)}, f32[128,512]{1,0:T(8,128)S(1)}, f32[128,512]{1,0:T(8,128)S(1)}, f32[128,512]{1,0:T(8,128)S(1)}) custom-call(s32[1]{0:T(128)} %bitcast.at_ref, bf16[128,2048]{1,0:T(8,128)(2,1)S(1)} %copy-done.2, s32[2,128,2048]{2,1,0:T(8,128)S(1)} %copy-done.1, f32[1,2048]{1,0:T(1,128)S(1)} %bitcast.25, ...), custom_call_target="tpu_custom_call" | custom-call | tf_op jit(solution)/shard_map/factors/pallas_call | solution.py:149
  39.6 1.0 %copy-done.5 = f32[128,2048]{1,0:T(8,128)} copy-done((f32[128,2048]{1,0:T(8,128)}, f32[128,2048]{1,0:T(8,128)S(1)}, u32[]{:S(2)}) %copy-start.5) | copy-done | bytes 1048600
  40.6 0.7 copy-done.7
  41.3 0.7 copy-done.9
  42.0 0.7 copy-done.11
  43.8 2.1 %collective-permute-done.6.refs_7_ = bf16[128,1024]{1,0:T(8,128)(2,1)} collective-permute-done((bf16[128,1024]{1,0:T(8,128)(2,1)}, bf16[128,1024]{1,0:T(8,128)(2,1)}, u32[]{:S(2)}, u32[]{:S(2)}) %collective-permute-start.6) | collective-permute-done | bytes 262176 | tf_op jit(solution)/shard_map/ppermute | solution.py:321
  45.9 0.9 %copy-done.17 = bf16[128,1024]{1,0:T(8,128)(2,1)S(1)} copy-done((bf16[128,1024]{1,0:T(8,128)(2,1)S(1)}, bf16[128,1024]{1,0:T(8,128)(2,1)}, u32[]{:S(2)}) %copy-start.17) | copy-done | bytes 262168
  46.9 11.5 %attention.1.refs_4_ = bf16[4,1024,256]{2,1,0:T(8,128)(2,1)S(1)} custom-call(bf16[128,1024]{1,0:T(8,128)(2,1)} %get-tuple-element.24.refs_0_, bf16[128,1024]{1,0:T(8,128)(2,1)S(1)} %copy-done.17, bf16[128,1024]{1,0:T(8,128)(2,1)} %collective-permute-done.1.refs_2_, bf16[128,1024]{1,0:T(8,128)(2,1)} %collective-permute-done.2.refs_3_, ...), custom_call_target="tpu_custom_call" | custom-call | tf_op jit(solution)/shard_map/attention/pallas_call | solution.py:215
  58.5 1.4 %spread.1 = (f32[264,512]{1,0:T(8,128)S(1)}, f32[264,512]{1,0:T(8,128)S(1)}, f32[2,264,512]{2,1,0:T(8,128)S(1)}) custom-call(s32[1]{0:T(128)} %bitcast.at_ref, bf16[4,128,256]{2,1,0:T(8,128)(2,1)S(1)} %slice.62.grad_ref, bf16[3,2048,256]{2,1,0:T(8,128)(2,1)S(1)} %bitcast.23, bf16[256,2048]{1,0:T(8,128)(2,1)S(1)} %copy-done.3, ...), custom_call_target="tpu_custom_call" | custom-call | tf_op jit(solution)/shard_map/spread/pallas_call | solution.py:305
  60.6 2.1 %collective-permute-done.8 = f32[2,264,512]{2,1,0:T(8,128)S(1)} collective-permute-done((f32[2,264,512]{2,1,0:T(8,128)S(1)}, f32[2,264,512]{2,1,0:T(8,128)S(1)}, u32[]{:S(2)}, u32[]{:S(2)}) %collective-permute-start.8) | collective-permute-done | bytes 1081376 | tf_op jit(solution)/shard_map/ppermute | solution.py:321
  63.0 1.6 %collective-permute-start.10 = (f32[8,512]{1,0:T(8,128)S(1)}, f32[8,512]{1,0:T(8,128)S(1)}, u32[]{:S(2)}, u32[]{:S(2)}) collective-permute-start(f32[8,512]{1,0:T(8,128)S(1)} %slice.72), channel_id=1, source_target_pairs={{0,2},{1,3},{2,0},{3,1},{4,6},{5,7},{6,4},{7,5},{8,10},{9,11},{10,... | collective-permute-start | bytes 49160 | tf_op jit(solution)/shard_map/ppermute | solution.py:321
  64.8 1.7 %collective-permute-start.12 = (f32[512]{0:T(512)S(1)}, f32[512]{0:T(512)S(1)}, u32[]{:S(2)}, u32[]{:S(2)}) collective-permute-start(f32[512]{0:T(512)S(1)} %bitcast.30), channel_id=1, source_target_pairs={{0,6},{1,7},{2,4},{3,5},{4,2},{5,3},{6,0},{7,1},{8,14},{9,15},{10,... | collective-permute-start | bytes 6152 | tf_op jit(solution)/shard_map/ppermute | solution.py:413
  66.8 1.5 %collective-permute-start.9 = (bf16[256,512]{1,0:T(8,128)(2,1)S(1)}, bf16[256,512]{1,0:T(8,128)(2,1)S(1)}, u32[]{:S(2)}, u32[]{:S(2)}) collective-permute-start(bf16[256,512]{1,0:T(8,128)(2,1)S(1)} %pad_maximum_fusion), channel_id=1, source_target_pairs={{0,2},{1,3},{2,0},{3,1},{4,6},{5,7},{6,4},{7,5},{8,10},{9,11},{10,... | collective-permute-start | bytes 786440 | tf_op jit(solution)/shard_map/ppermute | solution.py:321
  68.3 1.0 %collective-permute-done.12 = f32[512]{0:T(512)S(1)} collective-permute-done((f32[512]{0:T(512)S(1)}, f32[512]{0:T(512)S(1)}, u32[]{:S(2)}, u32[]{:S(2)}) %collective-permute-start.12) | collective-permute-done | bytes 2080 | tf_op jit(solution)/shard_map/ppermute | solution.py:413
  69.3 2.5 %collective-permute-start.14 = (f32[512]{0:T(512)S(1)}, f32[512]{0:T(512)S(1)}, u32[]{:S(2)}, u32[]{:S(2)}) collective-permute-start(f32[512]{0:T(512)S(1)} %add_add_fusion.1), channel_id=1, source_target_pairs={{0,16},{4,20},{8,24},{12,28},{16,0},{20,4},{24,8},{28,12},{1,17},{... | collective-permute-start | bytes 6152 | tf_op jit(solution)/shard_map/ppermute | solution.py:321
  72.5 1.3 %collective-permute-start.15 = (f32[512]{0:T(512)S(1)}, f32[512]{0:T(512)S(1)}, u32[]{:S(2)}, u32[]{:S(2)}) collective-permute-start(f32[512]{0:T(512)S(1)} %add_add_fusion.1), channel_id=1, source_target_pairs={{0,24},{4,28},{8,16},{12,20},{16,8},{20,12},{24,0},{28,4},{1,25},{... | collective-permute-start | bytes 6152 | tf_op jit(solution)/shard_map/ppermute | solution.py:321
  73.8 2.7 %weight_grads.1 = (f32[3,256,256]{2,1,0:T(8,128)}, f32[256,256]{1,0:T(8,128)}) custom-call(s32[2]{0:T(128)S(1)} %pad_add_fusion.at_ref, bf16[8,32,512]{2,1,0:T(8,128)(2,1)S(1)} %all-to-all-done.refs_0_, bf16[8,32,512]{2,1,0:T(8,128)(2,1)S(1)} %collective-permute-done.16.refs_1_, bf16[8,32,512]{2,1,0:T(8,128)(2,1)} %collective-permute-done.7.refs_2_, ...), custom_call_target="tpu_custom_call" | custom-call | tf_op jit(solution)/shard_map/weight_grads/pallas_call | solution.py:342
  76.6 0.9 %fusion.4 = (f32[128,512]{1,0:T(8,128)}, bf16[128,512]{1,0:T(8,128)(2,1)}) fusion(f32[128,512]{1,0:T(8,128)S(1)} %copy-done.12, f32[128,512]{1,0:T(8,128)S(1)} %copy-done.8, f32[264,512]{1,0:T(8,128)S(1)} %get-tuple-element.41, f32[128,512]{1,0:T(8,128)S(1)} %copy-done.10, bf16[256,512]{1,0:T(8,128)(2,1)S(1)} %collective-permute-done.9, ...), kind=kLoop, calls=%fused_computation.7 | loop fusion | flops 655360 | bytes 2228736 | tf_op jit(solution)/shard_map/add | solution.py:421
  (75 shorter events, 5.3 us)
Async XLA Ops:
  0.6 22.0 %copy-start.19 = (s32[1024]{0:T(1024)S(1)}, s32[1024]{0:T(1024)}, u32[]{:S(2)}) copy-start(s32[1024]{0:T(1024)} %param.8) | copy-start | bytes 12292
  0.6 36.5 %copy-start.1 = (s32[2,128,2048]{2,1,0:T(8,128)S(1)}, s32[2,128,2048]{2,1,0:T(8,128)}, u32[]{:S(2)}) copy-start(s32[2,128,2048]{2,1,0:T(8,128)} %pulse_ref.1) | copy-start | bytes 6291460
  0.7 36.5 %copy-start.2 = (bf16[128,2048]{1,0:T(8,128)(2,1)S(1)}, bf16[128,2048]{1,0:T(8,128)(2,1)}, u32[]{:S(2)}) copy-start(bf16[128,2048]{1,0:T(8,128)(2,1)} %tok_ref.3) | copy-start | bytes 1572868
  0.7 36.5 %copy-start.4 = (bf16[128,2048]{1,0:T(8,128)(2,1)S(1)}, bf16[128,2048]{1,0:T(8,128)(2,1)}, u32[]{:S(2)}) copy-start(bf16[128,2048]{1,0:T(8,128)(2,1)} %up_ref.1) | copy-start | bytes 1572868
  0.7 36.5 %copy-start.18 = (f32[2048]{0:T(1024)S(1)}, f32[2048]{0:T(1024)}, u32[]{:S(2)}) copy-start(f32[2048]{0:T(1024)} %param.10) | copy-start | bytes 24580
  6.4 9.5 %collective-permute-start = (bf16[128,1024]{1,0:T(8,128)(2,1)}, bf16[128,1024]{1,0:T(8,128)(2,1)S(1)}, u32[]{:S(2)}, u32[]{:S(2)}) collective-permute-start(bf16[128,1024]{1,0:T(8,128)(2,1)} %get-tuple-element.24.refs_0_), channel_id=1, source_target_pairs={{0,4},{4,0},{8,12},{12,8},{16,20},{20,16},{24,28},{28,24},{1,5},{5... | collective-permute-start | bytes 786440 | tf_op jit(solution)/shard_map/ppermute | solution.py:321
  9.3 14.7 %collective-permute-start.3 = (bf16[128,1024]{1,0:T(8,128)(2,1)}, bf16[128,1024]{1,0:T(8,128)(2,1)}, u32[]{:S(2)}, u32[]{:S(2)}) collective-permute-start(bf16[128,1024]{1,0:T(8,128)(2,1)} %get-tuple-element.24.refs_0_), channel_id=1, source_target_pairs={{0,16},{4,20},{8,24},{12,28},{16,0},{20,4},{24,8},{28,12},{1,17},{... | collective-permute-start | bytes 786440 | tf_op jit(solution)/shard_map/ppermute | solution.py:321
  11.9 14.6 %collective-permute-start.1 = (bf16[128,1024]{1,0:T(8,128)(2,1)}, bf16[128,1024]{1,0:T(8,128)(2,1)}, u32[]{:S(2)}, u32[]{:S(2)}) collective-permute-start(bf16[128,1024]{1,0:T(8,128)(2,1)} %get-tuple-element.24.refs_0_), channel_id=1, source_target_pairs={{0,8},{4,12},{8,0},{12,4},{16,24},{20,28},{24,16},{28,20},{1,9},{5... | collective-permute-start | bytes 786440 | tf_op jit(solution)/shard_map/ppermute | solution.py:321
  16.5 19.0 %all-to-all-start = ((bf16[8,32,512]{2,1,0:T(8,128)(2,1)}), bf16[8,32,512]{2,1,0:T(8,128)(2,1)S(1)}, u32[]{:S(2)}, u32[]{:S(2)}) async-start(bf16[8,32,512]{2,1,0:T(8,128)(2,1)} %copy-done.15), calls=%async_computation | async-start | bytes 524288 | tf_op jit(solution)/shard_map/all_to_all | solution.py:385
  24.0 11.0 %collective-permute-start.5 = (bf16[128,1024]{1,0:T(8,128)(2,1)}, bf16[128,1024]{1,0:T(8,128)(2,1)}, u32[]{:S(2)}, u32[]{:S(2)}) collective-permute-start(bf16[128,1024]{1,0:T(8,128)(2,1)} %collective-permute-done.3.refs_4_), channel_id=1, source_target_pairs={{0,8},{4,12},{8,0},{12,4},{16,24},{20,28},{24,16},{28,20},{1,9},{5... | collective-permute-start | bytes 786440 | tf_op jit(solution)/shard_map/ppermute | solution.py:321
  25.5 18.3 %collective-permute-start.4 = (bf16[128,1024]{1,0:T(8,128)(2,1)}, bf16[128,1024]{1,0:T(8,128)(2,1)}, u32[]{:S(2)}, u32[]{:S(2)}) collective-permute-start(bf16[128,1024]{1,0:T(8,128)(2,1)} %collective-permute-done.3.refs_4_), channel_id=1, source_target_pairs={{0,4},{4,0},{8,12},{12,8},{16,20},{20,16},{24,28},{28,24},{1,5},{5... | collective-permute-start | bytes 786440 | tf_op jit(solution)/shard_map/ppermute | solution.py:321
  26.5 17.3 %collective-permute-start.2 = (bf16[128,1024]{1,0:T(8,128)(2,1)}, bf16[128,1024]{1,0:T(8,128)(2,1)}, u32[]{:S(2)}, u32[]{:S(2)}) collective-permute-start(bf16[128,1024]{1,0:T(8,128)(2,1)} %collective-permute-done.1.refs_2_), channel_id=1, source_target_pairs={{0,4},{4,0},{8,12},{12,8},{16,20},{20,16},{24,28},{28,24},{1,5},{5... | collective-permute-start | bytes 786440 | tf_op jit(solution)/shard_map/ppermute | solution.py:321
  35.0 10.9 %collective-permute-start.6 = (bf16[128,1024]{1,0:T(8,128)(2,1)}, bf16[128,1024]{1,0:T(8,128)(2,1)}, u32[]{:S(2)}, u32[]{:S(2)}) collective-permute-start(bf16[128,1024]{1,0:T(8,128)(2,1)} %collective-permute-done.5.refs_6_), channel_id=1, source_target_pairs={{0,4},{4,0},{8,12},{12,8},{16,20},{20,16},{24,28},{28,24},{1,5},{5... | collective-permute-start | bytes 786440 | tf_op jit(solution)/shard_map/ppermute | solution.py:321
  35.6 8.0 %collective-permute-start.7 = (bf16[8,32,512]{2,1,0:T(8,128)(2,1)S(1)}, bf16[8,32,512]{2,1,0:T(8,128)(2,1)}, u32[]{:S(2)}, u32[]{:S(2)}) collective-permute-start(bf16[8,32,512]{2,1,0:T(8,128)(2,1)S(1)} %all-to-all-done.refs_0_), channel_id=1, source_target_pairs={{0,2},{1,3},{2,0},{3,1},{4,6},{5,7},{6,4},{7,5},{8,10},{9,11},{10,... | collective-permute-start | bytes 786440 | tf_op jit(solution)/shard_map/ppermute | solution.py:321
  39.6 1.0 %copy-start.5 = (f32[128,2048]{1,0:T(8,128)}, f32[128,2048]{1,0:T(8,128)S(1)}, u32[]{:S(2)}) copy-start(f32[128,2048]{1,0:T(8,128)S(1)} %get-tuple-element.28.factor_ref) | copy-start | bytes 3145732
  46.9 11.6 %copy-start = (bf16[2048,3,256]{2,0,1:T(8,128)(2,1)S(1)}, bf16[2048,3,256]{2,0,1:T(8,128)(2,1)}, u32[]{:S(2)}) copy-start(bf16[2048,3,256]{2,0,1:T(8,128)(2,1)} %param.11) | copy-start | bytes 9437188
  46.9 11.6 %copy-start.3 = (bf16[256,2048]{1,0:T(8,128)(2,1)S(1)}, bf16[256,2048]{1,0:T(8,128)(2,1)}, u32[]{:S(2)}) copy-start(bf16[256,2048]{1,0:T(8,128)(2,1)} %wout_ref.1) | copy-start | bytes 3145732
  46.9 11.6 %copy-start.6 = (f32[128,2048]{1,0:T(8,128)S(1)}, f32[128,2048]{1,0:T(8,128)}, u32[]{:S(2)}) copy-start(f32[128,2048]{1,0:T(8,128)} %copy-done.5) | copy-start | bytes 3145732
  59.9 2.7 %collective-permute-start.8 = (f32[2,264,512]{2,1,0:T(8,128)S(1)}, f32[2,264,512]{2,1,0:T(8,128)S(1)}, u32[]{:S(2)}, u32[]{:S(2)}) collective-permute-start(f32[2,264,512]{2,1,0:T(8,128)S(1)} %get-tuple-element.30), channel_id=1, source_target_pairs={{0,1},{1,0},{2,3},{3,2},{4,5},{5,4},{6,7},{7,6},{8,9},{9,8},{10,11... | collective-permute-start | bytes 3244040 | tf_op jit(solution)/shard_map/ppermute | solution.py:321
  60.0 12.5 %collective-permute-start.16 = (bf16[8,32,512]{2,1,0:T(8,128)(2,1)S(1)}, bf16[8,32,512]{2,1,0:T(8,128)(2,1)S(1)}, u32[]{:S(2)}, u32[]{:S(2)}) collective-permute-start(bf16[8,32,512]{2,1,0:T(8,128)(2,1)S(1)} %all-to-all-done.refs_0_), channel_id=1, source_target_pairs={{0,1},{1,0},{2,3},{3,2},{4,5},{5,4},{6,7},{7,6},{8,9},{9,8},{10,11... | collective-permute-start | bytes 786440 | tf_op jit(solution)/shard_map/ppermute | solution.py:321
  60.5 13.3 %collective-permute-start.17 = (bf16[8,32,512]{2,1,0:T(8,128)(2,1)}, bf16[8,32,512]{2,1,0:T(8,128)(2,1)S(1)}, u32[]{:S(2)}, u32[]{:S(2)}) collective-permute-start(bf16[8,32,512]{2,1,0:T(8,128)(2,1)} %collective-permute-done.7.refs_2_), channel_id=1, source_target_pairs={{0,1},{1,0},{2,3},{3,2},{4,5},{5,4},{6,7},{7,6},{8,9},{9,8},{10,11... | collective-permute-start | bytes 786440 | tf_op jit(solution)/shard_map/ppermute | solution.py:321
  63.0 3.8 %collective-permute-start.10 = (f32[8,512]{1,0:T(8,128)S(1)}, f32[8,512]{1,0:T(8,128)S(1)}, u32[]{:S(2)}, u32[]{:S(2)}) collective-permute-start(f32[8,512]{1,0:T(8,128)S(1)} %slice.72), channel_id=1, source_target_pairs={{0,2},{1,3},{2,0},{3,1},{4,6},{5,7},{6,4},{7,5},{8,10},{9,11},{10,... | collective-permute-start | bytes 49160 | tf_op jit(solution)/shard_map/ppermute | solution.py:321
  64.5 3.7 %collective-permute-start.11 = (f32[512]{0:T(512)S(1)}, f32[512]{0:T(512)S(1)}, u32[]{:S(2)}, u32[]{:S(2)}) collective-permute-start(f32[512]{0:T(512)S(1)} %bitcast.31), channel_id=1, source_target_pairs={{0,4},{4,0},{8,12},{12,8},{16,20},{20,16},{24,28},{28,24},{1,5},{5... | collective-permute-start | bytes 6152 | tf_op jit(solution)/shard_map/ppermute | solution.py:321
  64.8 4.5 %collective-permute-start.12 = (f32[512]{0:T(512)S(1)}, f32[512]{0:T(512)S(1)}, u32[]{:S(2)}, u32[]{:S(2)}) collective-permute-start(f32[512]{0:T(512)S(1)} %bitcast.30), channel_id=1, source_target_pairs={{0,6},{1,7},{2,4},{3,5},{4,2},{5,3},{6,0},{7,1},{8,14},{9,15},{10,... | collective-permute-start | bytes 6152 | tf_op jit(solution)/shard_map/ppermute | solution.py:413
  66.5 10.0 %copy-start.8 = (f32[128,512]{1,0:T(8,128)S(1)}, f32[128,512]{1,0:T(8,128)}, u32[]{:S(2)}) copy-start(f32[128,512]{1,0:T(8,128)} %copy-done.7) | copy-start | bytes 786436
  66.5 10.0 %copy-start.10 = (f32[128,512]{1,0:T(8,128)S(1)}, f32[128,512]{1,0:T(8,128)}, u32[]{:S(2)}) copy-start(f32[128,512]{1,0:T(8,128)} %copy-done.9) | copy-start | bytes 786436
  66.5 10.0 %copy-start.12 = (f32[128,512]{1,0:T(8,128)S(1)}, f32[128,512]{1,0:T(8,128)}, u32[]{:S(2)}) copy-start(f32[128,512]{1,0:T(8,128)} %copy-done.11) | copy-start | bytes 786436
  66.5 10.0 %copy-start.14 = (f32[128,512]{1,0:T(8,128)S(1)}, f32[128,512]{1,0:T(8,128)}, u32[]{:S(2)}) copy-start(f32[128,512]{1,0:T(8,128)} %copy-done.13) | copy-start | bytes 786436
  66.8 9.7 %collective-permute-start.9 = (bf16[256,512]{1,0:T(8,128)(2,1)S(1)}, bf16[256,512]{1,0:T(8,128)(2,1)S(1)}, u32[]{:S(2)}, u32[]{:S(2)}) collective-permute-start(bf16[256,512]{1,0:T(8,128)(2,1)S(1)} %pad_maximum_fusion), channel_id=1, source_target_pairs={{0,2},{1,3},{2,0},{3,1},{4,6},{5,7},{6,4},{7,5},{8,10},{9,11},{10,... | collective-permute-start | bytes 786440 | tf_op jit(solution)/shard_map/ppermute | solution.py:321
  69.3 8.1 %collective-permute-start.14 = (f32[512]{0:T(512)S(1)}, f32[512]{0:T(512)S(1)}, u32[]{:S(2)}, u32[]{:S(2)}) collective-permute-start(f32[512]{0:T(512)S(1)} %add_add_fusion.1), channel_id=1, source_target_pairs={{0,16},{4,20},{8,24},{12,28},{16,0},{20,4},{24,8},{28,12},{1,17},{... | collective-permute-start | bytes 6152 | tf_op jit(solution)/shard_map/ppermute | solution.py:321
  71.8 5.6 %collective-permute-start.13 = (f32[512]{0:T(512)S(1)}, f32[512]{0:T(512)S(1)}, u32[]{:S(2)}, u32[]{:S(2)}) collective-permute-start(f32[512]{0:T(512)S(1)} %add_add_fusion.1), channel_id=1, source_target_pairs={{0,8},{4,12},{8,0},{12,4},{16,24},{20,28},{24,16},{28,20},{1,9},{5... | collective-permute-start | bytes 6152 | tf_op jit(solution)/shard_map/ppermute | solution.py:321
  72.5 5.4 %collective-permute-start.15 = (f32[512]{0:T(512)S(1)}, f32[512]{0:T(512)S(1)}, u32[]{:S(2)}, u32[]{:S(2)}) collective-permute-start(f32[512]{0:T(512)S(1)} %add_add_fusion.1), channel_id=1, source_target_pairs={{0,24},{4,28},{8,16},{12,20},{16,8},{20,12},{24,0},{28,4},{1,25},{... | collective-permute-start | bytes 6152 | tf_op jit(solution)/shard_map/ppermute | solution.py:321
  (7 other events, 5.2 us)

commit v5 on v4

--- a/solution.py
+++ b/solution.py
@@ -33,8 +33,8 @@
 
 
 def project_kernel(
-    at_ref, tok_hbm, pulse_hbm, gain_hbm, win_hbm, up_hbm, wout_hbm, pay_ref, spikes_ref, inv_ref, send_ref,
-    tok_ref, pulse_ref, gain_ref, win_ref, up_ref, wout_ref, acc_ref, sems, block_sems,
+    at_ref, tok_hbm, pulse_hbm, gain_hbm, win_hbm, up_hbm, wout_hbm, pay_ref, spikes_ref, inv_ref, send_hbm,
+    tok_ref, pulse_ref, gain_ref, win_ref, up_ref, wout_ref, acc_ref, ready_ref, sems, block_sems,
 ):
     model = tok_ref.shape[1]
     local = wout_ref.shape[0]
@@ -75,16 +75,19 @@
             share = dot(spikes, win_ref[part, here, :], NN)
             acc_ref[:, columns] = share if k == 0 else acc_ref[:, columns] + share
     pay_ref[:, : 3 * local] = acc_ref[...].astype(BF16)
-    for copy in whole[2:]:
-        copy.wait()
-    pay_ref[:, 3 * local :] = dot(up_ref[...], wout_ref[...], NT).astype(BF16)
-    ranks, quarter, both = send_ref.shape
+    whole[2].wait()
+    ranks, quarter, both = ready_ref.shape
     features = both // 2
     mine = pl.ds(pl.multiple_of(at_ref[0] * quarter, quarter), quarter)
     for rank in range(ranks):
         here = slice(rank * features, (rank + 1) * features)
-        send_ref[rank, :, :features] = spikes_ref[mine, here]
-        send_ref[rank, :, features:] = up_ref[mine, here]
+        ready_ref[rank, :, :features] = spikes_ref[mine, here]
+        ready_ref[rank, :, features:] = up_ref[mine, here]
+    leave = pltpu.make_async_copy(ready_ref, send_hbm, sems.at[4])
+    leave.start()
+    whole[3].wait()
+    pay_ref[:, 3 * local :] = dot(up_ref[...], wout_ref[...], NT).astype(BF16)
+    leave.wait()
 
 
 def project(fsdp_rank, ctx, tokens, pulse, gain, win, upstream, wout):
@@ -97,17 +100,18 @@
         project_kernel,
         in_specs=[pl.BlockSpec(memory_space=pltpu.SMEM)]
         + [pl.BlockSpec(memory_space=pltpu.HBM)] * 6,
-        out_specs=[in_vmem] * 4,
+        out_specs=[in_vmem] * 3 + [pl.BlockSpec(memory_space=pltpu.HBM)],
         out_shape=[
             jax.ShapeDtypeStruct((rows, 4 * local), BF16),
             jax.ShapeDtypeStruct((rows, model), BF16),
             jax.ShapeDtypeStruct((rows, 1), F32),
-            jax.ShapeDtypeStruct((ctx, rows // 4, 2 * (model // ctx)), BF16),
+            pltpu.HBM((ctx, rows // 4, 2 * (model // ctx)), BF16),
         ],
         scratch_shapes=[pltpu.VMEM(array.shape, array.dtype) for array in arrays]
         + [
             pltpu.VMEM((rows, 3 * local), F32),
-            pltpu.SemaphoreType.DMA((4,)),
+            pltpu.VMEM((ctx, rows // 4, 2 * (model // ctx)), BF16),
+            pltpu.SemaphoreType.DMA((5,)),
             pltpu.SemaphoreType.DMA((blocks, 2)),
         ],
         compiler_params=params(24),
@@ -119,7 +123,8 @@
 
 
 def factor_kernel(
-    at_ref, tok_ref, pulse_ref, gain_ref, inv_ref, up_ref, factor_ref, rise_ref, fall_ref, base_ref, own_ref
+    at_ref, tok_ref, pulse_ref, gain_ref, inv_ref, up_ref, factor_hbm, rise_hbm, fall_hbm, base_hbm, own_hbm,
+    factor_ref, rise_ref, fall_ref, base_ref, own_ref, sems,
 ):
     model = tok_ref.shape[1]
     width = own_ref.shape[1]
@@ -141,6 +146,14 @@
     base_ref[...] = up_ref[:, here].astype(F32)
     rise_ref[...] = factor_ref[:, here] * gain_ref[:, here] * inv
     fall_ref[...] = own * inv * (inv / model)
+    ends = [
+        (factor_ref, factor_hbm), (rise_ref, rise_hbm), (fall_ref, fall_hbm), (base_ref, base_hbm), (own_ref, own_hbm)
+    ]
+    copies = [pltpu.make_async_copy(*pair, sems.at[k]) for k, pair in enumerate(ends)]
+    for copy in copies:
+        copy.start()
+    for copy in copies:
+        copy.wait()
 
 
 def factors(fsdp_rank, tokens, pulse, gain, inv, upstream, share):
@@ -149,9 +162,11 @@
     return pl.pallas_call(
         factor_kernel,
         in_specs=[pl.BlockSpec(memory_space=pltpu.SMEM)] + [in_vmem] * 5,
-        out_specs=[in_vmem] * 5,
-        out_shape=[jax.ShapeDtypeStruct((rows, model), F32)]
-        + [jax.ShapeDtypeStruct((rows, share), F32)] * 4,
+        out_specs=[pl.BlockSpec(memory_space=pltpu.HBM)] * 5,
+        out_shape=[pltpu.HBM((rows, model), F32)] + [pltpu.HBM((rows, share), F32)] * 4,
+        scratch_shapes=[pltpu.VMEM((rows, model), F32)]
+        + [pltpu.VMEM((rows, share), F32)] * 4
+        + [pltpu.SemaphoreType.DMA((5,))],
         compiler_params=params(24),
         name="factors",
     )(fsdp_rank[None], tokens, pulse, gain, inv, upstream)
@@ -169,7 +184,7 @@
     low = prob.astype(BF16)
     grad_prob = dot(grad, values, NT)
     delta = jnp.sum(prob * grad_prob, axis=-1, keepdims=True)
-    score_grad = (prob * (grad_prob - delta) * ((1.0 - squashed * squashed) * scale)).astype(BF16)
+    score_grad = (prob * (grad_prob - delta) * (scale - (scale * squashed) * squashed)).astype(BF16)
     attended = dot(low, values, NN).astype(BF16)
     grad_query = dot(score_grad, keys, NN).astype(BF16)
     return attended, grad_query, dot(score_grad, query, TN), dot(low, grad, TN)
@@ -180,7 +195,7 @@
     rows = piece_refs[0].shape[0]
     length, width = all_ref.shape
     local = width // 4
-    block = length // 2
+    block = length
     for j, piece in enumerate(piece_refs):
         all_ref[j * rows : (j + 1) * rows, :] = piece[...]
     dk_ref[...] = jnp.zeros_like(dk_ref)
@@ -219,7 +234,7 @@
         out_shape=jax.ShapeDtypeStruct((4, length, local), BF16),
         scratch_shapes=[pltpu.VMEM((length, width), BF16)]
         + [pltpu.VMEM((length, local), F32)] * 2,
-        compiler_params=params(36),
+        compiler_params=params(44),
         name="attention",
     )(*pieces, positions[None, :], positions[:, None])
 
@@ -374,7 +389,7 @@
         beside = swap(payload, "ctx", 2)
         below = swap(payload, "ctx", 1)
         across = swap(payload, "ctx", 4)
-        diagonal = swap(beside, "ctx", 1)
+        diagonal = swap(below, "ctx", 2)
         corner = swap(across, "ctx", 2)
         across_below = swap(across, "ctx", 1)
         blocks = [payload, below, beside, diagonal, across, across_below]

time: 78.7 us -> 76.7 us (0.975)
  local copies, waits for them, and re-layouts: 7.15 us -> 2.6 us
  Pallas kernels: 23.1 us -> 24.4 us
  starting transfers between devices: 28.5 us -> 29.3 us
    unnamed x47 -> x35, local copies, waits for them, and re-layouts: 6.8 us -> 2.25 us
    pallas_call x1, Pallas kernels: 2.39 us -> 3.66 us  [factors(): pl.pallas_call(factor_kernel, in_specs=[pl.BlockSpec(memory_space=pltpu.S...]
    ppermute x17, starting transfers between devices: 20.7 us -> 21.7 us  [swap(): return lax.ppermute(value, axis, [(i, i ^ mask) for i in range(count)])]
  transfers between devices with their start and end apart: 19 -> 19, of which waited for: 8 -> 8; matrix products, arithmetic and copies ran while one was open for 3% -> 3% of each run, Pallas kernels for 7% -> 8%
where the time goes in v5:
time: 76.7 us; the launch traced here: 76.4 us
  starting transfers between devices  29.3 us (38%)
  Pallas kernels  24.4 us (32%)
  waiting for transfers between devices  17.4 us (23%)
  local copies, waits for them, and re-layouts  2.6 us (3%)
  other arithmetic  1.81 us (2%)
  between operations  0.92 us (1%)
    ppermute x17, starting transfers between devices, swap(): return lax.ppermute(value, axis, [(i, i ^ mask) for i in range(count)])  21.7 us
    ppermute x17, waiting for transfers between devices, swap(): return lax.ppermute(value, axis, [(i, i ^ mask) for i in range(count)])  16.2 us
    pallas_call x1, Pallas kernels, attention(): pl.pallas_call(attention_kernel, in_specs=[in_vmem] * (len(pieces) + 2),...  11.2 us
    all_to_all x1, starting transfers between devices, body(): both = lax.all_to_all(after(both, below), 'ctx', 0, 0)  6.06 us
    pallas_call x1, Pallas kernels, project(): pl.pallas_call(project_kernel, in_specs=[pl.BlockSpec(memory_space=pltpu....  5.26 us
    pallas_call x1, Pallas kernels, factors(): pl.pallas_call(factor_kernel, in_specs=[pl.BlockSpec(memory_space=pltpu.S...  3.66 us
    pallas_call x1, Pallas kernels, weight_grads(): pl.pallas_call(weight_kernel, in_specs=[pl.BlockSpec(memory_space=pltpu.S...  2.74 us
    unnamed x35, local copies, waits for them, and re-layouts  2.25 us
  transfers between devices with their start and end apart: 19, of which 8 were waited for; matrix products, arithmetic and copies ran while one was open for 3% of the time, Pallas kernels for 8%

profile of v5, /device:TPU:0, one launch (start us, length us, event | category | flops | bytes accessed | tf_op | source)
XLA Modules:
  0.0 76.4 jit_solution(8269423982867847868)
XLA Ops:
  0.7 5.3 %project.1 = (bf16[128,1024]{1,0:T(8,128)(2,1)}, bf16[128,2048]{1,0:T(8,128)(2,1)}, f32[128,1]{1,0:T(8,128)S(1)}, bf16[8,32,512]{2,1,0:T(8,128)(2,1)}) custom-call(s32[1]{0:T(128)} %bitcast.at_ref, bf16[128,2048]{1,0:T(8,128)(2,1)} %tok_ref.3, s32[2,128,2048]{2,1,0:T(8,128)} %pulse_ref.1, f32[1,2048]{1,0:T(1,128)} %bitcast.24, ...), custom_call_target="tpu_custom_call" | custom-call | tf_op jit(solution)/shard_map/project/pallas_call | solution.py:99
  6.0 3.0 %collective-permute-start = (bf16[128,1024]{1,0:T(8,128)(2,1)}, bf16[128,1024]{1,0:T(8,128)(2,1)S(1)}, u32[]{:S(2)}, u32[]{:S(2)}) collective-permute-start(bf16[128,1024]{1,0:T(8,128)(2,1)} %get-tuple-element.24.refs_0_), channel_id=1, source_target_pairs={{0,4},{4,0},{8,12},{12,8},{16,20},{20,16},{24,28},{28,24},{1,5},{5... | collective-permute-start | bytes 786440 | tf_op jit(solution)/shard_map/ppermute | solution.py:336
  9.0 2.6 %collective-permute-start.3 = (bf16[128,1024]{1,0:T(8,128)(2,1)}, bf16[128,1024]{1,0:T(8,128)(2,1)}, u32[]{:S(2)}, u32[]{:S(2)}) collective-permute-start(bf16[128,1024]{1,0:T(8,128)(2,1)} %get-tuple-element.24.refs_0_), channel_id=1, source_target_pairs={{0,16},{4,20},{8,24},{12,28},{16,0},{20,4},{24,8},{28,12},{1,17},{... | collective-permute-start | bytes 786440 | tf_op jit(solution)/shard_map/ppermute | solution.py:336
  11.6 1.6 %collective-permute-start.1 = (bf16[128,1024]{1,0:T(8,128)(2,1)}, bf16[128,1024]{1,0:T(8,128)(2,1)}, u32[]{:S(2)}, u32[]{:S(2)}) collective-permute-start(bf16[128,1024]{1,0:T(8,128)(2,1)} %get-tuple-element.24.refs_0_), channel_id=1, source_target_pairs={{0,8},{4,12},{8,0},{12,4},{16,24},{20,28},{24,16},{28,20},{1,9},{5... | collective-permute-start | bytes 786440 | tf_op jit(solution)/shard_map/ppermute | solution.py:336
  13.2 2.3 %collective-permute-done.refs_1_ = bf16[128,1024]{1,0:T(8,128)(2,1)S(1)} collective-permute-done((bf16[128,1024]{1,0:T(8,128)(2,1)}, bf16[128,1024]{1,0:T(8,128)(2,1)S(1)}, u32[]{:S(2)}, u32[]{:S(2)}) %collective-permute-start) | collective-permute-done | bytes 262176 | tf_op jit(solution)/shard_map/ppermute | solution.py:336
  15.5 0.7 copy-done.6
  16.2 6.1 %all-to-all-start = ((bf16[8,32,512]{2,1,0:T(8,128)(2,1)}), bf16[8,32,512]{2,1,0:T(8,128)(2,1)S(1)}, u32[]{:S(2)}, u32[]{:S(2)}) async-start(bf16[8,32,512]{2,1,0:T(8,128)(2,1)} %get-tuple-element.26), calls=%async_computation | async-start | bytes 524288 | tf_op jit(solution)/shard_map/all_to_all | solution.py:400
  22.4 1.3 %collective-permute-done.3.refs_4_ = bf16[128,1024]{1,0:T(8,128)(2,1)} collective-permute-done((bf16[128,1024]{1,0:T(8,128)(2,1)}, bf16[128,1024]{1,0:T(8,128)(2,1)}, u32[]{:S(2)}, u32[]{:S(2)}) %collective-permute-start.3) | collective-permute-done | bytes 262176 | tf_op jit(solution)/shard_map/ppermute | solution.py:336
  23.7 1.2 %collective-permute-start.5 = (bf16[128,1024]{1,0:T(8,128)(2,1)}, bf16[128,1024]{1,0:T(8,128)(2,1)}, u32[]{:S(2)}, u32[]{:S(2)}) collective-permute-start(bf16[128,1024]{1,0:T(8,128)(2,1)} %collective-permute-done.3.refs_4_), channel_id=1, source_target_pairs={{0,8},{4,12},{8,0},{12,4},{16,24},{20,28},{24,16},{28,20},{1,9},{5... | collective-permute-start | bytes 786440 | tf_op jit(solution)/shard_map/ppermute | solution.py:336
  25.1 0.9 %collective-permute-start.2 = (bf16[128,1024]{1,0:T(8,128)(2,1)}, bf16[128,1024]{1,0:T(8,128)(2,1)}, u32[]{:S(2)}, u32[]{:S(2)}) collective-permute-start(bf16[128,1024]{1,0:T(8,128)(2,1)} %copy-done.6), channel_id=1, source_target_pairs={{0,8},{4,12},{8,0},{12,4},{16,24},{20,28},{24,16},{28,20},{1,9},{5... | collective-permute-start | bytes 786440 | tf_op jit(solution)/shard_map/ppermute | solution.py:336
  26.0 0.7 collective-permute-start.4
  26.7 8.7 %collective-permute-done.5.refs_6_ = bf16[128,1024]{1,0:T(8,128)(2,1)} collective-permute-done((bf16[128,1024]{1,0:T(8,128)(2,1)}, bf16[128,1024]{1,0:T(8,128)(2,1)}, u32[]{:S(2)}, u32[]{:S(2)}) %collective-permute-start.5) | collective-permute-done | bytes 262176 | tf_op jit(solution)/shard_map/ppermute | solution.py:336
  35.4 1.7 %collective-permute-start.6 = (bf16[128,1024]{1,0:T(8,128)(2,1)}, bf16[128,1024]{1,0:T(8,128)(2,1)}, u32[]{:S(2)}, u32[]{:S(2)}) collective-permute-start(bf16[128,1024]{1,0:T(8,128)(2,1)} %collective-permute-done.5.refs_6_), channel_id=1, source_target_pairs={{0,4},{4,0},{8,12},{12,8},{16,20},{20,16},{24,28},{28,24},{1,5},{5... | collective-permute-start | bytes 786440 | tf_op jit(solution)/shard_map/ppermute | solution.py:336
  37.1 1.5 %collective-permute-start.7 = (bf16[8,32,512]{2,1,0:T(8,128)(2,1)S(1)}, bf16[8,32,512]{2,1,0:T(8,128)(2,1)}, u32[]{:S(2)}, u32[]{:S(2)}) collective-permute-start(bf16[8,32,512]{2,1,0:T(8,128)(2,1)S(1)} %all-to-all-done.refs_0_), channel_id=1, source_target_pairs={{0,2},{1,3},{2,0},{3,1},{4,6},{5,7},{6,4},{7,5},{8,10},{9,11},{10,... | collective-permute-start | bytes 786440 | tf_op jit(solution)/shard_map/ppermute | solution.py:336
  38.7 3.7 %factors.1 = (f32[128,2048]{1,0:T(8,128)}, f32[128,512]{1,0:T(8,128)}, f32[128,512]{1,0:T(8,128)}, f32[128,512]{1,0:T(8,128)}, f32[128,512]{1,0:T(8,128)}) custom-call(s32[1]{0:T(128)} %bitcast.at_ref, bf16[128,2048]{1,0:T(8,128)(2,1)S(1)} %copy-done.2, s32[2,128,2048]{2,1,0:T(8,128)S(1)} %copy-done.1, f32[1,2048]{1,0:T(1,128)S(1)} %bitcast.25, ...), custom_call_target="tpu_custom_call" | custom-call | tf_op jit(solution)/shard_map/factors/pallas_call | solution.py:162
  42.6 1.0 %collective-permute-done.7.refs_2_ = bf16[8,32,512]{2,1,0:T(8,128)(2,1)} collective-permute-done((bf16[8,32,512]{2,1,0:T(8,128)(2,1)S(1)}, bf16[8,32,512]{2,1,0:T(8,128)(2,1)}, u32[]{:S(2)}, u32[]{:S(2)}) %collective-permute-start.7) | collective-permute-done | bytes 262176 | tf_op jit(solution)/shard_map/ppermute | solution.py:336
  43.9 0.9 %copy-done.7 = bf16[128,1024]{1,0:T(8,128)(2,1)S(1)} copy-done((bf16[128,1024]{1,0:T(8,128)(2,1)S(1)}, bf16[128,1024]{1,0:T(8,128)(2,1)}, u32[]{:S(2)}) %copy-start.7) | copy-done | bytes 262168
  44.9 11.2 %attention.1.refs_4_ = bf16[4,1024,256]{2,1,0:T(8,128)(2,1)S(1)} custom-call(bf16[128,1024]{1,0:T(8,128)(2,1)} %get-tuple-element.24.refs_0_, bf16[128,1024]{1,0:T(8,128)(2,1)S(1)} %copy-done.7, bf16[128,1024]{1,0:T(8,128)(2,1)} %collective-permute-done.1.refs_2_, bf16[128,1024]{1,0:T(8,128)(2,1)} %collective-permute-done.2.refs_3_, ...), custom_call_target="tpu_custom_call" | custom-call | tf_op jit(solution)/shard_map/attention/pallas_call | solution.py:230
  56.2 1.5 %spread.1 = (f32[264,512]{1,0:T(8,128)S(1)}, f32[264,512]{1,0:T(8,128)S(1)}, f32[2,264,512]{2,1,0:T(8,128)S(1)}) custom-call(s32[1]{0:T(128)} %bitcast.at_ref, bf16[4,128,256]{2,1,0:T(8,128)(2,1)S(1)} %slice.62.grad_ref, bf16[3,2048,256]{2,1,0:T(8,128)(2,1)S(1)} %bitcast.23, bf16[256,2048]{1,0:T(8,128)(2,1)S(1)} %copy-done.3, ...), custom_call_target="tpu_custom_call" | custom-call | tf_op jit(solution)/shard_map/spread/pallas_call | solution.py:320
  57.7 0.5 collective-permute-start.16
  58.2 2.1 %collective-permute-done.8 = f32[2,264,512]{2,1,0:T(8,128)S(1)} collective-permute-done((f32[2,264,512]{2,1,0:T(8,128)S(1)}, f32[2,264,512]{2,1,0:T(8,128)S(1)}, u32[]{:S(2)}, u32[]{:S(2)}) %collective-permute-start.8) | collective-permute-done | bytes 1081376 | tf_op jit(solution)/shard_map/ppermute | solution.py:336
  60.6 1.6 %collective-permute-start.10 = (f32[8,512]{1,0:T(8,128)S(1)}, f32[8,512]{1,0:T(8,128)S(1)}, u32[]{:S(2)}, u32[]{:S(2)}) collective-permute-start(f32[8,512]{1,0:T(8,128)S(1)} %slice.72), channel_id=1, source_target_pairs={{0,2},{1,3},{2,0},{3,1},{4,6},{5,7},{6,4},{7,5},{8,10},{9,11},{10,... | collective-permute-start | bytes 49160 | tf_op jit(solution)/shard_map/ppermute | solution.py:336
  62.2 0.5 collective-permute-start.11
  62.7 1.5 %collective-permute-start.12 = (f32[512]{0:T(512)S(1)}, f32[512]{0:T(512)S(1)}, u32[]{:S(2)}, u32[]{:S(2)}) collective-permute-start(f32[512]{0:T(512)S(1)} %bitcast.30), channel_id=1, source_target_pairs={{0,6},{1,7},{2,4},{3,5},{4,2},{5,3},{6,0},{7,1},{8,14},{9,15},{10,... | collective-permute-start | bytes 6152 | tf_op jit(solution)/shard_map/ppermute | solution.py:428
  64.4 1.5 %collective-permute-start.9 = (bf16[256,512]{1,0:T(8,128)(2,1)S(1)}, bf16[256,512]{1,0:T(8,128)(2,1)S(1)}, u32[]{:S(2)}, u32[]{:S(2)}) collective-permute-start(bf16[256,512]{1,0:T(8,128)(2,1)S(1)} %pad_maximum_fusion), channel_id=1, source_target_pairs={{0,2},{1,3},{2,0},{3,1},{4,6},{5,7},{6,4},{7,5},{8,10},{9,11},{10,... | collective-permute-start | bytes 786440 | tf_op jit(solution)/shard_map/ppermute | solution.py:336
  65.9 1.2 %collective-permute-done.12 = f32[512]{0:T(512)S(1)} collective-permute-done((f32[512]{0:T(512)S(1)}, f32[512]{0:T(512)S(1)}, u32[]{:S(2)}, u32[]{:S(2)}) %collective-permute-start.12) | collective-permute-done | bytes 2080 | tf_op jit(solution)/shard_map/ppermute | solution.py:428
  67.2 2.3 %collective-permute-start.14 = (f32[512]{0:T(512)S(1)}, f32[512]{0:T(512)S(1)}, u32[]{:S(2)}, u32[]{:S(2)}) collective-permute-start(f32[512]{0:T(512)S(1)} %add_add_fusion.1), channel_id=1, source_target_pairs={{0,16},{4,20},{8,24},{12,28},{16,0},{20,4},{24,8},{28,12},{1,17},{... | collective-permute-start | bytes 6152 | tf_op jit(solution)/shard_map/ppermute | solution.py:336
  69.5 0.9 %collective-permute-start.13 = (f32[512]{0:T(512)S(1)}, f32[512]{0:T(512)S(1)}, u32[]{:S(2)}, u32[]{:S(2)}) collective-permute-start(f32[512]{0:T(512)S(1)} %add_add_fusion.1), channel_id=1, source_target_pairs={{0,8},{4,12},{8,0},{12,4},{16,24},{20,28},{24,16},{28,20},{1,9},{5... | collective-permute-start | bytes 6152 | tf_op jit(solution)/shard_map/ppermute | solution.py:336
  70.4 1.2 %collective-permute-start.15 = (f32[512]{0:T(512)S(1)}, f32[512]{0:T(512)S(1)}, u32[]{:S(2)}, u32[]{:S(2)}) collective-permute-start(f32[512]{0:T(512)S(1)} %add_add_fusion.1), channel_id=1, source_target_pairs={{0,24},{4,28},{8,16},{12,20},{16,8},{20,12},{24,0},{28,4},{1,25},{... | collective-permute-start | bytes 6152 | tf_op jit(solution)/shard_map/ppermute | solution.py:336
  71.7 2.7 %weight_grads.1 = (f32[3,256,256]{2,1,0:T(8,128)}, f32[256,256]{1,0:T(8,128)}) custom-call(s32[2]{0:T(128)S(1)} %pad_add_fusion.at_ref, bf16[8,32,512]{2,1,0:T(8,128)(2,1)S(1)} %all-to-all-done.refs_0_, bf16[8,32,512]{2,1,0:T(8,128)(2,1)S(1)} %collective-permute-done.16.refs_1_, bf16[8,32,512]{2,1,0:T(8,128)(2,1)} %collective-permute-done.7.refs_2_, ...), custom_call_target="tpu_custom_call" | custom-call | tf_op jit(solution)/shard_map/weight_grads/pallas_call | solution.py:357
  74.4 0.9 %fusion.4 = (f32[128,512]{1,0:T(8,128)}, bf16[128,512]{1,0:T(8,128)(2,1)}) fusion(f32[128,512]{1,0:T(8,128)S(1)} %copy-done.11, f32[128,512]{1,0:T(8,128)S(1)} %copy-done.9, f32[264,512]{1,0:T(8,128)S(1)} %get-tuple-element.41, f32[128,512]{1,0:T(8,128)S(1)} %copy-done.10, bf16[256,512]{1,0:T(8,128)(2,1)S(1)} %collective-permute-done.9, ...), kind=kLoop, calls=%fused_computation.7 | loop fusion | flops 655360 | bytes 2228736 | tf_op jit(solution)/shard_map/add | solution.py:436
  75.8 0.6 add_add_fusion
  (63 shorter events, 2.1 us)
Async XLA Ops:
  0.6 21.6 %copy-start.13 = (s32[1024]{0:T(1024)S(1)}, s32[1024]{0:T(1024)}, u32[]{:S(2)}) copy-start(s32[1024]{0:T(1024)} %param.8) | copy-start | bytes 12292
  0.6 38.1 %copy-start.1 = (s32[2,128,2048]{2,1,0:T(8,128)S(1)}, s32[2,128,2048]{2,1,0:T(8,128)}, u32[]{:S(2)}) copy-start(s32[2,128,2048]{2,1,0:T(8,128)} %pulse_ref.1) | copy-start | bytes 6291460
  0.7 38.1 %copy-start.2 = (bf16[128,2048]{1,0:T(8,128)(2,1)S(1)}, bf16[128,2048]{1,0:T(8,128)(2,1)}, u32[]{:S(2)}) copy-start(bf16[128,2048]{1,0:T(8,128)(2,1)} %tok_ref.3) | copy-start | bytes 1572868
  0.7 38.1 %copy-start.4 = (bf16[128,2048]{1,0:T(8,128)(2,1)S(1)}, bf16[128,2048]{1,0:T(8,128)(2,1)}, u32[]{:S(2)}) copy-start(bf16[128,2048]{1,0:T(8,128)(2,1)} %up_ref.1) | copy-start | bytes 1572868
  0.7 38.0 %copy-start.8 = (f32[2048]{0:T(1024)S(1)}, f32[2048]{0:T(1024)}, u32[]{:S(2)}) copy-start(f32[2048]{0:T(1024)} %param.10) | copy-start | bytes 24580
  6.0 9.6 %collective-permute-start = (bf16[128,1024]{1,0:T(8,128)(2,1)}, bf16[128,1024]{1,0:T(8,128)(2,1)S(1)}, u32[]{:S(2)}, u32[]{:S(2)}) collective-permute-start(bf16[128,1024]{1,0:T(8,128)(2,1)} %get-tuple-element.24.refs_0_), channel_id=1, source_target_pairs={{0,4},{4,0},{8,12},{12,8},{16,20},{20,16},{24,28},{28,24},{1,5},{5... | collective-permute-start | bytes 786440 | tf_op jit(solution)/shard_map/ppermute | solution.py:336
  9.0 14.7 %collective-permute-start.3 = (bf16[128,1024]{1,0:T(8,128)(2,1)}, bf16[128,1024]{1,0:T(8,128)(2,1)}, u32[]{:S(2)}, u32[]{:S(2)}) collective-permute-start(bf16[128,1024]{1,0:T(8,128)(2,1)} %get-tuple-element.24.refs_0_), channel_id=1, source_target_pairs={{0,16},{4,20},{8,24},{12,28},{16,0},{20,4},{24,8},{28,12},{1,17},{... | collective-permute-start | bytes 786440 | tf_op jit(solution)/shard_map/ppermute | solution.py:336
  11.6 32.3 %collective-permute-start.1 = (bf16[128,1024]{1,0:T(8,128)(2,1)}, bf16[128,1024]{1,0:T(8,128)(2,1)}, u32[]{:S(2)}, u32[]{:S(2)}) collective-permute-start(bf16[128,1024]{1,0:T(8,128)(2,1)} %get-tuple-element.24.refs_0_), channel_id=1, source_target_pairs={{0,8},{4,12},{8,0},{12,4},{16,24},{20,28},{24,16},{28,20},{1,9},{5... | collective-permute-start | bytes 786440 | tf_op jit(solution)/shard_map/ppermute | solution.py:336
  16.2 20.9 %all-to-all-start = ((bf16[8,32,512]{2,1,0:T(8,128)(2,1)}), bf16[8,32,512]{2,1,0:T(8,128)(2,1)S(1)}, u32[]{:S(2)}, u32[]{:S(2)}) async-start(bf16[8,32,512]{2,1,0:T(8,128)(2,1)} %get-tuple-element.26), calls=%async_computation | async-start | bytes 524288 | tf_op jit(solution)/shard_map/all_to_all | solution.py:400
  23.7 11.7 %collective-permute-start.5 = (bf16[128,1024]{1,0:T(8,128)(2,1)}, bf16[128,1024]{1,0:T(8,128)(2,1)}, u32[]{:S(2)}, u32[]{:S(2)}) collective-permute-start(bf16[128,1024]{1,0:T(8,128)(2,1)} %collective-permute-done.3.refs_4_), channel_id=1, source_target_pairs={{0,8},{4,12},{8,0},{12,4},{16,24},{20,28},{24,16},{28,20},{1,9},{5... | collective-permute-start | bytes 786440 | tf_op jit(solution)/shard_map/ppermute | solution.py:336
  25.1 18.7 %collective-permute-start.2 = (bf16[128,1024]{1,0:T(8,128)(2,1)}, bf16[128,1024]{1,0:T(8,128)(2,1)}, u32[]{:S(2)}, u32[]{:S(2)}) collective-permute-start(bf16[128,1024]{1,0:T(8,128)(2,1)} %copy-done.6), channel_id=1, source_target_pairs={{0,8},{4,12},{8,0},{12,4},{16,24},{20,28},{24,16},{28,20},{1,9},{5... | collective-permute-start | bytes 786440 | tf_op jit(solution)/shard_map/ppermute | solution.py:336
  26.0 17.9 %collective-permute-start.4 = (bf16[128,1024]{1,0:T(8,128)(2,1)}, bf16[128,1024]{1,0:T(8,128)(2,1)}, u32[]{:S(2)}, u32[]{:S(2)}) collective-permute-start(bf16[128,1024]{1,0:T(8,128)(2,1)} %collective-permute-done.3.refs_4_), channel_id=1, source_target_pairs={{0,4},{4,0},{8,12},{12,8},{16,20},{20,16},{24,28},{28,24},{1,5},{5... | collective-permute-start | bytes 786440 | tf_op jit(solution)/shard_map/ppermute | solution.py:336
  35.4 8.5 %collective-permute-start.6 = (bf16[128,1024]{1,0:T(8,128)(2,1)}, bf16[128,1024]{1,0:T(8,128)(2,1)}, u32[]{:S(2)}, u32[]{:S(2)}) collective-permute-start(bf16[128,1024]{1,0:T(8,128)(2,1)} %collective-permute-done.5.refs_6_), channel_id=1, source_target_pairs={{0,4},{4,0},{8,12},{12,8},{16,20},{20,16},{24,28},{28,24},{1,5},{5... | collective-permute-start | bytes 786440 | tf_op jit(solution)/shard_map/ppermute | solution.py:336
  37.1 6.5 %collective-permute-start.7 = (bf16[8,32,512]{2,1,0:T(8,128)(2,1)S(1)}, bf16[8,32,512]{2,1,0:T(8,128)(2,1)}, u32[]{:S(2)}, u32[]{:S(2)}) collective-permute-start(bf16[8,32,512]{2,1,0:T(8,128)(2,1)S(1)} %all-to-all-done.refs_0_), channel_id=1, source_target_pairs={{0,2},{1,3},{2,0},{3,1},{4,6},{5,7},{6,4},{7,5},{8,10},{9,11},{10,... | collective-permute-start | bytes 786440 | tf_op jit(solution)/shard_map/ppermute | solution.py:336
  43.9 1.0 %copy-start.7 = (bf16[128,1024]{1,0:T(8,128)(2,1)S(1)}, bf16[128,1024]{1,0:T(8,128)(2,1)}, u32[]{:S(2)}) copy-start(bf16[128,1024]{1,0:T(8,128)(2,1)} %copy-done.6) | copy-start | bytes 786436
  44.8 11.3 %copy-start = (bf16[2048,3,256]{2,0,1:T(8,128)(2,1)S(1)}, bf16[2048,3,256]{2,0,1:T(8,128)(2,1)}, u32[]{:S(2)}) copy-start(bf16[2048,3,256]{2,0,1:T(8,128)(2,1)} %param.11) | copy-start | bytes 9437188
  44.9 11.3 %copy-start.3 = (bf16[256,2048]{1,0:T(8,128)(2,1)S(1)}, bf16[256,2048]{1,0:T(8,128)(2,1)}, u32[]{:S(2)}) copy-start(bf16[256,2048]{1,0:T(8,128)(2,1)} %wout_ref.1) | copy-start | bytes 3145732
  44.9 11.3 %copy-start.5 = (f32[128,2048]{1,0:T(8,128)S(1)}, f32[128,2048]{1,0:T(8,128)}, u32[]{:S(2)}) copy-start(f32[128,2048]{1,0:T(8,128)} %get-tuple-element.28.factor_ref) | copy-start | bytes 3145732
  57.6 2.7 %collective-permute-start.8 = (f32[2,264,512]{2,1,0:T(8,128)S(1)}, f32[2,264,512]{2,1,0:T(8,128)S(1)}, u32[]{:S(2)}, u32[]{:S(2)}) collective-permute-start(f32[2,264,512]{2,1,0:T(8,128)S(1)} %get-tuple-element.30), channel_id=1, source_target_pairs={{0,1},{1,0},{2,3},{3,2},{4,5},{5,4},{6,7},{7,6},{8,9},{9,8},{10,11... | collective-permute-start | bytes 3244040 | tf_op jit(solution)/shard_map/ppermute | solution.py:336
  57.7 12.8 %collective-permute-start.16 = (bf16[8,32,512]{2,1,0:T(8,128)(2,1)S(1)}, bf16[8,32,512]{2,1,0:T(8,128)(2,1)S(1)}, u32[]{:S(2)}, u32[]{:S(2)}) collective-permute-start(bf16[8,32,512]{2,1,0:T(8,128)(2,1)S(1)} %all-to-all-done.refs_0_), channel_id=1, source_target_pairs={{0,1},{1,0},{2,3},{3,2},{4,5},{5,4},{6,7},{7,6},{8,9},{9,8},{10,11... | collective-permute-start | bytes 786440 | tf_op jit(solution)/shard_map/ppermute | solution.py:336
  58.2 13.5 %collective-permute-start.17 = (bf16[8,32,512]{2,1,0:T(8,128)(2,1)}, bf16[8,32,512]{2,1,0:T(8,128)(2,1)S(1)}, u32[]{:S(2)}, u32[]{:S(2)}) collective-permute-start(bf16[8,32,512]{2,1,0:T(8,128)(2,1)} %collective-permute-done.7.refs_2_), channel_id=1, source_target_pairs={{0,1},{1,0},{2,3},{3,2},{4,5},{5,4},{6,7},{7,6},{8,9},{9,8},{10,11... | collective-permute-start | bytes 786440 | tf_op jit(solution)/shard_map/ppermute | solution.py:336
  60.6 3.8 %collective-permute-start.10 = (f32[8,512]{1,0:T(8,128)S(1)}, f32[8,512]{1,0:T(8,128)S(1)}, u32[]{:S(2)}, u32[]{:S(2)}) collective-permute-start(f32[8,512]{1,0:T(8,128)S(1)} %slice.72), channel_id=1, source_target_pairs={{0,2},{1,3},{2,0},{3,1},{4,6},{5,7},{6,4},{7,5},{8,10},{9,11},{10,... | collective-permute-start | bytes 49160 | tf_op jit(solution)/shard_map/ppermute | solution.py:336
  62.2 3.7 %collective-permute-start.11 = (f32[512]{0:T(512)S(1)}, f32[512]{0:T(512)S(1)}, u32[]{:S(2)}, u32[]{:S(2)}) collective-permute-start(f32[512]{0:T(512)S(1)} %bitcast.31), channel_id=1, source_target_pairs={{0,4},{4,0},{8,12},{12,8},{16,20},{20,16},{24,28},{28,24},{1,5},{5... | collective-permute-start | bytes 6152 | tf_op jit(solution)/shard_map/ppermute | solution.py:336
  62.7 4.5 %collective-permute-start.12 = (f32[512]{0:T(512)S(1)}, f32[512]{0:T(512)S(1)}, u32[]{:S(2)}, u32[]{:S(2)}) collective-permute-start(f32[512]{0:T(512)S(1)} %bitcast.30), channel_id=1, source_target_pairs={{0,6},{1,7},{2,4},{3,5},{4,2},{5,3},{6,0},{7,1},{8,14},{9,15},{10,... | collective-permute-start | bytes 6152 | tf_op jit(solution)/shard_map/ppermute | solution.py:428
  64.2 10.2 %copy-start.9 = (f32[128,512]{1,0:T(8,128)S(1)}, f32[128,512]{1,0:T(8,128)}, u32[]{:S(2)}) copy-start(f32[128,512]{1,0:T(8,128)} %get-tuple-element.33) | copy-start | bytes 786436
  64.2 10.2 %copy-start.10 = (f32[128,512]{1,0:T(8,128)S(1)}, f32[128,512]{1,0:T(8,128)}, u32[]{:S(2)}) copy-start(f32[128,512]{1,0:T(8,128)} %get-tuple-element.34) | copy-start | bytes 786436
  64.2 10.2 %copy-start.11 = (f32[128,512]{1,0:T(8,128)S(1)}, f32[128,512]{1,0:T(8,128)}, u32[]{:S(2)}) copy-start(f32[128,512]{1,0:T(8,128)} %get-tuple-element.32) | copy-start | bytes 786436
  64.2 10.2 %copy-start.12 = (f32[128,512]{1,0:T(8,128)S(1)}, f32[128,512]{1,0:T(8,128)}, u32[]{:S(2)}) copy-start(f32[128,512]{1,0:T(8,128)} %get-tuple-element.23) | copy-start | bytes 786436
  64.4 10.0 %collective-permute-start.9 = (bf16[256,512]{1,0:T(8,128)(2,1)S(1)}, bf16[256,512]{1,0:T(8,128)(2,1)S(1)}, u32[]{:S(2)}, u32[]{:S(2)}) collective-permute-start(bf16[256,512]{1,0:T(8,128)(2,1)S(1)} %pad_maximum_fusion), channel_id=1, source_target_pairs={{0,2},{1,3},{2,0},{3,1},{4,6},{5,7},{6,4},{7,5},{8,10},{9,11},{10,... | collective-permute-start | bytes 786440 | tf_op jit(solution)/shard_map/ppermute | solution.py:336
  67.2 8.1 %collective-permute-start.14 = (f32[512]{0:T(512)S(1)}, f32[512]{0:T(512)S(1)}, u32[]{:S(2)}, u32[]{:S(2)}) collective-permute-start(f32[512]{0:T(512)S(1)} %add_add_fusion.1), channel_id=1, source_target_pairs={{0,16},{4,20},{8,24},{12,28},{16,0},{20,4},{24,8},{28,12},{1,17},{... | collective-permute-start | bytes 6152 | tf_op jit(solution)/shard_map/ppermute | solution.py:336
  69.5 5.9 %collective-permute-start.13 = (f32[512]{0:T(512)S(1)}, f32[512]{0:T(512)S(1)}, u32[]{:S(2)}, u32[]{:S(2)}) collective-permute-start(f32[512]{0:T(512)S(1)} %add_add_fusion.1), channel_id=1, source_target_pairs={{0,8},{4,12},{8,0},{12,4},{16,24},{20,28},{24,16},{28,20},{1,9},{5... | collective-permute-start | bytes 6152 | tf_op jit(solution)/shard_map/ppermute | solution.py:336
  70.4 5.4 %collective-permute-start.15 = (f32[512]{0:T(512)S(1)}, f32[512]{0:T(512)S(1)}, u32[]{:S(2)}, u32[]{:S(2)}) collective-permute-start(f32[512]{0:T(512)S(1)} %add_add_fusion.1), channel_id=1, source_target_pairs={{0,24},{4,28},{8,16},{12,20},{16,8},{20,12},{24,0},{28,4},{1,25},{... | collective-permute-start | bytes 6152 | tf_op jit(solution)/shard_map/ppermute | solution.py:336
  (1 other events, 0.7 us)

commit v6 on v5

--- a/solution.py
+++ b/solution.py
@@ -191,36 +191,28 @@
 
 
 def attention_kernel(*refs):
-    *piece_refs, prow_ref, pcol_ref, out_ref, all_ref, dk_ref, dv_ref = refs
+    *piece_refs, prow_ref, pcol_ref, out_ref, all_ref, sems = refs
     rows = piece_refs[0].shape[0]
-    length, width = all_ref.shape
-    local = width // 4
-    block = length
-    for j, piece in enumerate(piece_refs):
-        all_ref[j * rows : (j + 1) * rows, :] = piece[...]
-    dk_ref[...] = jnp.zeros_like(dk_ref)
-    dv_ref[...] = jnp.zeros_like(dv_ref)
-
-    def visit(step, carry):
-        at = pl.ds(pl.multiple_of(step * block, block), block)
-        allowed = prow_ref[...] <= pcol_ref[at, :]
-        for low in range(0, local, HEAD_DIM):
-            query, keys, values, grad = (
-                slice(part * local + low, part * local + low + HEAD_DIM) for part in range(4)
-            )
-            here = slice(low, low + HEAD_DIM)
-            attended, grad_query, key_part, value_part = attend(
-                all_ref[at, query], all_ref[:, keys], all_ref[:, values], all_ref[at, grad], allowed
-            )
-            out_ref[3, at, here] = attended
-            out_ref[0, at, here] = grad_query
-            dk_ref[:, here] += key_part
-            dv_ref[:, here] += value_part
-        return carry
-
-    lax.fori_loop(0, length // block, visit, 0)
-    out_ref[1] = dk_ref[...].astype(BF16)
-    out_ref[2] = dv_ref[...].astype(BF16)
+    local = all_ref.shape[1] // 4
+    copies = [
+        pltpu.make_async_copy(piece, all_ref.at[pl.ds(j * rows, rows), :], sems.at[j])
+        for j, piece in enumerate(piece_refs)
+    ]
+    for copy in copies:
+        copy.start()
+    for copy in copies:
+        copy.wait()
+    allowed = prow_ref[...] <= pcol_ref[...]
+    for low in range(0, local, HEAD_DIM):
+        query, keys, values, grad = (
+            all_ref[:, part * local + low : part * local + low + HEAD_DIM] for part in range(4)
+        )
+        attended, grad_query, grad_keys, grad_values = attend(query, keys, values, grad, allowed)
+        here = slice(low, low + HEAD_DIM)
+        out_ref[0, :, here] = grad_query
+        out_ref[1, :, here] = grad_keys.astype(BF16)
+        out_ref[2, :, here] = grad_values.astype(BF16)
+        out_ref[3, :, here] = attended
 
 
 def attention(pieces, positions):
@@ -229,11 +221,10 @@
     in_vmem = pl.BlockSpec(memory_space=pltpu.VMEM)
     return pl.pallas_call(
         attention_kernel,
-        in_specs=[in_vmem] * (len(pieces) + 2),
+        in_specs=[pl.BlockSpec(memory_space=pl.ANY)] * len(pieces) + [in_vmem] * 2,
         out_specs=in_vmem,
         out_shape=jax.ShapeDtypeStruct((4, length, local), BF16),
-        scratch_shapes=[pltpu.VMEM((length, width), BF16)]
-        + [pltpu.VMEM((length, local), F32)] * 2,
+        scratch_shapes=[pltpu.VMEM((length, width), BF16), pltpu.SemaphoreType.DMA((len(pieces),))],
         compiler_params=params(44),
         name="attention",
     )(*pieces, positions[None, :], positions[:, None])
@@ -394,6 +385,7 @@
         across_below = swap(across, "ctx", 1)
         blocks = [payload, below, beside, diagonal, across, across_below]
         blocks += [corner, swap(corner, "ctx", 1)]
+        blocks[1] = pltpu.with_memory_space_constraint(below, pltpu.HBM)
         placed = jnp.concatenate(
             [lax.dynamic_slice_in_dim(positions, (ctx_rank ^ j) * rows, rows) for j in range(ctx)]
         )

time: 76.7 us -> 75.7 us (0.987)
  local copies, waits for them, and re-layouts: 2.6 us -> 1.66 us
    unnamed x35 -> x33, local copies, waits for them, and re-layouts: 2.25 us -> 1.31 us
where the time goes in v6:
time: 75.7 us; the launch traced here: 75.4 us
  starting transfers between devices  29.3 us (39%)
  Pallas kernels  24.3 us (32%)
  waiting for transfers between devices  17.4 us (23%)
  other arithmetic  1.81 us (2%)
  local copies, waits for them, and re-layouts  1.66 us (2%)
  between operations  0.93 us (1%)
    ppermute x17, starting transfers between devices, swap(): return lax.ppermute(value, axis, [(i, i ^ mask) for i in range(count)])  21.7 us
    ppermute x17, waiting for transfers between devices, swap(): return lax.ppermute(value, axis, [(i, i ^ mask) for i in range(count)])  16.2 us
    pallas_call x1, Pallas kernels, attention(): pl.pallas_call(attention_kernel, in_specs=[pl.BlockSpec(memory_space=pl.A...  11.2 us
    all_to_all x1, starting transfers between devices, body(): both = lax.all_to_all(after(both, below), 'ctx', 0, 0)  6.06 us
    pallas_call x1, Pallas kernels, project(): pl.pallas_call(project_kernel, in_specs=[pl.BlockSpec(memory_space=pltpu....  5.26 us
    pallas_call x1, Pallas kernels, factors(): pl.pallas_call(factor_kernel, in_specs=[pl.BlockSpec(memory_space=pltpu.S...  3.67 us
    pallas_call x1, Pallas kernels, weight_grads(): pl.pallas_call(weight_kernel, in_specs=[pl.BlockSpec(memory_space=pltpu.S...  2.74 us
  transfers between devices with their start and end apart: 19, of which 8 were waited for; matrix products, arithmetic and copies ran while one was open for 3% of the time, Pallas kernels for 8%

profile of v6, /device:TPU:0, one launch (start us, length us, event | category | flops | bytes accessed | tf_op | source)
XLA Modules:
  0.0 75.4 jit_solution(5107672486520498393)
XLA Ops:
  0.7 5.3 %project.1 = (bf16[128,1024]{1,0:T(8,128)(2,1)}, bf16[128,2048]{1,0:T(8,128)(2,1)}, f32[128,1]{1,0:T(8,128)S(1)}, bf16[8,32,512]{2,1,0:T(8,128)(2,1)}) custom-call(s32[1]{0:T(128)} %bitcast.at_ref, bf16[128,2048]{1,0:T(8,128)(2,1)} %tok_ref.3, s32[2,128,2048]{2,1,0:T(8,128)} %pulse_ref.1, f32[1,2048]{1,0:T(1,128)} %bitcast.24, ...), custom_call_target="tpu_custom_call" | custom-call | tf_op jit(solution)/shard_map/project/pallas_call | solution.py:99
  6.0 3.0 %collective-permute-start = (bf16[128,1024]{1,0:T(8,128)(2,1)}, bf16[128,1024]{1,0:T(8,128)(2,1)S(1)}, u32[]{:S(2)}, u32[]{:S(2)}) collective-permute-start(bf16[128,1024]{1,0:T(8,128)(2,1)} %get-tuple-element.24.refs_0_), channel_id=1, source_target_pairs={{0,4},{4,0},{8,12},{12,8},{16,20},{20,16},{24,28},{28,24},{1,5},{5... | collective-permute-start | bytes 786440 | tf_op jit(solution)/shard_map/ppermute | solution.py:327
  9.0 2.6 %collective-permute-start.3 = (bf16[128,1024]{1,0:T(8,128)(2,1)}, bf16[128,1024]{1,0:T(8,128)(2,1)}, u32[]{:S(2)}, u32[]{:S(2)}) collective-permute-start(bf16[128,1024]{1,0:T(8,128)(2,1)} %get-tuple-element.24.refs_0_), channel_id=1, source_target_pairs={{0,16},{4,20},{8,24},{12,28},{16,0},{20,4},{24,8},{28,12},{1,17},{... | collective-permute-start | bytes 786440 | tf_op jit(solution)/shard_map/ppermute | solution.py:327
  11.6 1.6 %collective-permute-start.1 = (bf16[128,1024]{1,0:T(8,128)(2,1)}, bf16[128,1024]{1,0:T(8,128)(2,1)}, u32[]{:S(2)}, u32[]{:S(2)}) collective-permute-start(bf16[128,1024]{1,0:T(8,128)(2,1)} %get-tuple-element.24.refs_0_), channel_id=1, source_target_pairs={{0,8},{4,12},{8,0},{12,4},{16,24},{20,28},{24,16},{28,20},{1,9},{5... | collective-permute-start | bytes 786440 | tf_op jit(solution)/shard_map/ppermute | solution.py:327
  13.2 2.3 %collective-permute-done.refs_1_ = bf16[128,1024]{1,0:T(8,128)(2,1)S(1)} collective-permute-done((bf16[128,1024]{1,0:T(8,128)(2,1)}, bf16[128,1024]{1,0:T(8,128)(2,1)S(1)}, u32[]{:S(2)}, u32[]{:S(2)}) %collective-permute-start) | collective-permute-done | bytes 262176 | tf_op jit(solution)/shard_map/ppermute | solution.py:327
  15.5 0.7 copy-done.11
  16.2 6.1 %all-to-all-start = ((bf16[8,32,512]{2,1,0:T(8,128)(2,1)}), bf16[8,32,512]{2,1,0:T(8,128)(2,1)S(1)}, u32[]{:S(2)}, u32[]{:S(2)}) async-start(bf16[8,32,512]{2,1,0:T(8,128)(2,1)} %get-tuple-element.26), calls=%async_computation | async-start | bytes 524288 | tf_op jit(solution)/shard_map/all_to_all | solution.py:392
  22.4 1.3 %collective-permute-done.3.refs_4_ = bf16[128,1024]{1,0:T(8,128)(2,1)} collective-permute-done((bf16[128,1024]{1,0:T(8,128)(2,1)}, bf16[128,1024]{1,0:T(8,128)(2,1)}, u32[]{:S(2)}, u32[]{:S(2)}) %collective-permute-start.3) | collective-permute-done | bytes 262176 | tf_op jit(solution)/shard_map/ppermute | solution.py:327
  23.7 1.2 %collective-permute-start.5 = (bf16[128,1024]{1,0:T(8,128)(2,1)}, bf16[128,1024]{1,0:T(8,128)(2,1)}, u32[]{:S(2)}, u32[]{:S(2)}) collective-permute-start(bf16[128,1024]{1,0:T(8,128)(2,1)} %collective-permute-done.3.refs_4_), channel_id=1, source_target_pairs={{0,8},{4,12},{8,0},{12,4},{16,24},{20,28},{24,16},{28,20},{1,9},{5... | collective-permute-start | bytes 786440 | tf_op jit(solution)/shard_map/ppermute | solution.py:327
  25.1 0.9 %collective-permute-start.2 = (bf16[128,1024]{1,0:T(8,128)(2,1)}, bf16[128,1024]{1,0:T(8,128)(2,1)}, u32[]{:S(2)}, u32[]{:S(2)}) collective-permute-start(bf16[128,1024]{1,0:T(8,128)(2,1)} %copy-done.11), channel_id=1, source_target_pairs={{0,8},{4,12},{8,0},{12,4},{16,24},{20,28},{24,16},{28,20},{1,9},{5... | collective-permute-start | bytes 786440 | tf_op jit(solution)/shard_map/ppermute | solution.py:327
  26.0 0.7 collective-permute-start.4
  26.7 8.7 %collective-permute-done.5.refs_6_ = bf16[128,1024]{1,0:T(8,128)(2,1)} collective-permute-done((bf16[128,1024]{1,0:T(8,128)(2,1)}, bf16[128,1024]{1,0:T(8,128)(2,1)}, u32[]{:S(2)}, u32[]{:S(2)}) %collective-permute-start.5) | collective-permute-done | bytes 262176 | tf_op jit(solution)/shard_map/ppermute | solution.py:327
  35.4 1.7 %collective-permute-start.6 = (bf16[128,1024]{1,0:T(8,128)(2,1)}, bf16[128,1024]{1,0:T(8,128)(2,1)}, u32[]{:S(2)}, u32[]{:S(2)}) collective-permute-start(bf16[128,1024]{1,0:T(8,128)(2,1)} %collective-permute-done.5.refs_6_), channel_id=1, source_target_pairs={{0,4},{4,0},{8,12},{12,8},{16,20},{20,16},{24,28},{28,24},{1,5},{5... | collective-permute-start | bytes 786440 | tf_op jit(solution)/shard_map/ppermute | solution.py:327
  37.1 1.5 %collective-permute-start.7 = (bf16[8,32,512]{2,1,0:T(8,128)(2,1)S(1)}, bf16[8,32,512]{2,1,0:T(8,128)(2,1)}, u32[]{:S(2)}, u32[]{:S(2)}) collective-permute-start(bf16[8,32,512]{2,1,0:T(8,128)(2,1)S(1)} %all-to-all-done.refs_0_), channel_id=1, source_target_pairs={{0,2},{1,3},{2,0},{3,1},{4,6},{5,7},{6,4},{7,5},{8,10},{9,11},{10,... | collective-permute-start | bytes 786440 | tf_op jit(solution)/shard_map/ppermute | solution.py:327
  38.7 3.7 %factors.1 = (f32[128,2048]{1,0:T(8,128)}, f32[128,512]{1,0:T(8,128)}, f32[128,512]{1,0:T(8,128)}, f32[128,512]{1,0:T(8,128)}, f32[128,512]{1,0:T(8,128)}) custom-call(s32[1]{0:T(128)} %bitcast.at_ref, bf16[128,2048]{1,0:T(8,128)(2,1)S(1)} %copy-done.2, s32[2,128,2048]{2,1,0:T(8,128)S(1)} %copy-done.1, f32[1,2048]{1,0:T(1,128)S(1)} %bitcast.25, ...), custom_call_target="tpu_custom_call" | custom-call | tf_op jit(solution)/shard_map/factors/pallas_call | solution.py:162
  42.6 1.0 %collective-permute-done.7.refs_2_ = bf16[8,32,512]{2,1,0:T(8,128)(2,1)} collective-permute-done((bf16[8,32,512]{2,1,0:T(8,128)(2,1)S(1)}, bf16[8,32,512]{2,1,0:T(8,128)(2,1)}, u32[]{:S(2)}, u32[]{:S(2)}) %collective-permute-start.7) | collective-permute-done | bytes 262176 | tf_op jit(solution)/shard_map/ppermute | solution.py:327
  43.9 11.2 %attention.1.refs_4_ = bf16[4,1024,256]{2,1,0:T(8,128)(2,1)S(1)} custom-call(bf16[128,1024]{1,0:T(8,128)(2,1)} %get-tuple-element.24.refs_0_, bf16[128,1024]{1,0:T(8,128)(2,1)} %copy-done.11, bf16[128,1024]{1,0:T(8,128)(2,1)} %collective-permute-done.1.refs_2_, bf16[128,1024]{1,0:T(8,128)(2,1)} %collective-permute-done.2.refs_3_, ...), custom_call_target="tpu_custom_call" | custom-call | tf_op jit(solution)/shard_map/attention/pallas_call | solution.py:222
  55.2 1.5 %spread.1 = (f32[264,512]{1,0:T(8,128)S(1)}, f32[264,512]{1,0:T(8,128)S(1)}, f32[2,264,512]{2,1,0:T(8,128)S(1)}) custom-call(s32[1]{0:T(128)} %bitcast.at_ref, bf16[4,128,256]{2,1,0:T(8,128)(2,1)S(1)} %slice.62.grad_ref, bf16[3,2048,256]{2,1,0:T(8,128)(2,1)S(1)} %bitcast.23, bf16[256,2048]{1,0:T(8,128)(2,1)S(1)} %copy-done.3, ...), custom_call_target="tpu_custom_call" | custom-call | tf_op jit(solution)/shard_map/spread/pallas_call | solution.py:311
  56.7 0.5 collective-permute-start.16
  57.3 2.1 %collective-permute-done.8 = f32[2,264,512]{2,1,0:T(8,128)S(1)} collective-permute-done((f32[2,264,512]{2,1,0:T(8,128)S(1)}, f32[2,264,512]{2,1,0:T(8,128)S(1)}, u32[]{:S(2)}, u32[]{:S(2)}) %collective-permute-start.8) | collective-permute-done | bytes 1081376 | tf_op jit(solution)/shard_map/ppermute | solution.py:327
  59.7 1.6 %collective-permute-start.10 = (f32[8,512]{1,0:T(8,128)S(1)}, f32[8,512]{1,0:T(8,128)S(1)}, u32[]{:S(2)}, u32[]{:S(2)}) collective-permute-start(f32[8,512]{1,0:T(8,128)S(1)} %slice.72), channel_id=1, source_target_pairs={{0,2},{1,3},{2,0},{3,1},{4,6},{5,7},{6,4},{7,5},{8,10},{9,11},{10,... | collective-permute-start | bytes 49160 | tf_op jit(solution)/shard_map/ppermute | solution.py:327
  61.2 0.5 collective-permute-start.11
  61.7 1.5 %collective-permute-start.12 = (f32[512]{0:T(512)S(1)}, f32[512]{0:T(512)S(1)}, u32[]{:S(2)}, u32[]{:S(2)}) collective-permute-start(f32[512]{0:T(512)S(1)} %bitcast.30), channel_id=1, source_target_pairs={{0,6},{1,7},{2,4},{3,5},{4,2},{5,3},{6,0},{7,1},{8,14},{9,15},{10,... | collective-permute-start | bytes 6152 | tf_op jit(solution)/shard_map/ppermute | solution.py:420
  63.5 1.5 %collective-permute-start.9 = (bf16[256,512]{1,0:T(8,128)(2,1)S(1)}, bf16[256,512]{1,0:T(8,128)(2,1)S(1)}, u32[]{:S(2)}, u32[]{:S(2)}) collective-permute-start(bf16[256,512]{1,0:T(8,128)(2,1)S(1)} %pad_maximum_fusion), channel_id=1, source_target_pairs={{0,2},{1,3},{2,0},{3,1},{4,6},{5,7},{6,4},{7,5},{8,10},{9,11},{10,... | collective-permute-start | bytes 786440 | tf_op jit(solution)/shard_map/ppermute | solution.py:327
  65.0 1.2 %collective-permute-done.12 = f32[512]{0:T(512)S(1)} collective-permute-done((f32[512]{0:T(512)S(1)}, f32[512]{0:T(512)S(1)}, u32[]{:S(2)}, u32[]{:S(2)}) %collective-permute-start.12) | collective-permute-done | bytes 2080 | tf_op jit(solution)/shard_map/ppermute | solution.py:420
  66.2 2.3 %collective-permute-start.14 = (f32[512]{0:T(512)S(1)}, f32[512]{0:T(512)S(1)}, u32[]{:S(2)}, u32[]{:S(2)}) collective-permute-start(f32[512]{0:T(512)S(1)} %add_add_fusion.1), channel_id=1, source_target_pairs={{0,16},{4,20},{8,24},{12,28},{16,0},{20,4},{24,8},{28,12},{1,17},{... | collective-permute-start | bytes 6152 | tf_op jit(solution)/shard_map/ppermute | solution.py:327
  68.5 0.9 %collective-permute-start.13 = (f32[512]{0:T(512)S(1)}, f32[512]{0:T(512)S(1)}, u32[]{:S(2)}, u32[]{:S(2)}) collective-permute-start(f32[512]{0:T(512)S(1)} %add_add_fusion.1), channel_id=1, source_target_pairs={{0,8},{4,12},{8,0},{12,4},{16,24},{20,28},{24,16},{28,20},{1,9},{5... | collective-permute-start | bytes 6152 | tf_op jit(solution)/shard_map/ppermute | solution.py:327
  69.5 1.2 %collective-permute-start.15 = (f32[512]{0:T(512)S(1)}, f32[512]{0:T(512)S(1)}, u32[]{:S(2)}, u32[]{:S(2)}) collective-permute-start(f32[512]{0:T(512)S(1)} %add_add_fusion.1), channel_id=1, source_target_pairs={{0,24},{4,28},{8,16},{12,20},{16,8},{20,12},{24,0},{28,4},{1,25},{... | collective-permute-start | bytes 6152 | tf_op jit(solution)/shard_map/ppermute | solution.py:327
  70.7 2.7 %weight_grads.1 = (f32[3,256,256]{2,1,0:T(8,128)}, f32[256,256]{1,0:T(8,128)}) custom-call(s32[2]{0:T(128)S(1)} %pad_add_fusion.at_ref, bf16[8,32,512]{2,1,0:T(8,128)(2,1)S(1)} %all-to-all-done.refs_0_, bf16[8,32,512]{2,1,0:T(8,128)(2,1)S(1)} %collective-permute-done.16.refs_1_, bf16[8,32,512]{2,1,0:T(8,128)(2,1)} %collective-permute-done.7.refs_2_, ...), custom_call_target="tpu_custom_call" | custom-call | tf_op jit(solution)/shard_map/weight_grads/pallas_call | solution.py:348
  73.5 0.9 %fusion.4 = (f32[128,512]{1,0:T(8,128)}, bf16[128,512]{1,0:T(8,128)(2,1)}) fusion(f32[128,512]{1,0:T(8,128)S(1)} %copy-done.9, f32[128,512]{1,0:T(8,128)S(1)} %copy-done.7, f32[264,512]{1,0:T(8,128)S(1)} %get-tuple-element.41, f32[128,512]{1,0:T(8,128)S(1)} %copy-done.8, bf16[256,512]{1,0:T(8,128)(2,1)S(1)} %collective-permute-done.9, ...), kind=kLoop, calls=%fused_computation.7 | loop fusion | flops 655360 | bytes 2228736 | tf_op jit(solution)/shard_map/add | solution.py:428
  74.4 0.5 collective-permute-done.15
  74.9 0.6 add_add_fusion
  (61 shorter events, 1.6 us)
Async XLA Ops:
  0.6 21.6 %copy-start.12 = (s32[1024]{0:T(1024)S(1)}, s32[1024]{0:T(1024)}, u32[]{:S(2)}) copy-start(s32[1024]{0:T(1024)} %param.8) | copy-start | bytes 12292
  0.6 38.1 %copy-start.1 = (s32[2,128,2048]{2,1,0:T(8,128)S(1)}, s32[2,128,2048]{2,1,0:T(8,128)}, u32[]{:S(2)}) copy-start(s32[2,128,2048]{2,1,0:T(8,128)} %pulse_ref.1) | copy-start | bytes 6291460
  0.7 38.1 %copy-start.2 = (bf16[128,2048]{1,0:T(8,128)(2,1)S(1)}, bf16[128,2048]{1,0:T(8,128)(2,1)}, u32[]{:S(2)}) copy-start(bf16[128,2048]{1,0:T(8,128)(2,1)} %tok_ref.3) | copy-start | bytes 1572868
  0.7 38.1 %copy-start.4 = (bf16[128,2048]{1,0:T(8,128)(2,1)S(1)}, bf16[128,2048]{1,0:T(8,128)(2,1)}, u32[]{:S(2)}) copy-start(bf16[128,2048]{1,0:T(8,128)(2,1)} %up_ref.1) | copy-start | bytes 1572868
  0.7 38.0 %copy-start.6 = (f32[2048]{0:T(1024)S(1)}, f32[2048]{0:T(1024)}, u32[]{:S(2)}) copy-start(f32[2048]{0:T(1024)} %param.10) | copy-start | bytes 24580
  6.0 9.6 %collective-permute-start = (bf16[128,1024]{1,0:T(8,128)(2,1)}, bf16[128,1024]{1,0:T(8,128)(2,1)S(1)}, u32[]{:S(2)}, u32[]{:S(2)}) collective-permute-start(bf16[128,1024]{1,0:T(8,128)(2,1)} %get-tuple-element.24.refs_0_), channel_id=1, source_target_pairs={{0,4},{4,0},{8,12},{12,8},{16,20},{20,16},{24,28},{28,24},{1,5},{5... | collective-permute-start | bytes 786440 | tf_op jit(solution)/shard_map/ppermute | solution.py:327
  9.0 14.7 %collective-permute-start.3 = (bf16[128,1024]{1,0:T(8,128)(2,1)}, bf16[128,1024]{1,0:T(8,128)(2,1)}, u32[]{:S(2)}, u32[]{:S(2)}) collective-permute-start(bf16[128,1024]{1,0:T(8,128)(2,1)} %get-tuple-element.24.refs_0_), channel_id=1, source_target_pairs={{0,16},{4,20},{8,24},{12,28},{16,0},{20,4},{24,8},{28,12},{1,17},{... | collective-permute-start | bytes 786440 | tf_op jit(solution)/shard_map/ppermute | solution.py:327
  11.6 32.3 %collective-permute-start.1 = (bf16[128,1024]{1,0:T(8,128)(2,1)}, bf16[128,1024]{1,0:T(8,128)(2,1)}, u32[]{:S(2)}, u32[]{:S(2)}) collective-permute-start(bf16[128,1024]{1,0:T(8,128)(2,1)} %get-tuple-element.24.refs_0_), channel_id=1, source_target_pairs={{0,8},{4,12},{8,0},{12,4},{16,24},{20,28},{24,16},{28,20},{1,9},{5... | collective-permute-start | bytes 786440 | tf_op jit(solution)/shard_map/ppermute | solution.py:327
  15.5 0.7 copy-start.11
  16.2 20.9 %all-to-all-start = ((bf16[8,32,512]{2,1,0:T(8,128)(2,1)}), bf16[8,32,512]{2,1,0:T(8,128)(2,1)S(1)}, u32[]{:S(2)}, u32[]{:S(2)}) async-start(bf16[8,32,512]{2,1,0:T(8,128)(2,1)} %get-tuple-element.26), calls=%async_computation | async-start | bytes 524288 | tf_op jit(solution)/shard_map/all_to_all | solution.py:392
  23.7 11.7 %collective-permute-start.5 = (bf16[128,1024]{1,0:T(8,128)(2,1)}, bf16[128,1024]{1,0:T(8,128)(2,1)}, u32[]{:S(2)}, u32[]{:S(2)}) collective-permute-start(bf16[128,1024]{1,0:T(8,128)(2,1)} %collective-permute-done.3.refs_4_), channel_id=1, source_target_pairs={{0,8},{4,12},{8,0},{12,4},{16,24},{20,28},{24,16},{28,20},{1,9},{5... | collective-permute-start | bytes 786440 | tf_op jit(solution)/shard_map/ppermute | solution.py:327
  25.1 18.7 %collective-permute-start.2 = (bf16[128,1024]{1,0:T(8,128)(2,1)}, bf16[128,1024]{1,0:T(8,128)(2,1)}, u32[]{:S(2)}, u32[]{:S(2)}) collective-permute-start(bf16[128,1024]{1,0:T(8,128)(2,1)} %copy-done.11), channel_id=1, source_target_pairs={{0,8},{4,12},{8,0},{12,4},{16,24},{20,28},{24,16},{28,20},{1,9},{5... | collective-permute-start | bytes 786440 | tf_op jit(solution)/shard_map/ppermute | solution.py:327
  26.0 17.9 %collective-permute-start.4 = (bf16[128,1024]{1,0:T(8,128)(2,1)}, bf16[128,1024]{1,0:T(8,128)(2,1)}, u32[]{:S(2)}, u32[]{:S(2)}) collective-permute-start(bf16[128,1024]{1,0:T(8,128)(2,1)} %collective-permute-done.3.refs_4_), channel_id=1, source_target_pairs={{0,4},{4,0},{8,12},{12,8},{16,20},{20,16},{24,28},{28,24},{1,5},{5... | collective-permute-start | bytes 786440 | tf_op jit(solution)/shard_map/ppermute | solution.py:327
  35.4 8.5 %collective-permute-start.6 = (bf16[128,1024]{1,0:T(8,128)(2,1)}, bf16[128,1024]{1,0:T(8,128)(2,1)}, u32[]{:S(2)}, u32[]{:S(2)}) collective-permute-start(bf16[128,1024]{1,0:T(8,128)(2,1)} %collective-permute-done.5.refs_6_), channel_id=1, source_target_pairs={{0,4},{4,0},{8,12},{12,8},{16,20},{20,16},{24,28},{28,24},{1,5},{5... | collective-permute-start | bytes 786440 | tf_op jit(solution)/shard_map/ppermute | solution.py:327
  37.1 6.5 %collective-permute-start.7 = (bf16[8,32,512]{2,1,0:T(8,128)(2,1)S(1)}, bf16[8,32,512]{2,1,0:T(8,128)(2,1)}, u32[]{:S(2)}, u32[]{:S(2)}) collective-permute-start(bf16[8,32,512]{2,1,0:T(8,128)(2,1)S(1)} %all-to-all-done.refs_0_), channel_id=1, source_target_pairs={{0,2},{1,3},{2,0},{3,1},{4,6},{5,7},{6,4},{7,5},{8,10},{9,11},{10,... | collective-permute-start | bytes 786440 | tf_op jit(solution)/shard_map/ppermute | solution.py:327
  43.9 11.3 %copy-start = (bf16[2048,3,256]{2,0,1:T(8,128)(2,1)S(1)}, bf16[2048,3,256]{2,0,1:T(8,128)(2,1)}, u32[]{:S(2)}) copy-start(bf16[2048,3,256]{2,0,1:T(8,128)(2,1)} %param.11) | copy-start | bytes 9437188
  43.9 11.3 %copy-start.3 = (bf16[256,2048]{1,0:T(8,128)(2,1)S(1)}, bf16[256,2048]{1,0:T(8,128)(2,1)}, u32[]{:S(2)}) copy-start(bf16[256,2048]{1,0:T(8,128)(2,1)} %wout_ref.1) | copy-start | bytes 3145732
  43.9 11.3 %copy-start.5 = (f32[128,2048]{1,0:T(8,128)S(1)}, f32[128,2048]{1,0:T(8,128)}, u32[]{:S(2)}) copy-start(f32[128,2048]{1,0:T(8,128)} %get-tuple-element.28.factor_ref) | copy-start | bytes 3145732
  56.7 2.7 %collective-permute-start.8 = (f32[2,264,512]{2,1,0:T(8,128)S(1)}, f32[2,264,512]{2,1,0:T(8,128)S(1)}, u32[]{:S(2)}, u32[]{:S(2)}) collective-permute-start(f32[2,264,512]{2,1,0:T(8,128)S(1)} %get-tuple-element.30), channel_id=1, source_target_pairs={{0,1},{1,0},{2,3},{3,2},{4,5},{5,4},{6,7},{7,6},{8,9},{9,8},{10,11... | collective-permute-start | bytes 3244040 | tf_op jit(solution)/shard_map/ppermute | solution.py:327
  56.7 12.8 %collective-permute-start.16 = (bf16[8,32,512]{2,1,0:T(8,128)(2,1)S(1)}, bf16[8,32,512]{2,1,0:T(8,128)(2,1)S(1)}, u32[]{:S(2)}, u32[]{:S(2)}) collective-permute-start(bf16[8,32,512]{2,1,0:T(8,128)(2,1)S(1)} %all-to-all-done.refs_0_), channel_id=1, source_target_pairs={{0,1},{1,0},{2,3},{3,2},{4,5},{5,4},{6,7},{7,6},{8,9},{9,8},{10,11... | collective-permute-start | bytes 786440 | tf_op jit(solution)/shard_map/ppermute | solution.py:327
  57.2 13.5 %collective-permute-start.17 = (bf16[8,32,512]{2,1,0:T(8,128)(2,1)}, bf16[8,32,512]{2,1,0:T(8,128)(2,1)S(1)}, u32[]{:S(2)}, u32[]{:S(2)}) collective-permute-start(bf16[8,32,512]{2,1,0:T(8,128)(2,1)} %collective-permute-done.7.refs_2_), channel_id=1, source_target_pairs={{0,1},{1,0},{2,3},{3,2},{4,5},{5,4},{6,7},{7,6},{8,9},{9,8},{10,11... | collective-permute-start | bytes 786440 | tf_op jit(solution)/shard_map/ppermute | solution.py:327
  59.7 3.8 %collective-permute-start.10 = (f32[8,512]{1,0:T(8,128)S(1)}, f32[8,512]{1,0:T(8,128)S(1)}, u32[]{:S(2)}, u32[]{:S(2)}) collective-permute-start(f32[8,512]{1,0:T(8,128)S(1)} %slice.72), channel_id=1, source_target_pairs={{0,2},{1,3},{2,0},{3,1},{4,6},{5,7},{6,4},{7,5},{8,10},{9,11},{10,... | collective-permute-start | bytes 49160 | tf_op jit(solution)/shard_map/ppermute | solution.py:327
  61.2 3.7 %collective-permute-start.11 = (f32[512]{0:T(512)S(1)}, f32[512]{0:T(512)S(1)}, u32[]{:S(2)}, u32[]{:S(2)}) collective-permute-start(f32[512]{0:T(512)S(1)} %bitcast.31), channel_id=1, source_target_pairs={{0,4},{4,0},{8,12},{12,8},{16,20},{20,16},{24,28},{28,24},{1,5},{5... | collective-permute-start | bytes 6152 | tf_op jit(solution)/shard_map/ppermute | solution.py:327
  61.7 4.5 %collective-permute-start.12 = (f32[512]{0:T(512)S(1)}, f32[512]{0:T(512)S(1)}, u32[]{:S(2)}, u32[]{:S(2)}) collective-permute-start(f32[512]{0:T(512)S(1)} %bitcast.30), channel_id=1, source_target_pairs={{0,6},{1,7},{2,4},{3,5},{4,2},{5,3},{6,0},{7,1},{8,14},{9,15},{10,... | collective-permute-start | bytes 6152 | tf_op jit(solution)/shard_map/ppermute | solution.py:420
  63.2 10.2 %copy-start.7 = (f32[128,512]{1,0:T(8,128)S(1)}, f32[128,512]{1,0:T(8,128)}, u32[]{:S(2)}) copy-start(f32[128,512]{1,0:T(8,128)} %get-tuple-element.33) | copy-start | bytes 786436
  63.2 10.2 %copy-start.8 = (f32[128,512]{1,0:T(8,128)S(1)}, f32[128,512]{1,0:T(8,128)}, u32[]{:S(2)}) copy-start(f32[128,512]{1,0:T(8,128)} %get-tuple-element.34) | copy-start | bytes 786436
  63.2 10.2 %copy-start.9 = (f32[128,512]{1,0:T(8,128)S(1)}, f32[128,512]{1,0:T(8,128)}, u32[]{:S(2)}) copy-start(f32[128,512]{1,0:T(8,128)} %get-tuple-element.32) | copy-start | bytes 786436
  63.2 10.2 %copy-start.10 = (f32[128,512]{1,0:T(8,128)S(1)}, f32[128,512]{1,0:T(8,128)}, u32[]{:S(2)}) copy-start(f32[128,512]{1,0:T(8,128)} %get-tuple-element.23) | copy-start | bytes 786436
  63.5 10.0 %collective-permute-start.9 = (bf16[256,512]{1,0:T(8,128)(2,1)S(1)}, bf16[256,512]{1,0:T(8,128)(2,1)S(1)}, u32[]{:S(2)}, u32[]{:S(2)}) collective-permute-start(bf16[256,512]{1,0:T(8,128)(2,1)S(1)} %pad_maximum_fusion), channel_id=1, source_target_pairs={{0,2},{1,3},{2,0},{3,1},{4,6},{5,7},{6,4},{7,5},{8,10},{9,11},{10,... | collective-permute-start | bytes 786440 | tf_op jit(solution)/shard_map/ppermute | solution.py:327
  66.2 8.1 %collective-permute-start.14 = (f32[512]{0:T(512)S(1)}, f32[512]{0:T(512)S(1)}, u32[]{:S(2)}, u32[]{:S(2)}) collective-permute-start(f32[512]{0:T(512)S(1)} %add_add_fusion.1), channel_id=1, source_target_pairs={{0,16},{4,20},{8,24},{12,28},{16,0},{20,4},{24,8},{28,12},{1,17},{... | collective-permute-start | bytes 6152 | tf_op jit(solution)/shard_map/ppermute | solution.py:327
  68.5 5.9 %collective-permute-start.13 = (f32[512]{0:T(512)S(1)}, f32[512]{0:T(512)S(1)}, u32[]{:S(2)}, u32[]{:S(2)}) collective-permute-start(f32[512]{0:T(512)S(1)} %add_add_fusion.1), channel_id=1, source_target_pairs={{0,8},{4,12},{8,0},{12,4},{16,24},{20,28},{24,16},{28,20},{1,9},{5... | collective-permute-start | bytes 6152 | tf_op jit(solution)/shard_map/ppermute | solution.py:327
  69.5 5.4 %collective-permute-start.15 = (f32[512]{0:T(512)S(1)}, f32[512]{0:T(512)S(1)}, u32[]{:S(2)}, u32[]{:S(2)}) collective-permute-start(f32[512]{0:T(512)S(1)} %add_add_fusion.1), channel_id=1, source_target_pairs={{0,24},{4,28},{8,16},{12,20},{16,8},{20,12},{24,0},{28,4},{1,25},{... | collective-permute-start | bytes 6152 | tf_op jit(solution)/shard_map/ppermute | solution.py:327

commit v7 on v6

--- a/solution.py
+++ b/solution.py
@@ -93,7 +93,7 @@
 def project(fsdp_rank, ctx, tokens, pulse, gain, win, upstream, wout):
     rows, model = tokens.shape
     local = wout.shape[0]
-    blocks = 4
+    blocks = 2
     arrays = (tokens, pulse, gain, win, upstream, wout)
     in_vmem = pl.BlockSpec(memory_space=pltpu.VMEM)
     return pl.pallas_call(

time: 75.7 us -> 75.5 us (level)
  transfers between devices with their start and end apart: 19 -> 19, of which waited for: 8 -> 8; matrix products, arithmetic and copies ran while one was open for 3% -> 3% of each run, Pallas kernels for 8% -> 9%
where the time goes in v7:
time: 75.5 us; the launch traced here: 75.3 us
  starting transfers between devices  29.3 us (39%)
  Pallas kernels  24.2 us (32%)
  waiting for transfers between devices  17.4 us (23%)
  other arithmetic  1.81 us (2%)
  local copies, waits for them, and re-layouts  1.66 us (2%)
  between operations  0.93 us (1%)
    ppermute x17, starting transfers between devices, swap(): return lax.ppermute(value, axis, [(i, i ^ mask) for i in range(count)])  21.7 us
    ppermute x17, waiting for transfers between devices, swap(): return lax.ppermute(value, axis, [(i, i ^ mask) for i in range(count)])  16.2 us
    pallas_call x1, Pallas kernels, attention(): pl.pallas_call(attention_kernel, in_specs=[pl.BlockSpec(memory_space=pl.A...  11.2 us
    all_to_all x1, starting transfers between devices, body(): both = lax.all_to_all(after(both, below), 'ctx', 0, 0)  6.05 us
    pallas_call x1, Pallas kernels, project(): pl.pallas_call(project_kernel, in_specs=[pl.BlockSpec(memory_space=pltpu....  5.11 us
    pallas_call x1, Pallas kernels, factors(): pl.pallas_call(factor_kernel, in_specs=[pl.BlockSpec(memory_space=pltpu.S...  3.66 us
    pallas_call x1, Pallas kernels, weight_grads(): pl.pallas_call(weight_kernel, in_specs=[pl.BlockSpec(memory_space=pltpu.S...  2.74 us
  transfers between devices with their start and end apart: 19, of which 8 were waited for; matrix products, arithmetic and copies ran while one was open for 3% of the time, Pallas kernels for 9%

profile of v7, /device:TPU:0, one launch (start us, length us, event | category | flops | bytes accessed | tf_op | source)
XLA Modules:
  0.0 75.3 jit_solution(10542170892179834817)
XLA Ops:
  0.7 5.1 %project.1 = (bf16[128,1024]{1,0:T(8,128)(2,1)}, bf16[128,2048]{1,0:T(8,128)(2,1)}, f32[128,1]{1,0:T(8,128)S(1)}, bf16[8,32,512]{2,1,0:T(8,128)(2,1)}) custom-call(s32[1]{0:T(128)} %bitcast.at_ref, bf16[128,2048]{1,0:T(8,128)(2,1)} %tok_ref.3, s32[2,128,2048]{2,1,0:T(8,128)} %pulse_ref.1, f32[1,2048]{1,0:T(1,128)} %bitcast.24, ...), custom_call_target="tpu_custom_call" | custom-call | tf_op jit(solution)/shard_map/project/pallas_call | solution.py:99
  5.8 3.0 %collective-permute-start = (bf16[128,1024]{1,0:T(8,128)(2,1)}, bf16[128,1024]{1,0:T(8,128)(2,1)S(1)}, u32[]{:S(2)}, u32[]{:S(2)}) collective-permute-start(bf16[128,1024]{1,0:T(8,128)(2,1)} %get-tuple-element.24.refs_0_), channel_id=1, source_target_pairs={{0,4},{4,0},{8,12},{12,8},{16,20},{20,16},{24,28},{28,24},{1,5},{5... | collective-permute-start | bytes 786440 | tf_op jit(solution)/shard_map/ppermute | solution.py:327
  8.8 2.6 %collective-permute-start.3 = (bf16[128,1024]{1,0:T(8,128)(2,1)}, bf16[128,1024]{1,0:T(8,128)(2,1)}, u32[]{:S(2)}, u32[]{:S(2)}) collective-permute-start(bf16[128,1024]{1,0:T(8,128)(2,1)} %get-tuple-element.24.refs_0_), channel_id=1, source_target_pairs={{0,16},{4,20},{8,24},{12,28},{16,0},{20,4},{24,8},{28,12},{1,17},{... | collective-permute-start | bytes 786440 | tf_op jit(solution)/shard_map/ppermute | solution.py:327
  11.4 1.6 %collective-permute-start.1 = (bf16[128,1024]{1,0:T(8,128)(2,1)}, bf16[128,1024]{1,0:T(8,128)(2,1)}, u32[]{:S(2)}, u32[]{:S(2)}) collective-permute-start(bf16[128,1024]{1,0:T(8,128)(2,1)} %get-tuple-element.24.refs_0_), channel_id=1, source_target_pairs={{0,8},{4,12},{8,0},{12,4},{16,24},{20,28},{24,16},{28,20},{1,9},{5... | collective-permute-start | bytes 786440 | tf_op jit(solution)/shard_map/ppermute | solution.py:327
  13.0 2.3 %collective-permute-done.refs_1_ = bf16[128,1024]{1,0:T(8,128)(2,1)S(1)} collective-permute-done((bf16[128,1024]{1,0:T(8,128)(2,1)}, bf16[128,1024]{1,0:T(8,128)(2,1)S(1)}, u32[]{:S(2)}, u32[]{:S(2)}) %collective-permute-start) | collective-permute-done | bytes 262176 | tf_op jit(solution)/shard_map/ppermute | solution.py:327
  15.4 0.7 copy-done.11
  16.1 6.1 %all-to-all-start = ((bf16[8,32,512]{2,1,0:T(8,128)(2,1)}), bf16[8,32,512]{2,1,0:T(8,128)(2,1)S(1)}, u32[]{:S(2)}, u32[]{:S(2)}) async-start(bf16[8,32,512]{2,1,0:T(8,128)(2,1)} %get-tuple-element.26), calls=%async_computation | async-start | bytes 524288 | tf_op jit(solution)/shard_map/all_to_all | solution.py:392
  22.3 1.3 %collective-permute-done.3.refs_4_ = bf16[128,1024]{1,0:T(8,128)(2,1)} collective-permute-done((bf16[128,1024]{1,0:T(8,128)(2,1)}, bf16[128,1024]{1,0:T(8,128)(2,1)}, u32[]{:S(2)}, u32[]{:S(2)}) %collective-permute-start.3) | collective-permute-done | bytes 262176 | tf_op jit(solution)/shard_map/ppermute | solution.py:327
  23.6 1.2 %collective-permute-start.5 = (bf16[128,1024]{1,0:T(8,128)(2,1)}, bf16[128,1024]{1,0:T(8,128)(2,1)}, u32[]{:S(2)}, u32[]{:S(2)}) collective-permute-start(bf16[128,1024]{1,0:T(8,128)(2,1)} %collective-permute-done.3.refs_4_), channel_id=1, source_target_pairs={{0,8},{4,12},{8,0},{12,4},{16,24},{20,28},{24,16},{28,20},{1,9},{5... | collective-permute-start | bytes 786440 | tf_op jit(solution)/shard_map/ppermute | solution.py:327
  25.0 0.8 %collective-permute-start.2 = (bf16[128,1024]{1,0:T(8,128)(2,1)}, bf16[128,1024]{1,0:T(8,128)(2,1)}, u32[]{:S(2)}, u32[]{:S(2)}) collective-permute-start(bf16[128,1024]{1,0:T(8,128)(2,1)} %copy-done.11), channel_id=1, source_target_pairs={{0,8},{4,12},{8,0},{12,4},{16,24},{20,28},{24,16},{28,20},{1,9},{5... | collective-permute-start | bytes 786440 | tf_op jit(solution)/shard_map/ppermute | solution.py:327
  25.8 0.7 collective-permute-start.4
  26.6 8.7 %collective-permute-done.5.refs_6_ = bf16[128,1024]{1,0:T(8,128)(2,1)} collective-permute-done((bf16[128,1024]{1,0:T(8,128)(2,1)}, bf16[128,1024]{1,0:T(8,128)(2,1)}, u32[]{:S(2)}, u32[]{:S(2)}) %collective-permute-start.5) | collective-permute-done | bytes 262176 | tf_op jit(solution)/shard_map/ppermute | solution.py:327
  35.3 1.7 %collective-permute-start.6 = (bf16[128,1024]{1,0:T(8,128)(2,1)}, bf16[128,1024]{1,0:T(8,128)(2,1)}, u32[]{:S(2)}, u32[]{:S(2)}) collective-permute-start(bf16[128,1024]{1,0:T(8,128)(2,1)} %collective-permute-done.5.refs_6_), channel_id=1, source_target_pairs={{0,4},{4,0},{8,12},{12,8},{16,20},{20,16},{24,28},{28,24},{1,5},{5... | collective-permute-start | bytes 786440 | tf_op jit(solution)/shard_map/ppermute | solution.py:327
  37.0 1.5 %collective-permute-start.7 = (bf16[8,32,512]{2,1,0:T(8,128)(2,1)S(1)}, bf16[8,32,512]{2,1,0:T(8,128)(2,1)}, u32[]{:S(2)}, u32[]{:S(2)}) collective-permute-start(bf16[8,32,512]{2,1,0:T(8,128)(2,1)S(1)} %all-to-all-done.refs_0_), channel_id=1, source_target_pairs={{0,2},{1,3},{2,0},{3,1},{4,6},{5,7},{6,4},{7,5},{8,10},{9,11},{10,... | collective-permute-start | bytes 786440 | tf_op jit(solution)/shard_map/ppermute | solution.py:327
  38.6 3.7 %factors.1 = (f32[128,2048]{1,0:T(8,128)}, f32[128,512]{1,0:T(8,128)}, f32[128,512]{1,0:T(8,128)}, f32[128,512]{1,0:T(8,128)}, f32[128,512]{1,0:T(8,128)}) custom-call(s32[1]{0:T(128)} %bitcast.at_ref, bf16[128,2048]{1,0:T(8,128)(2,1)S(1)} %copy-done.2, s32[2,128,2048]{2,1,0:T(8,128)S(1)} %copy-done.1, f32[1,2048]{1,0:T(1,128)S(1)} %bitcast.25, ...), custom_call_target="tpu_custom_call" | custom-call | tf_op jit(solution)/shard_map/factors/pallas_call | solution.py:162
  42.4 1.0 %collective-permute-done.7.refs_2_ = bf16[8,32,512]{2,1,0:T(8,128)(2,1)} collective-permute-done((bf16[8,32,512]{2,1,0:T(8,128)(2,1)S(1)}, bf16[8,32,512]{2,1,0:T(8,128)(2,1)}, u32[]{:S(2)}, u32[]{:S(2)}) %collective-permute-start.7) | collective-permute-done | bytes 262176 | tf_op jit(solution)/shard_map/ppermute | solution.py:327
  43.8 11.2 %attention.1.refs_4_ = bf16[4,1024,256]{2,1,0:T(8,128)(2,1)S(1)} custom-call(bf16[128,1024]{1,0:T(8,128)(2,1)} %get-tuple-element.24.refs_0_, bf16[128,1024]{1,0:T(8,128)(2,1)} %copy-done.11, bf16[128,1024]{1,0:T(8,128)(2,1)} %collective-permute-done.1.refs_2_, bf16[128,1024]{1,0:T(8,128)(2,1)} %collective-permute-done.2.refs_3_, ...), custom_call_target="tpu_custom_call" | custom-call | tf_op jit(solution)/shard_map/attention/pallas_call | solution.py:222
  55.0 1.5 %spread.1 = (f32[264,512]{1,0:T(8,128)S(1)}, f32[264,512]{1,0:T(8,128)S(1)}, f32[2,264,512]{2,1,0:T(8,128)S(1)}) custom-call(s32[1]{0:T(128)} %bitcast.at_ref, bf16[4,128,256]{2,1,0:T(8,128)(2,1)S(1)} %slice.62.grad_ref, bf16[3,2048,256]{2,1,0:T(8,128)(2,1)S(1)} %bitcast.23, bf16[256,2048]{1,0:T(8,128)(2,1)S(1)} %copy-done.3, ...), custom_call_target="tpu_custom_call" | custom-call | tf_op jit(solution)/shard_map/spread/pallas_call | solution.py:311
  56.6 0.5 collective-permute-start.16
  57.1 2.1 %collective-permute-done.8 = f32[2,264,512]{2,1,0:T(8,128)S(1)} collective-permute-done((f32[2,264,512]{2,1,0:T(8,128)S(1)}, f32[2,264,512]{2,1,0:T(8,128)S(1)}, u32[]{:S(2)}, u32[]{:S(2)}) %collective-permute-start.8) | collective-permute-done | bytes 1081376 | tf_op jit(solution)/shard_map/ppermute | solution.py:327
  59.5 1.6 %collective-permute-start.10 = (f32[8,512]{1,0:T(8,128)S(1)}, f32[8,512]{1,0:T(8,128)S(1)}, u32[]{:S(2)}, u32[]{:S(2)}) collective-permute-start(f32[8,512]{1,0:T(8,128)S(1)} %slice.72), channel_id=1, source_target_pairs={{0,2},{1,3},{2,0},{3,1},{4,6},{5,7},{6,4},{7,5},{8,10},{9,11},{10,... | collective-permute-start | bytes 49160 | tf_op jit(solution)/shard_map/ppermute | solution.py:327
  61.1 0.5 collective-permute-start.11
  61.6 1.5 %collective-permute-start.12 = (f32[512]{0:T(512)S(1)}, f32[512]{0:T(512)S(1)}, u32[]{:S(2)}, u32[]{:S(2)}) collective-permute-start(f32[512]{0:T(512)S(1)} %bitcast.30), channel_id=1, source_target_pairs={{0,6},{1,7},{2,4},{3,5},{4,2},{5,3},{6,0},{7,1},{8,14},{9,15},{10,... | collective-permute-start | bytes 6152 | tf_op jit(solution)/shard_map/ppermute | solution.py:420
  63.3 1.5 %collective-permute-start.9 = (bf16[256,512]{1,0:T(8,128)(2,1)S(1)}, bf16[256,512]{1,0:T(8,128)(2,1)S(1)}, u32[]{:S(2)}, u32[]{:S(2)}) collective-permute-start(bf16[256,512]{1,0:T(8,128)(2,1)S(1)} %pad_maximum_fusion), channel_id=1, source_target_pairs={{0,2},{1,3},{2,0},{3,1},{4,6},{5,7},{6,4},{7,5},{8,10},{9,11},{10,... | collective-permute-start | bytes 786440 | tf_op jit(solution)/shard_map/ppermute | solution.py:327
  64.8 1.2 %collective-permute-done.12 = f32[512]{0:T(512)S(1)} collective-permute-done((f32[512]{0:T(512)S(1)}, f32[512]{0:T(512)S(1)}, u32[]{:S(2)}, u32[]{:S(2)}) %collective-permute-start.12) | collective-permute-done | bytes 2080 | tf_op jit(solution)/shard_map/ppermute | solution.py:420
  66.1 2.3 %collective-permute-start.14 = (f32[512]{0:T(512)S(1)}, f32[512]{0:T(512)S(1)}, u32[]{:S(2)}, u32[]{:S(2)}) collective-permute-start(f32[512]{0:T(512)S(1)} %add_add_fusion.1), channel_id=1, source_target_pairs={{0,16},{4,20},{8,24},{12,28},{16,0},{20,4},{24,8},{28,12},{1,17},{... | collective-permute-start | bytes 6152 | tf_op jit(solution)/shard_map/ppermute | solution.py:327
  68.4 0.9 %collective-permute-start.13 = (f32[512]{0:T(512)S(1)}, f32[512]{0:T(512)S(1)}, u32[]{:S(2)}, u32[]{:S(2)}) collective-permute-start(f32[512]{0:T(512)S(1)} %add_add_fusion.1), channel_id=1, source_target_pairs={{0,8},{4,12},{8,0},{12,4},{16,24},{20,28},{24,16},{28,20},{1,9},{5... | collective-permute-start | bytes 6152 | tf_op jit(solution)/shard_map/ppermute | solution.py:327
  69.3 1.2 %collective-permute-start.15 = (f32[512]{0:T(512)S(1)}, f32[512]{0:T(512)S(1)}, u32[]{:S(2)}, u32[]{:S(2)}) collective-permute-start(f32[512]{0:T(512)S(1)} %add_add_fusion.1), channel_id=1, source_target_pairs={{0,24},{4,28},{8,16},{12,20},{16,8},{20,12},{24,0},{28,4},{1,25},{... | collective-permute-start | bytes 6152 | tf_op jit(solution)/shard_map/ppermute | solution.py:327
  70.6 2.7 %weight_grads.1 = (f32[3,256,256]{2,1,0:T(8,128)}, f32[256,256]{1,0:T(8,128)}) custom-call(s32[2]{0:T(128)S(1)} %pad_add_fusion.at_ref, bf16[8,32,512]{2,1,0:T(8,128)(2,1)S(1)} %all-to-all-done.refs_0_, bf16[8,32,512]{2,1,0:T(8,128)(2,1)S(1)} %collective-permute-done.16.refs_1_, bf16[8,32,512]{2,1,0:T(8,128)(2,1)} %collective-permute-done.7.refs_2_, ...), custom_call_target="tpu_custom_call" | custom-call | tf_op jit(solution)/shard_map/weight_grads/pallas_call | solution.py:348
  73.3 0.9 %fusion.4 = (f32[128,512]{1,0:T(8,128)}, bf16[128,512]{1,0:T(8,128)(2,1)}) fusion(f32[128,512]{1,0:T(8,128)S(1)} %copy-done.9, f32[128,512]{1,0:T(8,128)S(1)} %copy-done.7, f32[264,512]{1,0:T(8,128)S(1)} %get-tuple-element.41, f32[128,512]{1,0:T(8,128)S(1)} %copy-done.8, bf16[256,512]{1,0:T(8,128)(2,1)S(1)} %collective-permute-done.9, ...), kind=kLoop, calls=%fused_computation.7 | loop fusion | flops 655360 | bytes 2228736 | tf_op jit(solution)/shard_map/add | solution.py:428
  74.2 0.5 collective-permute-done.15
  74.7 0.6 add_add_fusion
  (61 shorter events, 1.6 us)
Async XLA Ops:
  0.6 21.5 %copy-start.12 = (s32[1024]{0:T(1024)S(1)}, s32[1024]{0:T(1024)}, u32[]{:S(2)}) copy-start(s32[1024]{0:T(1024)} %param.8) | copy-start | bytes 12292
  0.6 37.9 %copy-start.1 = (s32[2,128,2048]{2,1,0:T(8,128)S(1)}, s32[2,128,2048]{2,1,0:T(8,128)}, u32[]{:S(2)}) copy-start(s32[2,128,2048]{2,1,0:T(8,128)} %pulse_ref.1) | copy-start | bytes 6291460
  0.7 37.9 %copy-start.2 = (bf16[128,2048]{1,0:T(8,128)(2,1)S(1)}, bf16[128,2048]{1,0:T(8,128)(2,1)}, u32[]{:S(2)}) copy-start(bf16[128,2048]{1,0:T(8,128)(2,1)} %tok_ref.3) | copy-start | bytes 1572868
  0.7 37.9 %copy-start.4 = (bf16[128,2048]{1,0:T(8,128)(2,1)S(1)}, bf16[128,2048]{1,0:T(8,128)(2,1)}, u32[]{:S(2)}) copy-start(bf16[128,2048]{1,0:T(8,128)(2,1)} %up_ref.1) | copy-start | bytes 1572868
  0.7 37.9 %copy-start.6 = (f32[2048]{0:T(1024)S(1)}, f32[2048]{0:T(1024)}, u32[]{:S(2)}) copy-start(f32[2048]{0:T(1024)} %param.10) | copy-start | bytes 24580
  5.8 9.5 %collective-permute-start = (bf16[128,1024]{1,0:T(8,128)(2,1)}, bf16[128,1024]{1,0:T(8,128)(2,1)S(1)}, u32[]{:S(2)}, u32[]{:S(2)}) collective-permute-start(bf16[128,1024]{1,0:T(8,128)(2,1)} %get-tuple-element.24.refs_0_), channel_id=1, source_target_pairs={{0,4},{4,0},{8,12},{12,8},{16,20},{20,16},{24,28},{28,24},{1,5},{5... | collective-permute-start | bytes 786440 | tf_op jit(solution)/shard_map/ppermute | solution.py:327
  8.8 14.7 %collective-permute-start.3 = (bf16[128,1024]{1,0:T(8,128)(2,1)}, bf16[128,1024]{1,0:T(8,128)(2,1)}, u32[]{:S(2)}, u32[]{:S(2)}) collective-permute-start(bf16[128,1024]{1,0:T(8,128)(2,1)} %get-tuple-element.24.refs_0_), channel_id=1, source_target_pairs={{0,16},{4,20},{8,24},{12,28},{16,0},{20,4},{24,8},{28,12},{1,17},{... | collective-permute-start | bytes 786440 | tf_op jit(solution)/shard_map/ppermute | solution.py:327
  11.4 32.3 %collective-permute-start.1 = (bf16[128,1024]{1,0:T(8,128)(2,1)}, bf16[128,1024]{1,0:T(8,128)(2,1)}, u32[]{:S(2)}, u32[]{:S(2)}) collective-permute-start(bf16[128,1024]{1,0:T(8,128)(2,1)} %get-tuple-element.24.refs_0_), channel_id=1, source_target_pairs={{0,8},{4,12},{8,0},{12,4},{16,24},{20,28},{24,16},{28,20},{1,9},{5... | collective-permute-start | bytes 786440 | tf_op jit(solution)/shard_map/ppermute | solution.py:327
  15.4 0.7 copy-start.11
  16.1 20.9 %all-to-all-start = ((bf16[8,32,512]{2,1,0:T(8,128)(2,1)}), bf16[8,32,512]{2,1,0:T(8,128)(2,1)S(1)}, u32[]{:S(2)}, u32[]{:S(2)}) async-start(bf16[8,32,512]{2,1,0:T(8,128)(2,1)} %get-tuple-element.26), calls=%async_computation | async-start | bytes 524288 | tf_op jit(solution)/shard_map/all_to_all | solution.py:392
  23.6 11.7 %collective-permute-start.5 = (bf16[128,1024]{1,0:T(8,128)(2,1)}, bf16[128,1024]{1,0:T(8,128)(2,1)}, u32[]{:S(2)}, u32[]{:S(2)}) collective-permute-start(bf16[128,1024]{1,0:T(8,128)(2,1)} %collective-permute-done.3.refs_4_), channel_id=1, source_target_pairs={{0,8},{4,12},{8,0},{12,4},{16,24},{20,28},{24,16},{28,20},{1,9},{5... | collective-permute-start | bytes 786440 | tf_op jit(solution)/shard_map/ppermute | solution.py:327
  25.0 18.7 %collective-permute-start.2 = (bf16[128,1024]{1,0:T(8,128)(2,1)}, bf16[128,1024]{1,0:T(8,128)(2,1)}, u32[]{:S(2)}, u32[]{:S(2)}) collective-permute-start(bf16[128,1024]{1,0:T(8,128)(2,1)} %copy-done.11), channel_id=1, source_target_pairs={{0,8},{4,12},{8,0},{12,4},{16,24},{20,28},{24,16},{28,20},{1,9},{5... | collective-permute-start | bytes 786440 | tf_op jit(solution)/shard_map/ppermute | solution.py:327
  25.8 17.9 %collective-permute-start.4 = (bf16[128,1024]{1,0:T(8,128)(2,1)}, bf16[128,1024]{1,0:T(8,128)(2,1)}, u32[]{:S(2)}, u32[]{:S(2)}) collective-permute-start(bf16[128,1024]{1,0:T(8,128)(2,1)} %collective-permute-done.3.refs_4_), channel_id=1, source_target_pairs={{0,4},{4,0},{8,12},{12,8},{16,20},{20,16},{24,28},{28,24},{1,5},{5... | collective-permute-start | bytes 786440 | tf_op jit(solution)/shard_map/ppermute | solution.py:327
  35.3 8.5 %collective-permute-start.6 = (bf16[128,1024]{1,0:T(8,128)(2,1)}, bf16[128,1024]{1,0:T(8,128)(2,1)}, u32[]{:S(2)}, u32[]{:S(2)}) collective-permute-start(bf16[128,1024]{1,0:T(8,128)(2,1)} %collective-permute-done.5.refs_6_), channel_id=1, source_target_pairs={{0,4},{4,0},{8,12},{12,8},{16,20},{20,16},{24,28},{28,24},{1,5},{5... | collective-permute-start | bytes 786440 | tf_op jit(solution)/shard_map/ppermute | solution.py:327
  37.0 6.5 %collective-permute-start.7 = (bf16[8,32,512]{2,1,0:T(8,128)(2,1)S(1)}, bf16[8,32,512]{2,1,0:T(8,128)(2,1)}, u32[]{:S(2)}, u32[]{:S(2)}) collective-permute-start(bf16[8,32,512]{2,1,0:T(8,128)(2,1)S(1)} %all-to-all-done.refs_0_), channel_id=1, source_target_pairs={{0,2},{1,3},{2,0},{3,1},{4,6},{5,7},{6,4},{7,5},{8,10},{9,11},{10,... | collective-permute-start | bytes 786440 | tf_op jit(solution)/shard_map/ppermute | solution.py:327
  43.7 11.3 %copy-start = (bf16[2048,3,256]{2,0,1:T(8,128)(2,1)S(1)}, bf16[2048,3,256]{2,0,1:T(8,128)(2,1)}, u32[]{:S(2)}) copy-start(bf16[2048,3,256]{2,0,1:T(8,128)(2,1)} %param.11) | copy-start | bytes 9437188
  43.8 11.3 %copy-start.3 = (bf16[256,2048]{1,0:T(8,128)(2,1)S(1)}, bf16[256,2048]{1,0:T(8,128)(2,1)}, u32[]{:S(2)}) copy-start(bf16[256,2048]{1,0:T(8,128)(2,1)} %wout_ref.1) | copy-start | bytes 3145732
  43.8 11.3 %copy-start.5 = (f32[128,2048]{1,0:T(8,128)S(1)}, f32[128,2048]{1,0:T(8,128)}, u32[]{:S(2)}) copy-start(f32[128,2048]{1,0:T(8,128)} %get-tuple-element.28.factor_ref) | copy-start | bytes 3145732
  56.5 2.7 %collective-permute-start.8 = (f32[2,264,512]{2,1,0:T(8,128)S(1)}, f32[2,264,512]{2,1,0:T(8,128)S(1)}, u32[]{:S(2)}, u32[]{:S(2)}) collective-permute-start(f32[2,264,512]{2,1,0:T(8,128)S(1)} %get-tuple-element.30), channel_id=1, source_target_pairs={{0,1},{1,0},{2,3},{3,2},{4,5},{5,4},{6,7},{7,6},{8,9},{9,8},{10,11... | collective-permute-start | bytes 3244040 | tf_op jit(solution)/shard_map/ppermute | solution.py:327
  56.6 12.8 %collective-permute-start.16 = (bf16[8,32,512]{2,1,0:T(8,128)(2,1)S(1)}, bf16[8,32,512]{2,1,0:T(8,128)(2,1)S(1)}, u32[]{:S(2)}, u32[]{:S(2)}) collective-permute-start(bf16[8,32,512]{2,1,0:T(8,128)(2,1)S(1)} %all-to-all-done.refs_0_), channel_id=1, source_target_pairs={{0,1},{1,0},{2,3},{3,2},{4,5},{5,4},{6,7},{7,6},{8,9},{9,8},{10,11... | collective-permute-start | bytes 786440 | tf_op jit(solution)/shard_map/ppermute | solution.py:327
  57.1 13.5 %collective-permute-start.17 = (bf16[8,32,512]{2,1,0:T(8,128)(2,1)}, bf16[8,32,512]{2,1,0:T(8,128)(2,1)S(1)}, u32[]{:S(2)}, u32[]{:S(2)}) collective-permute-start(bf16[8,32,512]{2,1,0:T(8,128)(2,1)} %collective-permute-done.7.refs_2_), channel_id=1, source_target_pairs={{0,1},{1,0},{2,3},{3,2},{4,5},{5,4},{6,7},{7,6},{8,9},{9,8},{10,11... | collective-permute-start | bytes 786440 | tf_op jit(solution)/shard_map/ppermute | solution.py:327
  59.5 3.8 %collective-permute-start.10 = (f32[8,512]{1,0:T(8,128)S(1)}, f32[8,512]{1,0:T(8,128)S(1)}, u32[]{:S(2)}, u32[]{:S(2)}) collective-permute-start(f32[8,512]{1,0:T(8,128)S(1)} %slice.72), channel_id=1, source_target_pairs={{0,2},{1,3},{2,0},{3,1},{4,6},{5,7},{6,4},{7,5},{8,10},{9,11},{10,... | collective-permute-start | bytes 49160 | tf_op jit(solution)/shard_map/ppermute | solution.py:327
  61.1 3.7 %collective-permute-start.11 = (f32[512]{0:T(512)S(1)}, f32[512]{0:T(512)S(1)}, u32[]{:S(2)}, u32[]{:S(2)}) collective-permute-start(f32[512]{0:T(512)S(1)} %bitcast.31), channel_id=1, source_target_pairs={{0,4},{4,0},{8,12},{12,8},{16,20},{20,16},{24,28},{28,24},{1,5},{5... | collective-permute-start | bytes 6152 | tf_op jit(solution)/shard_map/ppermute | solution.py:327
  61.6 4.5 %collective-permute-start.12 = (f32[512]{0:T(512)S(1)}, f32[512]{0:T(512)S(1)}, u32[]{:S(2)}, u32[]{:S(2)}) collective-permute-start(f32[512]{0:T(512)S(1)} %bitcast.30), channel_id=1, source_target_pairs={{0,6},{1,7},{2,4},{3,5},{4,2},{5,3},{6,0},{7,1},{8,14},{9,15},{10,... | collective-permute-start | bytes 6152 | tf_op jit(solution)/shard_map/ppermute | solution.py:420
  63.1 10.2 %copy-start.7 = (f32[128,512]{1,0:T(8,128)S(1)}, f32[128,512]{1,0:T(8,128)}, u32[]{:S(2)}) copy-start(f32[128,512]{1,0:T(8,128)} %get-tuple-element.33) | copy-start | bytes 786436
  63.1 10.2 %copy-start.8 = (f32[128,512]{1,0:T(8,128)S(1)}, f32[128,512]{1,0:T(8,128)}, u32[]{:S(2)}) copy-start(f32[128,512]{1,0:T(8,128)} %get-tuple-element.34) | copy-start | bytes 786436
  63.1 10.2 %copy-start.9 = (f32[128,512]{1,0:T(8,128)S(1)}, f32[128,512]{1,0:T(8,128)}, u32[]{:S(2)}) copy-start(f32[128,512]{1,0:T(8,128)} %get-tuple-element.32) | copy-start | bytes 786436
  63.1 10.2 %copy-start.10 = (f32[128,512]{1,0:T(8,128)S(1)}, f32[128,512]{1,0:T(8,128)}, u32[]{:S(2)}) copy-start(f32[128,512]{1,0:T(8,128)} %get-tuple-element.23) | copy-start | bytes 786436
  63.3 10.0 %collective-permute-start.9 = (bf16[256,512]{1,0:T(8,128)(2,1)S(1)}, bf16[256,512]{1,0:T(8,128)(2,1)S(1)}, u32[]{:S(2)}, u32[]{:S(2)}) collective-permute-start(bf16[256,512]{1,0:T(8,128)(2,1)S(1)} %pad_maximum_fusion), channel_id=1, source_target_pairs={{0,2},{1,3},{2,0},{3,1},{4,6},{5,7},{6,4},{7,5},{8,10},{9,11},{10,... | collective-permute-start | bytes 786440 | tf_op jit(solution)/shard_map/ppermute | solution.py:327
  66.1 8.1 %collective-permute-start.14 = (f32[512]{0:T(512)S(1)}, f32[512]{0:T(512)S(1)}, u32[]{:S(2)}, u32[]{:S(2)}) collective-permute-start(f32[512]{0:T(512)S(1)} %add_add_fusion.1), channel_id=1, source_target_pairs={{0,16},{4,20},{8,24},{12,28},{16,0},{20,4},{24,8},{28,12},{1,17},{... | collective-permute-start | bytes 6152 | tf_op jit(solution)/shard_map/ppermute | solution.py:327
  68.4 5.9 %collective-permute-start.13 = (f32[512]{0:T(512)S(1)}, f32[512]{0:T(512)S(1)}, u32[]{:S(2)}, u32[]{:S(2)}) collective-permute-start(f32[512]{0:T(512)S(1)} %add_add_fusion.1), channel_id=1, source_target_pairs={{0,8},{4,12},{8,0},{12,4},{16,24},{20,28},{24,16},{28,20},{1,9},{5... | collective-permute-start | bytes 6152 | tf_op jit(solution)/shard_map/ppermute | solution.py:327
  69.3 5.4 %collective-permute-start.15 = (f32[512]{0:T(512)S(1)}, f32[512]{0:T(512)S(1)}, u32[]{:S(2)}, u32[]{:S(2)}) collective-permute-start(f32[512]{0:T(512)S(1)} %add_add_fusion.1), channel_id=1, source_target_pairs={{0,24},{4,28},{8,16},{12,20},{16,8},{20,12},{24,0},{28,4},{1,25},{... | collective-permute-start | bytes 6152 | tf_op jit(solution)/shard_map/ppermute | solution.py:327
